TPU v7x, 1024 devices: a whole 4x8x16 slice. The times are simulated.
1024 devices in a mesh: dp: 4 (over z_lo), tp: 256 (over y, x, z_hi, core).
Axes of the slice: x: 4, y: 8, z: 16 (z_hi: 4, z_lo: 4; z = z_hi * 4 + z_lo), core: 2. Of those that a mesh axis runs over, the one named last changes fastest.
Arguments:
- hidden: bfloat16 [1024, 26624], P('dp', 'tp'), may hold values from -0.1875 to 0.1875
- out_grad: bfloat16 [1024, 8192], P(('dp', 'tp')), may hold values from -6 to 6
- down_weight: bfloat16 [26624, 8192], P('tp', 'dp'), may hold values from -0.0625 to 0.0625
Outputs:
- input_grad: bfloat16 [1024, 26624], P('dp', 'tp')
- weight_grad: bfloat16 [26624, 8192], P('tp', 'dp')
All inputs are finite; a program needn't handle non-finite values.
Results may differ from a plain program's by a relative error of at most 0.009.
Values may be sent and summed in bfloat16 or wider, within the bound.
No kernel may reach another device: no remote copies, remote signals or barrier semaphores. Data moves between devices by JAX's collectives and lax.ppermute only.
A program may use at most 32 MiB of HBM per device.

v0:
```python
import jax
import jax.numpy as jnp
from jax import lax
from jax.sharding import PartitionSpec as P


def shards(hidden, out_grad, down_weight):
    whole_weight = lax.all_gather(down_weight, "dp", axis=1, tiled=True)
    received = lax.all_gather(out_grad, "tp", axis=0, tiled=True)
    weight_term = lax.dot_general(
        hidden, received, (((0,), (0,)), ((), ())), preferred_element_type=jnp.float32
    )
    block = lax.dot_general(
        received, whole_weight, (((1,), (1,)), ((), ())), preferred_element_type=jnp.float32
    )
    summed = lax.psum_scatter(
        weight_term.astype(jnp.bfloat16), "dp", scatter_dimension=1, tiled=True
    )
    return (block.astype(jnp.bfloat16), summed)


def solution(mesh):
    placed = (P("dp", "tp"), P(("dp", "tp"), None), P("tp", "dp"))
    return jax.shard_map(
        shards,
        mesh=mesh,
        in_specs=placed,
        out_specs=(P("dp", "tp"), P("tp", "dp")),
        check_vma=False,
    )
```

profile of v0, /device:TPU:1, one launch (start us, length us, event | category | flops | bytes accessed | tf_op | source)
XLA Modules:
  0.0 311.0 jit_solution(1437492388979168386)
XLA Ops:
  7.2 0.0 copy-start
  7.2 0.0 all-gather.6.cloned.1.call-start
  7.2 0.7 all-gather.6.cloned.1.call-update
  7.9 0.0 all-gather.4.cloned.1.call-start
  8.0 0.7 all-gather.4.cloned.1.call-update
  8.7 0.0 reduce-scatter.2.cloned.1.call-start
  8.7 196.0 %all-gather.6.cloned.1.call-done = bf16[256,1,8192]{2,1,0:T(2,128)(2,1)} async-done(((bf16[1,1,8192]{2,1,0:T(2,128)(2,1)}), bf16[256,1,8192]{2,1,0:T(2,128)(2,1)}) %all-gather.6.cloned.1.call-update) | async-done | bytes 4194320 | tf_op jit(solution)/shard_map/all_gather | solution.py:9
  204.7 0.0 copy-done
  204.7 9.4 %convolution_convert_fusion = bf16[104,8192]{1,0:T(8,128)(2,1)} fusion(bf16[256,104]{0,1:T(8,128)(2,1)S(1)} %copy-done, bf16[256,1,8192]{2,1,0:T(2,128)(2,1)} %all-gather.6.cloned.1.call-done), kind=kOutput, calls=%fused_computation | convolution fusion | flops 437059584 | bytes 5951488 | tf_op jit(solution)/shard_map/dot_general | solution.py:10
  214.1 0.0 reduce-scatter.2.cloned.1.call-update
  214.1 35.6 %all-gather.4.cloned.1.call-done = bf16[104,8192]{1,0:T(8,128)(2,1)} async-done(((bf16[104,2048]{1,0:T(8,128)(2,1)}), bf16[104,8192]{1,0:T(8,128)(2,1)}) %all-gather.4.cloned.1.call-update) | async-done | bytes 1703952 | tf_op jit(solution)/shard_map/all_gather | solution.py:8
  249.7 9.2 %fusion.5 = bf16[256,104]{0,1:T(8,128)(2,1)} fusion(bf16[104,8192]{1,0:T(8,128)(2,1)} %all-gather.4.cloned.1.call-done, bf16[256,1,8192]{2,1,0:T(2,128)(2,1)} %all-gather.6.cloned.1.call-done), kind=kOutput, calls=%fused_computation.6 | convolution fusion | flops 436234240 | bytes 5951488 | tf_op jit(solution)/shard_map/dot_general | solution.py:13
  258.9 45.6 %reduce-scatter.2.cloned.1.call-done = bf16[104,2048]{1,0:T(8,128)(2,1)} async-done(((bf16[104,8192]{1,0:T(8,128)(2,1)}), bf16[104,2048]{1,0:T(8,128)(2,1)}) %reduce-scatter.2.cloned.1.call-update) | async-done | bytes 426000 | tf_op jit(solution)/shard_map/reduce_scatter | solution.py:16
Async XLA Ops:
  7.2 197.5 %copy-start = (bf16[256,104]{0,1:T(8,128)(2,1)S(1)}, bf16[256,104]{0,1:T(8,128)(2,1)}, u32[]{:S(2)}) copy-start(bf16[256,104]{0,1:T(8,128)(2,1)} %param.3) | copy-start | bytes 159748
  7.2 197.5 %all-gather.6.cloned.1.call-start = ((), (), s32[]{:S(2)}) async-start(), calls=%async_computation.3 | async-start | bytes 8421376 | tf_op jit(solution)/shard_map/all_gather | solution.py:9
  7.9 241.8 %all-gather.4.cloned.1.call-start = ((), (), s32[]{:S(2)}) async-start(), calls=%async_computation.1 | async-start | bytes 2129920 | tf_op jit(solution)/shard_map/all_gather | solution.py:8
  8.7 295.8 %reduce-scatter.2.cloned.1.call-start = ((), (), s32[]{:S(2)}) async-start(), calls=%async_computation.2 | async-start | bytes 2129920 | tf_op jit(solution)/shard_map/reduce_scatter | solution.py:16
Sparse Core Ops, SparseCore 0:
  13.8 190.8 all-gather.5
  207.4 42.2 all-gather.3
  253.7 50.6 reduce-scatter.1
where the time goes:
time: 311 us
  waiting for transfers between devices  279 us (90%)
  matrix products  18.6 us (6%)
  between operations  13.7 us (4%)
    all_gather x1, waiting for transfers between devices, shards(): received = lax.all_gather(out_grad, 'tp', axis=0, tiled=True)  196 us
    reduce_scatter x1, waiting for transfers between devices, shards(): lax.psum_scatter(weight_term.astype(jnp.bfloat16), 'dp', scatter_dimensio...  45.6 us
    all_gather x1, waiting for transfers between devices, shards(): whole_weight = lax.all_gather(down_weight, 'dp', axis=1, tiled=True)  35.6 us
    dot_general x1, matrix products, shards(): lax.dot_general(hidden, received, (((0,), (0,)), ((), ())), preferred_ele...  9.39 us
    dot_general x1, matrix products, shards(): lax.dot_general(received, whole_weight, (((1,), (1,)), ((), ())), preferr...  9.2 us
  transfers between devices with their start and end apart: 3, of which 3 were waited for; matrix products, arithmetic and copies ran while one was open for 6% of the time, Pallas kernels for 0%

commit v1 on v0

v1 whole, which is shorter than its diff:
```python
import functools

import jax
import jax.numpy as jnp
from jax import lax
from jax.experimental import pallas as pl
from jax.experimental.pallas import tpu as pltpu
from jax.sharding import Mesh, PartitionSpec as P


BF16, F32 = jnp.bfloat16, jnp.float32
DP, Y, X, ZH, CORE = 4, 8, 4, 4, 2
ROWS = X * DP * ZH
CHUNKS = 8
EARLY = 6
TOK = 256
HALF = TOK // CORE
VMEM = pl.BlockSpec(memory_space=pltpu.VMEM)
SMEM = pl.BlockSpec(memory_space=pltpu.SMEM)
SWAP = [(0, 1), (1, 0)]


def ring_pairs(cross):
    pairs = []
    for y in range(Y):
        for core, way in ((0, 1), (1, -1)):
            pairs.append((y * CORE + (core ^ cross), ((y + way) % Y) * CORE + core))
    return pairs


def dot(a, b, ca, cb):
    return lax.dot_general(a, b, (((ca,), (cb,)), ((), ())), preferred_element_type=F32)


def call(body, outs, *args, flops=0, aliases=None):
    outs = [jax.ShapeDtypeStruct(s, d) for s, d in outs]
    moved = sum(a.size * a.dtype.itemsize for a in args) + sum(o.size * o.dtype.itemsize for o in outs)
    specs = [SMEM if a.dtype == jnp.int32 else VMEM for a in args]
    return pl.pallas_call(
        body,
        out_shape=outs,
        in_specs=specs,
        out_specs=[VMEM] * len(outs),
        input_output_aliases=aliases or {},
        cost_estimate=pl.CostEstimate(flops=flops, bytes_accessed=moved, transcendentals=0),
        compiler_params=pltpu.CompilerParams(vmem_limit_bytes=12 * 2**20),
    )(*args)


def token_at(p, y):
    core, q, x, zh = p >> 7, (p >> 4) & 7, (p >> 2) & 3, p & 3
    step = (q + 1) >> 1
    flip = jnp.where(((q & 1) == 0) & (q > 0), 1, 0)
    row = (y + jnp.where(core == 0, -step, step)) & 7
    return row * 32 + x * 8 + zh * 2 + (core ^ flip)


def iota(shape, dim):
    return lax.broadcasted_iota(jnp.int32, shape, dim)


def hidden_body(at, hidden, sent):
    hot = (iota((TOK, TOK), 0) == token_at(iota((TOK, TOK), 1), at[1])).astype(BF16)
    ordered = dot(hidden[...], hot, 1, 0).astype(BF16)
    for g in range(DP):
        for c in range(CORE):
            sent[g * CORE + c] = ordered[:, c * HALF:(c + 1) * HALF]


def units_body(ff, pad, at, got, mine, other, units, weight, grouped):
    me = at[0]
    a = iota((CHUNKS * ROWS, CHUNKS * ROWS), 0)
    b = iota((CHUNKS * ROWS, CHUNKS * ROWS), 1)
    place = ((a >> 2) & 3) * HALF + (a >> 6) * 16 + ((a >> 4) & 3) * 4 + (a & 3)
    hot = (place == b).astype(BF16)
    grouped[...] = hot
    gap = jnp.zeros((pad - ff, CHUNKS * ROWS), F32)
    rows = []
    for j in range(CORE):
        rows.append(jnp.concatenate([got[g * CORE + (me ^ j)] for g in range(DP)], axis=1))
    for j in range(CORE):
        moved = dot(rows[j], hot, 1, 1)
        units[pl.ds(j * pad, pad)] = jnp.concatenate([moved, gap], axis=0).astype(BF16)
    blank = jnp.zeros((pad - ff, mine.shape[1]), BF16)
    weight[pl.ds(0, ff)] = mine[...]
    weight[pl.ds(ff, pad - ff)] = blank
    weight[pl.ds(pad, ff)] = other[...]
    weight[pl.ds(pad + ff, pad - ff)] = blank


def early_body(units, weight, grouped, *refs):
    chunks, (grad, parts) = refs[:EARLY], refs[EARLY:]
    n = EARLY * ROWS
    width = weight.shape[1]
    inner = jnp.concatenate([c[...] for c in chunks], axis=0)
    ig = dot(weight[...], inner, 1, 1).astype(BF16)
    parts[...] = dot(ig, grouped[pl.ds(0, n)], 1, 0).astype(BF16)
    left = units[:, :n]
    for j in range(0, width, 512):
        cols = jnp.concatenate([c[:, j:j + 512] for c in chunks], axis=0)
        grad[:, j:j + 512] = dot(left, cols, 1, 0)


def parts_body(ff, pad, at, weight, grouped, early, *refs):
    chunks, (out,) = refs[:-1], refs[-1:]
    me = at[0]
    n = EARLY * ROWS
    inner = jnp.concatenate([c[...] for c in chunks], axis=0)
    ig = dot(weight[...], inner, 1, 1).astype(BF16)
    parts = (dot(ig, grouped[pl.ds(n, CHUNKS * ROWS - n)], 1, 0) + early[...].astype(F32)).astype(BF16)
    for g in range(DP):
        for j in range(CORE):
            out[g * CORE + (me ^ j)] = parts[j * pad:j * pad + ff, g * HALF:(g + 1) * HALF]


def late_body(ff, pad, units, grad, *refs):
    chunks, (keep, give) = refs[:-2], refs[-2:]
    n = EARLY * ROWS
    width = grad.shape[1]
    left = units[:, n:]
    for k in range(0, width, 512):
        cols = jnp.concatenate([c[:, k:k + 512] for c in chunks], axis=0)
        total = grad[:, k:k + 512] + dot(left, cols, 1, 0)
        keep[:, k:k + 512] = total[:ff]
        give[:, k:k + 512] = total[pad:pad + ff].astype(BF16)


def final_body(at, back, out):
    hot = (token_at(iota((TOK, TOK), 0), at[1]) == iota((TOK, TOK), 1)).astype(BF16)
    halves = []
    for c in range(CORE):
        total = back[c].astype(F32)
        for g in range(1, DP):
            total = total + back[g * CORE + c].astype(F32)
        halves.append(total.astype(BF16))
    out[...] = dot(jnp.concatenate(halves, axis=1), hot, 1, 0).astype(BF16)


def add_body(keep, taken, out):
    out[...] = (keep[...] + taken[...].astype(F32)).astype(BF16)


def ring(value, cross=0):
    return lax.ppermute(value, ("y", "core"), ring_pairs(cross))


def step(hidden, out_grad, down_weight):
    ff, width = down_weight.shape
    pad = -(-ff // 16) * 16
    at = jnp.stack([lax.axis_index("core"), lax.axis_index("y")]).astype(jnp.int32)

    row = jnp.broadcast_to(out_grad.reshape(DP, 1, 2, width // 2), (DP, ZH, 2, width // 2))
    row = row.reshape(DP * ZH, 2, width // 2)
    mine = lax.all_to_all(row, ("dp", "zh"), 0, 0, tiled=True).reshape(DP * ZH, width)
    spread = jnp.broadcast_to(mine[None], (X, DP * ZH, width))
    u0 = lax.all_to_all(spread, "x", 0, 0, tiled=True).reshape(ROWS, width)

    (sent,) = call(hidden_body, [((DP * CORE, ff, HALF), BF16)], at, hidden.T)
    got = lax.all_to_all(sent, ("dp", "core"), 0, 0, tiled=True)
    other = lax.ppermute(down_weight, "core", SWAP)
    units, weight, grouped = call(
        functools.partial(units_body, ff, pad),
        [((2 * pad, CHUNKS * ROWS), BF16), ((2 * pad, width), BF16), ((CHUNKS * ROWS, CHUNKS * ROWS), BF16)],
        at, got, down_weight, other,
    )

    u1 = ring(u0)
    v1 = ring(u0, cross=1)
    u2 = ring(u1)
    v2 = ring(v1)
    u3 = ring(u2)
    v3 = ring(v2)
    u4 = ring(u3)

    flops = 4 * pad * width * ROWS * CORE
    grad, parts = call(
        early_body, [((2 * pad, width), F32), ((2 * pad, CHUNKS * ROWS), BF16)],
        units, weight, grouped, u0, u1, v1, u2, v2, u3, flops=EARLY * flops,
    )
    (parts,) = call(
        functools.partial(parts_body, ff, pad), [((DP * CORE, ff, HALF), BF16)],
        at, weight, grouped, parts, v3, u4, flops=flops,
    )
    back = lax.all_to_all(parts, ("dp", "core"), 0, 0, tiled=True)
    keep, give = call(
        functools.partial(late_body, ff, pad), [((ff, width), F32), ((ff, width), BF16)],
        units, grad, v3, u4, flops=flops,
    )
    taken = lax.ppermute(give, "core", SWAP)
    (weight_grad,) = call(add_body, [((ff, width), BF16)], keep, taken)
    (input_grad,) = call(final_body, [((ff, TOK), BF16)], at, back)
    return input_grad.T, weight_grad


def solution(mesh):
    fine = Mesh(mesh.devices.reshape(DP, Y, X, ZH, CORE), ("dp", "y", "x", "zh", "core"))
    tp = ("y", "x", "zh", "core")
    return jax.shard_map(
        step,
        mesh=fine,
        in_specs=(P("dp", tp), P(("dp",) + tp, None), P(tp, "dp")),
        out_specs=(P("dp", tp), P(tp, "dp")),
        check_vma=False,
    )
```

time: 311 us -> 103 us (0.33)
  waiting for transfers between devices: 279 us -> 6.05 us
  starting transfers between devices: 0.11 us -> 42.1 us
  blocking collectives: 0 us -> 40.2 us
  matrix products: 18.6 us -> 0 us
  between operations: 13.7 us -> 0.84 us
  Pallas kernels: 0 us -> 9.58 us
    all_gather x2 -> x0, waiting for transfers between devices: 232 us -> none  [the longest x1 196 us: shards(): received = lax.all_gather(out_grad, 'tp', axis=0, tiled=True)]
    reduce_scatter x1 -> x0, waiting for transfers between devices: 45.6 us -> none  [shards(): lax.psum_scatter(weight_term.astype(jnp.bfloat16), 'dp', scatter_dimensio...]
    all_to_all x0 -> x2, blocking collectives: none -> 40.2 us  [the longest x1 30.9 us: step(): lax.all_to_all(row, ('dp', 'zh'), 0, 0, tiled=True).reshape(DP * ZH, width)]
    ppermute x0 -> x9, starting transfers between devices: none -> 29.6 us  [the longest x7 25.8 us: ring(): return lax.ppermute(value, ('y', 'core'), ring_pairs(cross))]
    dot_general x2 -> x0, matrix products: 18.6 us -> none  [the longest x1 9.39 us: shards(): lax.dot_general(hidden, received, (((0,), (0,)), ((), ())), preferred_ele...]
    all_to_all x0 -> x2, starting transfers between devices: none -> 12.4 us  [the longest x1 6.96 us: step(): back = lax.all_to_all(parts, ('dp', 'core'), 0, 0, tiled=True)]
    pallas_call x0 -> x7, Pallas kernels: none -> 9.58 us  [call(): pl.pallas_call(body, out_shape=outs, in_specs=specs, out_specs=[VMEM] * l...]
    ppermute x0 -> x9, waiting for transfers between devices: none -> 4.14 us  [the longest x7 2.4 us: ring(): return lax.ppermute(value, ('y', 'core'), ring_pairs(cross))]
  transfers between devices with their start and end apart: 3 -> 11, of which waited for: 3 -> 4; matrix products, arithmetic and copies ran while one was open for 6% -> 0% of each run, Pallas kernels for 0% -> 6%
where the time goes in v1:
time: 103 us; the launch traced here: 102 us
  starting transfers between devices  42.1 us (41%)
  blocking collectives  40.2 us (39%)
  Pallas kernels  9.58 us (9%)
  waiting for transfers between devices  6.05 us (6%)
  local copies, waits for them, and re-layouts  2.54 us (2%)
    all_to_all x1, blocking collectives, step(): lax.all_to_all(row, ('dp', 'zh'), 0, 0, tiled=True).reshape(DP * ZH, width)  30.9 us
    ppermute x7, starting transfers between devices, ring(): return lax.ppermute(value, ('y', 'core'), ring_pairs(cross))  25.8 us
    pallas_call x7, Pallas kernels, call(): pl.pallas_call(body, out_shape=outs, in_specs=specs, out_specs=[VMEM] * l...  9.58 us
    all_to_all x1, blocking collectives, step(): u0 = lax.all_to_all(spread, 'x', 0, 0, tiled=True).reshape(ROWS, width)  9.34 us
    all_to_all x1, starting transfers between devices, step(): back = lax.all_to_all(parts, ('dp', 'core'), 0, 0, tiled=True)  6.96 us
    all_to_all x1, starting transfers between devices, step(): got = lax.all_to_all(sent, ('dp', 'core'), 0, 0, tiled=True)  5.49 us
    unnamed x9, local copies, waits for them, and re-layouts  2.47 us
    ppermute x7, waiting for transfers between devices, ring(): return lax.ppermute(value, ('y', 'core'), ring_pairs(cross))  2.4 us
  transfers between devices with their start and end apart: 11, of which 4 were waited for; matrix products, arithmetic and copies ran while one was open for 0% of the time, Pallas kernels for 6%

profile of v1, /device:TPU:1, one launch (start us, length us, event | category | flops | bytes accessed | tf_op | source)
XLA Modules:
  0.0 102.3 jit_solution(788683424219605983)
XLA Ops:
  0.6 0.0 copy-start
  0.6 0.9 reduce
  1.6 30.9 %all_to_all.20 = bf16[16,2,1024]{2,1,0:T(2,128)(2,1)S(1)} all-to-all(bf16[16,2,1024]{2,1,0:T(2,128)(2,1)S(1)} %bitcast.13), channel_id=1, replica_groups=mesh['dp'=4,'y'=8,'x'=4,'zh'=4,'core'=2] {'dp','zh'}, dimensions={0} | all-to-all | bytes 131072 | tf_op jit(solution)/shard_map/all_to_all | solution.py:154
  32.5 9.3 %all_to_all.21 = bf16[4,16,2048]{2,1,0:T(8,128)(2,1)S(1)} all-to-all(bf16[4,16,2048]{2,1,0:T(8,128)(2,1)S(1)} %broadcast_in_dim.17), channel_id=1, replica_groups=mesh['dp'=4,'y'=8,'x'=4,'zh'=4,'core'=2] {'x'}, dimensions={0} | all-to-all | bytes 524288 | tf_op jit(solution)/shard_map/all_to_all | solution.py:156
  41.9 5.1 %collective-permute-start.1 = (bf16[64,2048]{1,0:T(8,128)(2,1)S(1)}, bf16[64,2048]{1,0:T(8,128)(2,1)S(1)}, u32[]{:S(2)}, u32[]{:S(2)}) collective-permute-start(bf16[64,2048]{1,0:T(8,128)(2,1)S(1)} %bitcast.8), channel_id=1, source_target_pairs={{0,32},{1,225},{32,64},{33,1},{64,96},{65,33},{96,128},{97,65},{12... | collective-permute-start | bytes 786440 | tf_op jit(solution)/shard_map/ppermute | solution.py:144
  47.0 0.1 pad_add_fusion.at
  47.0 0.0 copy-start.3
  47.0 0.8 copy-done.3
  47.8 1.4 %shard_map.50 = bf16[8,104,128]{2,1,0:T(8,128)(2,1)} custom-call(s32[2]{0:T(128)S(1)} %pad_add_fusion.at, bf16[104,256]{1,0:T(8,128)(2,1)S(1)} %bitcast.11), custom_call_target="tpu_custom_call" | custom-call | bytes 266248 | tf_op jit(solution)/shard_map/pallas_call | solution.py:39
  49.3 5.5 %all-to-all-start = ((bf16[8,104,128]{2,1,0:T(8,128)(2,1)}), bf16[8,104,128]{2,1,0:T(8,128)(2,1)S(1)}, u32[]{:S(2)}, u32[]{:S(2)}) async-start(bf16[8,104,128]{2,1,0:T(8,128)(2,1)} %shard_map.50), calls=%async_computation | async-start | bytes 425984 | tf_op jit(solution)/shard_map/all_to_all | solution.py:159
  54.8 3.2 %collective-permute-start.2 = (bf16[64,2048]{1,0:T(8,128)(2,1)S(1)}, bf16[64,2048]{1,0:T(8,128)(2,1)S(1)}, u32[]{:S(2)}, u32[]{:S(2)}) collective-permute-start(bf16[64,2048]{1,0:T(8,128)(2,1)S(1)} %bitcast.9), channel_id=1, source_target_pairs={{1,32},{0,225},{33,64},{32,1},{65,96},{64,33},{97,128},{96,65},{12... | collective-permute-start | bytes 786440 | tf_op jit(solution)/shard_map/ppermute | solution.py:144
  58.0 0.0 collective-permute-done.1.refs_1_
  58.0 3.3 %collective-permute-start.3 = (bf16[64,2048]{1,0:T(8,128)(2,1)S(1)}, bf16[64,2048]{1,0:T(8,128)(2,1)S(1)}, u32[]{:S(2)}, u32[]{:S(2)}) collective-permute-start(bf16[64,2048]{1,0:T(8,128)(2,1)S(1)} %collective-permute-done.1.refs_1_), channel_id=1, source_target_pairs={{0,32},{1,225},{32,64},{33,1},{64,96},{65,33},{96,128},{97,65},{12... | collective-permute-start | bytes 786440 | tf_op jit(solution)/shard_map/ppermute | solution.py:144
  61.3 1.6 %collective-permute-done.2.refs_2_ = bf16[64,2048]{1,0:T(8,128)(2,1)S(1)} collective-permute-done((bf16[64,2048]{1,0:T(8,128)(2,1)S(1)}, bf16[64,2048]{1,0:T(8,128)(2,1)S(1)}, u32[]{:S(2)}, u32[]{:S(2)}) %collective-permute-start.2) | collective-permute-done | bytes 262176 | tf_op jit(solution)/shard_map/ppermute | solution.py:144
  62.9 4.7 %collective-permute-start.4 = (bf16[64,2048]{1,0:T(8,128)(2,1)S(1)}, bf16[64,2048]{1,0:T(8,128)(2,1)}, u32[]{:S(2)}, u32[]{:S(2)}) collective-permute-start(bf16[64,2048]{1,0:T(8,128)(2,1)S(1)} %collective-permute-done.2.refs_2_), channel_id=1, source_target_pairs={{0,32},{1,225},{32,64},{33,1},{64,96},{65,33},{96,128},{97,65},{12... | collective-permute-start | bytes 786440 | tf_op jit(solution)/shard_map/ppermute | solution.py:144
  67.6 0.0 collective-permute-done.3.refs_3_
  67.6 3.8 %collective-permute-start.5 = (bf16[64,2048]{1,0:T(8,128)(2,1)S(1)}, bf16[64,2048]{1,0:T(8,128)(2,1)}, u32[]{:S(2)}, u32[]{:S(2)}) collective-permute-start(bf16[64,2048]{1,0:T(8,128)(2,1)S(1)} %collective-permute-done.3.refs_3_), channel_id=1, source_target_pairs={{0,32},{1,225},{32,64},{33,1},{64,96},{65,33},{96,128},{97,65},{12... | collective-permute-start | bytes 786440 | tf_op jit(solution)/shard_map/ppermute | solution.py:144
  71.4 0.0 copy-start.1
  71.4 0.7 copy-done.1
  72.1 0.0 copy-done
  72.1 1.9 %collective-permute-start = (bf16[104,2048]{1,0:T(8,128)(2,1)S(1)}, bf16[104,2048]{1,0:T(8,128)(2,1)S(1)}, u32[]{:S(2)}, u32[]{:S(2)}) collective-permute-start(bf16[104,2048]{1,0:T(8,128)(2,1)S(1)} %copy-done), channel_id=1, source_target_pairs={{0,1},{1,0},{2,3},{3,2},{4,5},{5,4},{6,7},{7,6},{8,9},{9,8},{10,11... | collective-permute-start | bytes 1277960 | tf_op jit(solution)/shard_map/ppermute | solution.py:160
  74.0 0.0 collective-permute-done.4.refs_4_
  74.0 3.6 %collective-permute-start.6 = (bf16[64,2048]{1,0:T(8,128)(2,1)}, bf16[64,2048]{1,0:T(8,128)(2,1)S(1)}, u32[]{:S(2)}, u32[]{:S(2)}) collective-permute-start(bf16[64,2048]{1,0:T(8,128)(2,1)} %collective-permute-done.4.refs_4_), channel_id=1, source_target_pairs={{0,32},{1,225},{32,64},{33,1},{64,96},{65,33},{96,128},{97,65},{12... | collective-permute-start | bytes 786440 | tf_op jit(solution)/shard_map/ppermute | solution.py:144
  77.6 0.0 collective-permute-done.5.refs_5_
  77.6 2.2 %collective-permute-start.7 = (bf16[64,2048]{1,0:T(8,128)(2,1)}, bf16[64,2048]{1,0:T(8,128)(2,1)S(1)}, u32[]{:S(2)}, u32[]{:S(2)}) collective-permute-start(bf16[64,2048]{1,0:T(8,128)(2,1)} %collective-permute-done.5.refs_5_), channel_id=1, source_target_pairs={{0,32},{1,225},{32,64},{33,1},{64,96},{65,33},{96,128},{97,65},{12... | collective-permute-start | bytes 786440 | tf_op jit(solution)/shard_map/ppermute | solution.py:144
  79.8 0.0 collective-permute-done.other
  79.8 0.0 all-to-all-done.got
  79.8 1.2 %shard_map.51 = (bf16[224,512]{1,0:T(8,128)(2,1)S(1)}, bf16[224,2048]{1,0:T(8,128)(2,1)S(1)}, bf16[512,512]{1,0:T(8,128)(2,1)S(1)}) custom-call(s32[2]{0:T(128)S(1)} %pad_add_fusion.at, bf16[8,104,128]{2,1,0:T(8,128)(2,1)S(1)} %all-to-all-done.got, bf16[104,2048]{1,0:T(8,128)(2,1)S(1)} %copy-done, bf16[104,2048]{1,0:T(8,128)(2,1)S(1)} %collective-permute-done.other), custom_call_target="tpu_custom_call" | custom-call | bytes 2736136 | tf_op jit(solution)/shard_map/pallas_call | solution.py:39
  81.0 0.0 copy-start.2
  81.0 0.9 copy-done.2
  81.9 2.5 %shard_map.52 = (f32[224,2048]{1,0:T(8,128)S(1)}, bf16[224,512]{1,0:T(8,128)(2,1)S(1)}) custom-call(bf16[224,512]{1,0:T(8,128)(2,1)S(1)} %get-tuple-element.11.units, bf16[224,2048]{1,0:T(8,128)(2,1)S(1)} %get-tuple-element.9.weight, bf16[512,512]{1,0:T(8,128)(2,1)S(1)} %get-tuple-element.10.grouped, bf16[64,2048]{1,0:T(8,128)(2,1)S(1)} %bitcast.10, ...), custom_call_target="tpu_custom_call" | custom-call | flops 704643072 | bytes 5308416 | tf_op jit(solution)/shard_map/pallas_call | solution.py:39
  84.4 0.0 collective-permute-done.6.refs_0_
  84.4 0.8 collective-permute-done.7.refs_1_
  85.2 1.9 %shard_map.53 = bf16[8,104,128]{2,1,0:T(8,128)(2,1)} custom-call(s32[2]{0:T(128)S(1)} %pad_add_fusion.at, bf16[224,2048]{1,0:T(8,128)(2,1)S(1)} %get-tuple-element.9.weight, bf16[512,512]{1,0:T(8,128)(2,1)S(1)} %get-tuple-element.10.grouped, bf16[224,512]{1,0:T(8,128)(2,1)S(1)} %get-tuple-element.12.early, ...), custom_call_target="tpu_custom_call" | custom-call | flops 117440512 | bytes 2408456 | tf_op jit(solution)/shard_map/pallas_call | solution.py:39
  87.1 7.0 %all-to-all-start.3 = ((bf16[8,104,128]{2,1,0:T(8,128)(2,1)}), bf16[8,104,128]{2,1,0:T(8,128)(2,1)S(1)}, u32[]{:S(2)}, u32[]{:S(2)}) async-start(bf16[8,104,128]{2,1,0:T(8,128)(2,1)} %shard_map.53), calls=%async_computation.3 | async-start | bytes 425984 | tf_op jit(solution)/shard_map/all_to_all | solution.py:184
  94.0 0.4 shard_map.55
  94.4 1.9 %collective-permute-start.8 = (bf16[104,2048]{1,0:T(8,128)(2,1)S(1)}, bf16[104,2048]{1,0:T(8,128)(2,1)S(1)}, u32[]{:S(2)}, u32[]{:S(2)}) collective-permute-start(bf16[104,2048]{1,0:T(8,128)(2,1)S(1)} %get-tuple-element.15), channel_id=1, source_target_pairs={{0,1},{1,0},{2,3},{3,2},{4,5},{5,4},{6,7},{7,6},{8,9},{9,8},{10,11... | collective-permute-start | bytes 1277960 | tf_op jit(solution)/shard_map/ppermute | solution.py:189
  96.4 1.7 %collective-permute-done.8.taken = bf16[104,2048]{1,0:T(8,128)(2,1)S(1)} collective-permute-done((bf16[104,2048]{1,0:T(8,128)(2,1)S(1)}, bf16[104,2048]{1,0:T(8,128)(2,1)S(1)}, u32[]{:S(2)}, u32[]{:S(2)}) %collective-permute-start.8) | collective-permute-done | bytes 426016 | tf_op jit(solution)/shard_map/ppermute | solution.py:189
  98.1 0.8 shard_map.56
  98.9 1.9 %all-to-all-done.3.back = bf16[8,104,128]{2,1,0:T(8,128)(2,1)S(1)} async-done(((bf16[8,104,128]{2,1,0:T(8,128)(2,1)}), bf16[8,104,128]{2,1,0:T(8,128)(2,1)S(1)}, u32[]{:S(2)}, u32[]{:S(2)}) %all-to-all-start.3) | async-done | bytes 213024 | tf_op jit(solution)/shard_map/all_to_all | solution.py:184
  100.8 1.4 %shard_map.54 = bf16[104,256]{1,0:T(8,128)(2,1)} custom-call(s32[2]{0:T(128)S(1)} %pad_add_fusion.at, bf16[8,104,128]{2,1,0:T(8,128)(2,1)S(1)} %all-to-all-done.3.back), custom_call_target="tpu_custom_call" | custom-call | bytes 266248 | tf_op jit(solution)/shard_map/pallas_call | solution.py:39
  (4 shorter events, 0.1 us)
Async XLA Ops:
  0.6 71.5 %copy-start = (bf16[104,2048]{1,0:T(8,128)(2,1)S(1)}, bf16[104,2048]{1,0:T(8,128)(2,1)}, u32[]{:S(2)}) copy-start(bf16[104,2048]{1,0:T(8,128)(2,1)} %mine.1) | copy-start | bytes 1277956
  41.9 16.1 %collective-permute-start.1 = (bf16[64,2048]{1,0:T(8,128)(2,1)S(1)}, bf16[64,2048]{1,0:T(8,128)(2,1)S(1)}, u32[]{:S(2)}, u32[]{:S(2)}) collective-permute-start(bf16[64,2048]{1,0:T(8,128)(2,1)S(1)} %bitcast.8), channel_id=1, source_target_pairs={{0,32},{1,225},{32,64},{33,1},{64,96},{65,33},{96,128},{97,65},{12... | collective-permute-start | bytes 786440 | tf_op jit(solution)/shard_map/ppermute | solution.py:144
  47.0 0.8 copy-start.3
  49.3 30.5 %all-to-all-start = ((bf16[8,104,128]{2,1,0:T(8,128)(2,1)}), bf16[8,104,128]{2,1,0:T(8,128)(2,1)S(1)}, u32[]{:S(2)}, u32[]{:S(2)}) async-start(bf16[8,104,128]{2,1,0:T(8,128)(2,1)} %shard_map.50), calls=%async_computation | async-start | bytes 425984 | tf_op jit(solution)/shard_map/all_to_all | solution.py:159
  54.8 8.1 %collective-permute-start.2 = (bf16[64,2048]{1,0:T(8,128)(2,1)S(1)}, bf16[64,2048]{1,0:T(8,128)(2,1)S(1)}, u32[]{:S(2)}, u32[]{:S(2)}) collective-permute-start(bf16[64,2048]{1,0:T(8,128)(2,1)S(1)} %bitcast.9), channel_id=1, source_target_pairs={{1,32},{0,225},{33,64},{32,1},{65,96},{64,33},{97,128},{96,65},{12... | collective-permute-start | bytes 786440 | tf_op jit(solution)/shard_map/ppermute | solution.py:144
  58.0 9.6 %collective-permute-start.3 = (bf16[64,2048]{1,0:T(8,128)(2,1)S(1)}, bf16[64,2048]{1,0:T(8,128)(2,1)S(1)}, u32[]{:S(2)}, u32[]{:S(2)}) collective-permute-start(bf16[64,2048]{1,0:T(8,128)(2,1)S(1)} %collective-permute-done.1.refs_1_), channel_id=1, source_target_pairs={{0,32},{1,225},{32,64},{33,1},{64,96},{65,33},{96,128},{97,65},{12... | collective-permute-start | bytes 786440 | tf_op jit(solution)/shard_map/ppermute | solution.py:144
  62.9 11.1 %collective-permute-start.4 = (bf16[64,2048]{1,0:T(8,128)(2,1)S(1)}, bf16[64,2048]{1,0:T(8,128)(2,1)}, u32[]{:S(2)}, u32[]{:S(2)}) collective-permute-start(bf16[64,2048]{1,0:T(8,128)(2,1)S(1)} %collective-permute-done.2.refs_2_), channel_id=1, source_target_pairs={{0,32},{1,225},{32,64},{33,1},{64,96},{65,33},{96,128},{97,65},{12... | collective-permute-start | bytes 786440 | tf_op jit(solution)/shard_map/ppermute | solution.py:144
  67.6 10.0 %collective-permute-start.5 = (bf16[64,2048]{1,0:T(8,128)(2,1)S(1)}, bf16[64,2048]{1,0:T(8,128)(2,1)}, u32[]{:S(2)}, u32[]{:S(2)}) collective-permute-start(bf16[64,2048]{1,0:T(8,128)(2,1)S(1)} %collective-permute-done.3.refs_3_), channel_id=1, source_target_pairs={{0,32},{1,225},{32,64},{33,1},{64,96},{65,33},{96,128},{97,65},{12... | collective-permute-start | bytes 786440 | tf_op jit(solution)/shard_map/ppermute | solution.py:144
  71.4 0.7 copy-start.1
  72.1 7.7 %collective-permute-start = (bf16[104,2048]{1,0:T(8,128)(2,1)S(1)}, bf16[104,2048]{1,0:T(8,128)(2,1)S(1)}, u32[]{:S(2)}, u32[]{:S(2)}) collective-permute-start(bf16[104,2048]{1,0:T(8,128)(2,1)S(1)} %copy-done), channel_id=1, source_target_pairs={{0,1},{1,0},{2,3},{3,2},{4,5},{5,4},{6,7},{7,6},{8,9},{9,8},{10,11... | collective-permute-start | bytes 1277960 | tf_op jit(solution)/shard_map/ppermute | solution.py:160
  74.0 10.4 %collective-permute-start.6 = (bf16[64,2048]{1,0:T(8,128)(2,1)}, bf16[64,2048]{1,0:T(8,128)(2,1)S(1)}, u32[]{:S(2)}, u32[]{:S(2)}) collective-permute-start(bf16[64,2048]{1,0:T(8,128)(2,1)} %collective-permute-done.4.refs_4_), channel_id=1, source_target_pairs={{0,32},{1,225},{32,64},{33,1},{64,96},{65,33},{96,128},{97,65},{12... | collective-permute-start | bytes 786440 | tf_op jit(solution)/shard_map/ppermute | solution.py:144
  77.6 7.6 %collective-permute-start.7 = (bf16[64,2048]{1,0:T(8,128)(2,1)}, bf16[64,2048]{1,0:T(8,128)(2,1)S(1)}, u32[]{:S(2)}, u32[]{:S(2)}) collective-permute-start(bf16[64,2048]{1,0:T(8,128)(2,1)} %collective-permute-done.5.refs_5_), channel_id=1, source_target_pairs={{0,32},{1,225},{32,64},{33,1},{64,96},{65,33},{96,128},{97,65},{12... | collective-permute-start | bytes 786440 | tf_op jit(solution)/shard_map/ppermute | solution.py:144
  81.0 1.0 copy-start.2
  87.1 13.8 %all-to-all-start.3 = ((bf16[8,104,128]{2,1,0:T(8,128)(2,1)}), bf16[8,104,128]{2,1,0:T(8,128)(2,1)S(1)}, u32[]{:S(2)}, u32[]{:S(2)}) async-start(bf16[8,104,128]{2,1,0:T(8,128)(2,1)} %shard_map.53), calls=%async_computation.3 | async-start | bytes 425984 | tf_op jit(solution)/shard_map/all_to_all | solution.py:184
  94.4 3.7 %collective-permute-start.8 = (bf16[104,2048]{1,0:T(8,128)(2,1)S(1)}, bf16[104,2048]{1,0:T(8,128)(2,1)S(1)}, u32[]{:S(2)}, u32[]{:S(2)}) collective-permute-start(bf16[104,2048]{1,0:T(8,128)(2,1)S(1)} %get-tuple-element.15), channel_id=1, source_target_pairs={{0,1},{1,0},{2,3},{3,2},{4,5},{5,4},{6,7},{7,6},{8,9},{9,8},{10,11... | collective-permute-start | bytes 1277960 | tf_op jit(solution)/shard_map/ppermute | solution.py:189

commit v2 on v1

--- a/solution.py
+++ b/solution.py
@@ -49,8 +49,8 @@
 
 def token_at(p, y):
     core, q, x, zh = p >> 7, (p >> 4) & 7, (p >> 2) & 3, p & 3
-    step = (q + 1) >> 1
-    flip = jnp.where(((q & 1) == 0) & (q > 0), 1, 0)
+    step = jnp.where(q == 1, 4, q >> 1)
+    flip = jnp.where(q == 1, 0, q & 1)
     row = (y + jnp.where(core == 0, -step, step)) & 7
     return row * 32 + x * 8 + zh * 2 + (core ^ flip)
 
@@ -59,27 +59,25 @@
     return lax.broadcasted_iota(jnp.int32, shape, dim)
 
 
-def hidden_body(at, hidden, sent):
-    hot = (iota((TOK, TOK), 0) == token_at(iota((TOK, TOK), 1), at[1])).astype(BF16)
-    ordered = dot(hidden[...], hot, 1, 0).astype(BF16)
-    for g in range(DP):
-        for c in range(CORE):
-            sent[g * CORE + c] = ordered[:, c * HALF:(c + 1) * HALF]
-
-
-def units_body(ff, pad, at, got, mine, other, units, weight, grouped):
-    me = at[0]
-    a = iota((CHUNKS * ROWS, CHUNKS * ROWS), 0)
-    b = iota((CHUNKS * ROWS, CHUNKS * ROWS), 1)
+def units_body(ff, pad, at, held, partner, mine, other, units, weight, grouped, hot_last):
+    me, y, g = at[0], at[1], at[2]
+    total = CHUNKS * ROWS
+    a = iota((total, total), 0)
     place = ((a >> 2) & 3) * HALF + (a >> 6) * 16 + ((a >> 4) & 3) * 4 + (a & 3)
-    hot = (place == b).astype(BF16)
-    grouped[...] = hot
-    gap = jnp.zeros((pad - ff, CHUNKS * ROWS), F32)
-    rows = []
+    grouped[...] = (place == iota((total, total), 1)).astype(BF16)
+    p = iota((1, total), 1)
+    slot = me * HALF + (p >> 6) * 16 + ((p >> 4) & 3) * 4 + (p & 3)
+    group = (p >> 2) & 3
+    token = token_at(slot, y)
+    hot_last[...] = (token_at(iota((TOK, TOK), 0), y) == iota((TOK, TOK), 1)).astype(BF16)
+    gap = jnp.zeros((pad - ff, total), F32)
     for j in range(CORE):
-        rows.append(jnp.concatenate([got[g * CORE + (me ^ j)] for g in range(DP)], axis=1))
-    for j in range(CORE):
-        moved = dot(rows[j], hot, 1, 1)
+        moved = None
+        for k in range(DP):
+            wanted = jnp.where(group == ((g - k) & 3), token, -1)
+            hot = (iota((TOK, total), 0) == wanted).astype(BF16)
+            term = dot((held, partner)[j][k], hot, 1, 0)
+            moved = term if moved is None else moved + term
         units[pl.ds(j * pad, pad)] = jnp.concatenate([moved, gap], axis=0).astype(BF16)
     blank = jnp.zeros((pad - ff, mine.shape[1]), BF16)
     weight[pl.ds(0, ff)] = mine[...]
@@ -88,17 +86,23 @@
     weight[pl.ds(pad + ff, pad - ff)] = blank
 
 
-def early_body(units, weight, grouped, *refs):
-    chunks, (grad, parts) = refs[:EARLY], refs[EARLY:]
-    n = EARLY * ROWS
+def early_body(first, units, weight, grouped, *refs):
+    grad, parts = refs[-2:]
+    before, chunks = (refs[:2], refs[2:-2]) if first > 0 else (None, refs[:-2])
+    n = len(chunks) * ROWS
+    start = first * ROWS
     width = weight.shape[1]
     inner = jnp.concatenate([c[...] for c in chunks], axis=0)
     ig = dot(weight[...], inner, 1, 1).astype(BF16)
-    parts[...] = dot(ig, grouped[pl.ds(0, n)], 1, 0).astype(BF16)
-    left = units[:, :n]
+    moved = dot(ig, grouped[pl.ds(start, n)], 1, 0)
+    if before:
+        moved = moved + before[1][...].astype(F32)
+    parts[...] = moved.astype(BF16)
+    left = units[:, start:start + n]
     for j in range(0, width, 512):
         cols = jnp.concatenate([c[:, j:j + 512] for c in chunks], axis=0)
-        grad[:, j:j + 512] = dot(left, cols, 1, 0)
+        total = dot(left, cols, 1, 0)
+        grad[:, j:j + 512] = before[0][:, j:j + 512] + total if before else total
 
 
 def parts_body(ff, pad, at, weight, grouped, early, *refs):
@@ -125,15 +129,14 @@
         give[:, k:k + 512] = total[pad:pad + ff].astype(BF16)
 
 
-def final_body(at, back, out):
-    hot = (token_at(iota((TOK, TOK), 0), at[1]) == iota((TOK, TOK), 1)).astype(BF16)
+def final_body(hot, back, out):
     halves = []
     for c in range(CORE):
         total = back[c].astype(F32)
         for g in range(1, DP):
             total = total + back[g * CORE + c].astype(F32)
         halves.append(total.astype(BF16))
-    out[...] = dot(jnp.concatenate(halves, axis=1), hot, 1, 0).astype(BF16)
+    out[...] = dot(jnp.concatenate(halves, axis=1), hot[...], 1, 0).astype(BF16)
 
 
 def add_body(keep, taken, out):
@@ -147,21 +150,31 @@
 def step(hidden, out_grad, down_weight):
     ff, width = down_weight.shape
     pad = -(-ff // 16) * 16
-    at = jnp.stack([lax.axis_index("core"), lax.axis_index("y")]).astype(jnp.int32)
+    at = jnp.stack([lax.axis_index(name) for name in ("core", "y", "dp")]).astype(jnp.int32)
 
     row = jnp.broadcast_to(out_grad.reshape(DP, 1, 2, width // 2), (DP, ZH, 2, width // 2))
     row = row.reshape(DP * ZH, 2, width // 2)
     mine = lax.all_to_all(row, ("dp", "zh"), 0, 0, tiled=True).reshape(DP * ZH, width)
     spread = jnp.broadcast_to(mine[None], (X, DP * ZH, width))
     u0 = lax.all_to_all(spread, "x", 0, 0, tiled=True).reshape(ROWS, width)
-
-    (sent,) = call(hidden_body, [((DP * CORE, ff, HALF), BF16)], at, hidden.T)
-    got = lax.all_to_all(sent, ("dp", "core"), 0, 0, tiled=True)
+    away = lax.ppermute(mine, "y", [(y, (y + Y // 2) % Y) for y in range(Y)])
+    away = jnp.broadcast_to(away[None], (X, DP * ZH, width))
+    u4 = lax.all_to_all(away, "x", 0, 0, tiled=True).reshape(ROWS, width)
+
+    here = hidden.T
+    there = []
+    for k in range(1, DP):
+        there.append(lax.ppermute(here, "dp", [(g, (g + k) % DP) for g in range(DP)]))
+    held = jnp.stack([here] + there)
+    partner = lax.ppermute(held, "core", SWAP)
     other = lax.ppermute(down_weight, "core", SWAP)
-    units, weight, grouped = call(
+    units, weight, grouped, hot = call(
         functools.partial(units_body, ff, pad),
-        [((2 * pad, CHUNKS * ROWS), BF16), ((2 * pad, width), BF16), ((CHUNKS * ROWS, CHUNKS * ROWS), BF16)],
-        at, got, down_weight, other,
+        [
+            ((2 * pad, CHUNKS * ROWS), BF16), ((2 * pad, width), BF16),
+            ((CHUNKS * ROWS, CHUNKS * ROWS), BF16), ((TOK, TOK), BF16),
+        ],
+        at, held, partner, down_weight, other,
     )
 
     u1 = ring(u0)
@@ -170,25 +183,28 @@
     v2 = ring(v1)
     u3 = ring(u2)
     v3 = ring(v2)
-    u4 = ring(u3)
 
     flops = 4 * pad * width * ROWS * CORE
+    shapes = [((2 * pad, width), F32), ((2 * pad, CHUNKS * ROWS), BF16)]
     grad, parts = call(
-        early_body, [((2 * pad, width), F32), ((2 * pad, CHUNKS * ROWS), BF16)],
-        units, weight, grouped, u0, u1, v1, u2, v2, u3, flops=EARLY * flops,
+        functools.partial(early_body, 0), shapes, units, weight, grouped, u0, u4, u1, v1, flops=4 * flops
+    )
+    grad, parts = call(
+        functools.partial(early_body, 4), shapes, units, weight, grouped, grad, parts, u2, v2,
+        flops=2 * flops, aliases={3: 0, 4: 1},
     )
     (parts,) = call(
         functools.partial(parts_body, ff, pad), [((DP * CORE, ff, HALF), BF16)],
-        at, weight, grouped, parts, v3, u4, flops=flops,
+        at, weight, grouped, parts, u3, v3, flops=2 * flops,
     )
     back = lax.all_to_all(parts, ("dp", "core"), 0, 0, tiled=True)
     keep, give = call(
         functools.partial(late_body, ff, pad), [((ff, width), F32), ((ff, width), BF16)],
-        units, grad, v3, u4, flops=flops,
+        units, grad, u3, v3, flops=2 * flops,
     )
     taken = lax.ppermute(give, "core", SWAP)
     (weight_grad,) = call(add_body, [((ff, width), BF16)], keep, taken)
-    (input_grad,) = call(final_body, [((ff, TOK), BF16)], at, back)
+    (input_grad,) = call(final_body, [((ff, TOK), BF16)], hot, back)
     return input_grad.T, weight_grad
 
 

time: 103 us -> 124 us (1.20)
  starting transfers between devices: 42.1 us -> 57.2 us
  local copies, waits for them, and re-layouts: 2.54 us -> 7.38 us
    ppermute x0 -> x5, starting transfers between devices: none -> 17.5 us  [the longest x3 8.18 us: step(): lax.ppermute(here, 'dp', [(g, (g + k) % DP) for g in range(DP)])]
    unnamed x9 -> x25, local copies, waits for them, and re-layouts: 2.47 us -> 6.56 us
    ppermute x0 -> x5, waiting for transfers between devices: none -> 2.3 us  [the longest x3 2.3 us: step(): lax.ppermute(here, 'dp', [(g, (g + k) % DP) for g in range(DP)])]
    all_to_all x1, starting transfers between devices: 5.49 us -> 3.4 us  [step(): u4 = lax.all_to_all(away, 'x', 0, 0, tiled=True).reshape(ROWS, width)]
    ppermute x7 -> x6, waiting for transfers between devices: 2.4 us -> 0.35 us  [ring(): return lax.ppermute(value, ('y', 'core'), ring_pairs(cross))]
    ppermute x1, starting transfers between devices: 1.91 us -> 3.54 us  [step(): other = lax.ppermute(down_weight, 'core', SWAP)]
    all_to_all x1, starting transfers between devices: 6.96 us -> 5.66 us  [step(): back = lax.all_to_all(parts, ('dp', 'core'), 0, 0, tiled=True)]
    ppermute x7 -> x6, starting transfers between devices: 25.8 us -> 25 us  [ring(): return lax.ppermute(value, ('y', 'core'), ring_pairs(cross))]
  transfers between devices with their start and end apart: 11 -> 15, of which waited for: 4 -> 4; matrix products, arithmetic and copies ran while one was open for 0% -> 1% of each run, Pallas kernels for 6% -> 6%
where the time goes in v2:
time: 124 us; the launch traced here: 123 us
  starting transfers between devices  57.2 us (46%)
  blocking collectives  40.2 us (32%)
  Pallas kernels  9.9 us (8%)
  local copies, waits for them, and re-layouts  7.38 us (6%)
  waiting for transfers between devices  5.15 us (4%)
  other arithmetic  1.82 us (1%)
    all_to_all x1, blocking collectives, step(): lax.all_to_all(row, ('dp', 'zh'), 0, 0, tiled=True).reshape(DP * ZH, width)  30.9 us
    ppermute x6, starting transfers between devices, ring(): return lax.ppermute(value, ('y', 'core'), ring_pairs(cross))  25 us
    pallas_call x7, Pallas kernels, call(): pl.pallas_call(body, out_shape=outs, in_specs=specs, out_specs=[VMEM] * l...  9.9 us
    all_to_all x1, blocking collectives, step(): u0 = lax.all_to_all(spread, 'x', 0, 0, tiled=True).reshape(ROWS, width)  9.34 us
    ppermute x3, starting transfers between devices, step(): lax.ppermute(here, 'dp', [(g, (g + k) % DP) for g in range(DP)])  8.18 us
    unnamed x25, local copies, waits for them, and re-layouts  6.56 us
    ppermute x1, starting transfers between devices, step(): away = lax.ppermute(mine, 'y', [(y, (y + Y // 2) % Y) for y in range(Y)])  6.43 us
    all_to_all x1, starting transfers between devices, step(): back = lax.all_to_all(parts, ('dp', 'core'), 0, 0, tiled=True)  5.66 us
  transfers between devices with their start and end apart: 15, of which 4 were waited for; matrix products, arithmetic and copies ran while one was open for 1% of the time, Pallas kernels for 6%

profile of v2, /device:TPU:1, one launch (start us, length us, event | category | flops | bytes accessed | tf_op | source)
XLA Modules:
  0.0 122.5 jit_solution(12352719933211899507)
XLA Ops:
  0.6 0.0 copy-start.5
  0.6 0.9 reduce
  1.6 30.9 %all_to_all.20 = bf16[16,2,1024]{2,1,0:T(2,128)(2,1)S(1)} all-to-all(bf16[16,2,1024]{2,1,0:T(2,128)(2,1)S(1)} %bitcast.21), channel_id=1, replica_groups=mesh['dp'=4,'y'=8,'x'=4,'zh'=4,'core'=2] {'dp','zh'}, dimensions={0} | all-to-all | bytes 131072 | tf_op jit(solution)/shard_map/all_to_all | solution.py:157
  32.5 9.3 %all_to_all.21 = bf16[4,16,2048]{2,1,0:T(8,128)(2,1)S(1)} all-to-all(bf16[4,16,2048]{2,1,0:T(8,128)(2,1)S(1)} %broadcast_in_dim.23), channel_id=1, replica_groups=mesh['dp'=4,'y'=8,'x'=4,'zh'=4,'core'=2] {'x'}, dimensions={0} | all-to-all | bytes 524288 | tf_op jit(solution)/shard_map/all_to_all | solution.py:159
  41.9 5.1 %collective-permute-start.6 = (bf16[64,2048]{1,0:T(8,128)(2,1)S(1)}, bf16[64,2048]{1,0:T(8,128)(2,1)S(1)}, u32[]{:S(2)}, u32[]{:S(2)}) collective-permute-start(bf16[64,2048]{1,0:T(8,128)(2,1)S(1)} %bitcast.15), channel_id=1, source_target_pairs={{0,32},{1,225},{32,64},{33,1},{64,96},{65,33},{96,128},{97,65},{12... | collective-permute-start | bytes 786440 | tf_op jit(solution)/shard_map/ppermute | solution.py:147
  47.0 5.3 %collective-permute-start.7 = (bf16[64,2048]{1,0:T(8,128)(2,1)S(1)}, bf16[64,2048]{1,0:T(8,128)(2,1)S(1)}, u32[]{:S(2)}, u32[]{:S(2)}) collective-permute-start(bf16[64,2048]{1,0:T(8,128)(2,1)S(1)} %bitcast.16), channel_id=1, source_target_pairs={{1,32},{0,225},{33,64},{32,1},{65,96},{64,33},{97,128},{96,65},{12... | collective-permute-start | bytes 786440 | tf_op jit(solution)/shard_map/ppermute | solution.py:147
  52.2 0.0 copy-start
  52.3 0.7 copy-done
  53.0 0.0 collective-permute-done.6.refs_2_
  53.0 3.3 %collective-permute-start.8 = (bf16[64,2048]{1,0:T(8,128)(2,1)S(1)}, bf16[64,2048]{1,0:T(8,128)(2,1)}, u32[]{:S(2)}, u32[]{:S(2)}) collective-permute-start(bf16[64,2048]{1,0:T(8,128)(2,1)S(1)} %collective-permute-done.6.refs_2_), channel_id=1, source_target_pairs={{0,32},{1,225},{32,64},{33,1},{64,96},{65,33},{96,128},{97,65},{12... | collective-permute-start | bytes 786440 | tf_op jit(solution)/shard_map/ppermute | solution.py:147
  56.2 0.3 collective-permute-done.7.refs_3_
  56.6 3.0 %collective-permute-start.9 = (bf16[64,2048]{1,0:T(8,128)(2,1)S(1)}, bf16[64,2048]{1,0:T(8,128)(2,1)}, u32[]{:S(2)}, u32[]{:S(2)}) collective-permute-start(bf16[64,2048]{1,0:T(8,128)(2,1)S(1)} %collective-permute-done.7.refs_3_), channel_id=1, source_target_pairs={{0,32},{1,225},{32,64},{33,1},{64,96},{65,33},{96,128},{97,65},{12... | collective-permute-start | bytes 786440 | tf_op jit(solution)/shard_map/ppermute | solution.py:147
  59.6 2.8 %collective-permute-start.2 = (bf16[104,256]{1,0:T(8,128)(2,1)}, bf16[104,256]{1,0:T(8,128)(2,1)S(1)}, u32[]{:S(2)}, u32[]{:S(2)}) collective-permute-start(bf16[104,256]{1,0:T(8,128)(2,1)} %bitcast.24), channel_id=1, source_target_pairs={{0,768},{256,0},{512,256},{768,512},{1,769},{257,1},{513,257},{769... | collective-permute-start | bytes 159752 | tf_op jit(solution)/shard_map/ppermute | solution.py:167
  62.4 3.5 %collective-permute-start.4 = (bf16[104,2048]{1,0:T(8,128)(2,1)}, bf16[104,2048]{1,0:T(8,128)(2,1)S(1)}, u32[]{:S(2)}, u32[]{:S(2)}) collective-permute-start(bf16[104,2048]{1,0:T(8,128)(2,1)} %mine.1), channel_id=1, source_target_pairs={{0,1},{1,0},{2,3},{3,2},{4,5},{5,4},{6,7},{7,6},{8,9},{9,8},{10,11... | collective-permute-start | bytes 1277960 | tf_op jit(solution)/shard_map/ppermute | solution.py:170
  66.0 2.9 %collective-permute-start.1 = (bf16[104,256]{1,0:T(8,128)(2,1)}, bf16[104,256]{1,0:T(8,128)(2,1)S(1)}, u32[]{:S(2)}, u32[]{:S(2)}) collective-permute-start(bf16[104,256]{1,0:T(8,128)(2,1)} %bitcast.25), channel_id=1, source_target_pairs={{0,512},{256,768},{512,0},{768,256},{1,513},{257,769},{513,1},{769... | collective-permute-start | bytes 159752 | tf_op jit(solution)/shard_map/ppermute | solution.py:167
  68.9 2.5 %collective-permute-start = (bf16[104,256]{1,0:T(8,128)(2,1)}, bf16[104,256]{1,0:T(8,128)(2,1)S(1)}, u32[]{:S(2)}, u32[]{:S(2)}) collective-permute-start(bf16[104,256]{1,0:T(8,128)(2,1)} %bitcast.26), channel_id=1, source_target_pairs={{0,256},{256,512},{512,768},{768,0},{1,257},{257,513},{513,769},{7... | collective-permute-start | bytes 159752 | tf_op jit(solution)/shard_map/ppermute | solution.py:167
  71.3 2.3 %collective-permute-done.1 = bf16[104,256]{1,0:T(8,128)(2,1)S(1)} collective-permute-done((bf16[104,256]{1,0:T(8,128)(2,1)}, bf16[104,256]{1,0:T(8,128)(2,1)S(1)}, u32[]{:S(2)}, u32[]{:S(2)}) %collective-permute-start.1) | collective-permute-done | bytes 53280 | tf_op jit(solution)/shard_map/ppermute | solution.py:167
  73.6 6.4 %collective-permute-start.5 = (bf16[16,2048]{1,0:T(8,128)(2,1)S(1)}, bf16[16,2048]{1,0:T(8,128)(2,1)S(1)}, u32[]{:S(2)}, u32[]{:S(2)}) collective-permute-start(bf16[16,2048]{1,0:T(8,128)(2,1)S(1)} %bitcast.20), channel_id=1, source_target_pairs={{0,128},{32,160},{64,192},{96,224},{128,0},{160,32},{192,64},{224,... | collective-permute-start | bytes 196616 | tf_op jit(solution)/shard_map/ppermute | solution.py:160
  80.1 0.8 pad_maximum_fusion.held
  80.9 2.9 %collective-permute-start.3 = (bf16[4,104,256]{2,1,0:T(8,128)(2,1)S(1)}, bf16[4,104,256]{2,1,0:T(8,128)(2,1)S(1)}, u32[]{:S(2)}, u32[]{:S(2)}) collective-permute-start(bf16[4,104,256]{2,1,0:T(8,128)(2,1)S(1)} %pad_maximum_fusion.held), channel_id=1, source_target_pairs={{0,1},{1,0},{2,3},{3,2},{4,5},{5,4},{6,7},{7,6},{8,9},{9,8},{10,11... | collective-permute-start | bytes 638984 | tf_op jit(solution)/shard_map/ppermute | solution.py:169
  83.9 0.7 broadcast_in_dim.24
  84.6 3.4 %all-to-all-start.2 = ((bf16[4,16,2048]{2,1,0:T(8,128)(2,1)}), bf16[4,16,2048]{2,1,0:T(8,128)(2,1)S(1)}, u32[]{:S(2)}, u32[]{:S(2)}) async-start(bf16[4,16,2048]{2,1,0:T(8,128)(2,1)} %broadcast_in_dim.24), calls=%async_computation.2 | async-start | bytes 524288 | tf_op jit(solution)/shard_map/all_to_all | solution.py:162
  88.0 0.0 collective-permute-done.8.refs_2_
  88.0 4.8 %collective-permute-start.10 = (bf16[64,2048]{1,0:T(8,128)(2,1)}, bf16[64,2048]{1,0:T(8,128)(2,1)}, u32[]{:S(2)}, u32[]{:S(2)}) collective-permute-start(bf16[64,2048]{1,0:T(8,128)(2,1)} %collective-permute-done.8.refs_2_), channel_id=1, source_target_pairs={{0,32},{1,225},{32,64},{33,1},{64,96},{65,33},{96,128},{97,65},{12... | collective-permute-start | bytes 786440 | tf_op jit(solution)/shard_map/ppermute | solution.py:147
  92.9 3.6 %collective-permute-start.11 = (bf16[64,2048]{1,0:T(8,128)(2,1)}, bf16[64,2048]{1,0:T(8,128)(2,1)}, u32[]{:S(2)}, u32[]{:S(2)}) collective-permute-start(bf16[64,2048]{1,0:T(8,128)(2,1)} %collective-permute-done.9.refs_3_), channel_id=1, source_target_pairs={{0,32},{1,225},{32,64},{33,1},{64,96},{65,33},{96,128},{97,65},{12... | collective-permute-start | bytes 786440 | tf_op jit(solution)/shard_map/ppermute | solution.py:147
  96.4 0.1 pad_add_fusion.at
  96.5 0.0 collective-permute-done.4.other
  96.5 1.5 %shard_map.50 = (bf16[224,512]{1,0:T(8,128)(2,1)S(1)}, bf16[224,2048]{1,0:T(8,128)(2,1)S(1)}, bf16[512,512]{1,0:T(8,128)(2,1)S(1)}, bf16[256,256]{1,0:T(8,128)(2,1)S(1)}) custom-call(s32[3]{0:T(128)S(1)} %pad_add_fusion.at, bf16[4,104,256]{2,1,0:T(8,128)(2,1)S(1)} %pad_maximum_fusion.held, bf16[4,104,256]{2,1,0:T(8,128)(2,1)S(1)} %collective-permute-done.3.partner, ...), custom_call_target="tpu_custom_call" | custom-call | bytes 3080204 | tf_op jit(solution)/shard_map/pallas_call | solution.py:39
  98.1 0.6 copy-done.10
  98.7 0.0 all-to-all-done.2
  98.7 0.7 copy-done.2
  99.4 0.9 copy-done.1
  100.4 0.9 copy-done.3
  101.3 0.9 copy-done.7
  102.3 0.9 copy-done.9
  103.2 1.4 %shard_map.51 = (f32[224,2048]{1,0:T(8,128)S(1)}, bf16[224,512]{1,0:T(8,128)(2,1)S(1)}) custom-call(bf16[224,512]{1,0:T(8,128)(2,1)S(1)} %get-tuple-element.15.units, bf16[224,2048]{1,0:T(8,128)(2,1)S(1)} %get-tuple-element.13.weight, bf16[512,512]{1,0:T(8,128)(2,1)S(1)} %get-tuple-element.14.grouped, bf16[64,2048]{1,0:T(8,128)(2,1)S(1)} %bitcast.17, ...), custom_call_target="tpu_custom_call" | custom-call | flops 469762048 | bytes 4784128 | tf_op jit(solution)/shard_map/pallas_call | solution.py:39
  104.6 2.3 %shard_map.52 = (f32[224,2048]{1,0:T(8,128)S(1)}, bf16[224,512]{1,0:T(8,128)(2,1)S(1)}) custom-call(bf16[224,512]{1,0:T(8,128)(2,1)S(1)} %get-tuple-element.15.units, bf16[224,2048]{1,0:T(8,128)(2,1)S(1)} %get-tuple-element.13.weight, bf16[512,512]{1,0:T(8,128)(2,1)S(1)} %get-tuple-element.14.grouped, ...), custom_call_target="tpu_custom_call", output_to_operand_aliasing={{0}: (3, {}), {1}: (4, {})} | custom-call | flops 234881024 | bytes 6324224 | tf_op jit(solution)/shard_map/pallas_call | solution.py:39
  106.9 0.0 collective-permute-done.10.refs_0_
  106.9 0.0 collective-permute-done.11.refs_1_
  106.9 1.7 %shard_map.53 = bf16[8,104,128]{2,1,0:T(8,128)(2,1)S(1)} custom-call(s32[3]{0:T(128)S(1)} %pad_add_fusion.at, bf16[224,2048]{1,0:T(8,128)(2,1)S(1)} %get-tuple-element.13.weight, bf16[512,512]{1,0:T(8,128)(2,1)S(1)} %get-tuple-element.14.grouped, bf16[224,512]{1,0:T(8,128)(2,1)S(1)} %get-tuple-element.18.early, ...), custom_call_target="tpu_custom_call" | custom-call | flops 234881024 | bytes 2408460 | tf_op jit(solution)/shard_map/pallas_call | solution.py:39
  108.6 0.7 copy-done.4
  109.3 5.7 %all-to-all-start.3 = ((bf16[8,104,128]{2,1,0:T(8,128)(2,1)}), bf16[8,104,128]{2,1,0:T(8,128)(2,1)S(1)}, u32[]{:S(2)}, u32[]{:S(2)}) async-start(bf16[8,104,128]{2,1,0:T(8,128)(2,1)} %copy-done.4), calls=%async_computation.3 | async-start | bytes 425984 | tf_op jit(solution)/shard_map/all_to_all | solution.py:200
  115.0 1.4 %shard_map.55 = (f32[104,2048]{1,0:T(8,128)S(1)}, bf16[104,2048]{1,0:T(8,128)(2,1)S(1)}) custom-call(bf16[224,512]{1,0:T(8,128)(2,1)S(1)} %get-tuple-element.15.units, f32[224,2048]{1,0:T(8,128)S(1)} %get-tuple-element.19.grad, bf16[64,2048]{1,0:T(8,128)(2,1)} %collective-permute-done.10.refs_0_, bf16[64,2048]{1,0:T(8,128)(2,1)} %collective-permute-done.11.refs_1_), custom_call_target="tpu_custom_call" | custom-call | flops 234881024 | bytes 3866624 | tf_op jit(solution)/shard_map/pallas_call | solution.py:39
  116.4 2.0 %collective-permute-start.12 = (bf16[104,2048]{1,0:T(8,128)(2,1)S(1)}, bf16[104,2048]{1,0:T(8,128)(2,1)S(1)}, u32[]{:S(2)}, u32[]{:S(2)}) collective-permute-start(bf16[104,2048]{1,0:T(8,128)(2,1)S(1)} %get-tuple-element.21), channel_id=1, source_target_pairs={{0,1},{1,0},{2,3},{3,2},{4,5},{5,4},{6,7},{7,6},{8,9},{9,8},{10,11... | collective-permute-start | bytes 1277960 | tf_op jit(solution)/shard_map/ppermute | solution.py:205
  118.4 1.6 %collective-permute-done.12.taken = bf16[104,2048]{1,0:T(8,128)(2,1)S(1)} collective-permute-done((bf16[104,2048]{1,0:T(8,128)(2,1)S(1)}, bf16[104,2048]{1,0:T(8,128)(2,1)S(1)}, u32[]{:S(2)}, u32[]{:S(2)}) %collective-permute-start.12) | collective-permute-done | bytes 426016 | tf_op jit(solution)/shard_map/ppermute | solution.py:205
  120.1 0.8 shard_map.56
  120.9 0.9 all-to-all-done.3.back
  121.8 0.8 shard_map.54
  (23 shorter events, 0.1 us)
Async XLA Ops:
  0.6 95.9 %copy-start.5 = (bf16[104,2048]{1,0:T(8,128)(2,1)S(1)}, bf16[104,2048]{1,0:T(8,128)(2,1)}, u32[]{:S(2)}) copy-start(bf16[104,2048]{1,0:T(8,128)(2,1)} %mine.1) | copy-start | bytes 1277956
  41.9 11.1 %collective-permute-start.6 = (bf16[64,2048]{1,0:T(8,128)(2,1)S(1)}, bf16[64,2048]{1,0:T(8,128)(2,1)S(1)}, u32[]{:S(2)}, u32[]{:S(2)}) collective-permute-start(bf16[64,2048]{1,0:T(8,128)(2,1)S(1)} %bitcast.15), channel_id=1, source_target_pairs={{0,32},{1,225},{32,64},{33,1},{64,96},{65,33},{96,128},{97,65},{12... | collective-permute-start | bytes 786440 | tf_op jit(solution)/shard_map/ppermute | solution.py:147
  47.0 9.6 %collective-permute-start.7 = (bf16[64,2048]{1,0:T(8,128)(2,1)S(1)}, bf16[64,2048]{1,0:T(8,128)(2,1)S(1)}, u32[]{:S(2)}, u32[]{:S(2)}) collective-permute-start(bf16[64,2048]{1,0:T(8,128)(2,1)S(1)} %bitcast.16), channel_id=1, source_target_pairs={{1,32},{0,225},{33,64},{32,1},{65,96},{64,33},{97,128},{96,65},{12... | collective-permute-start | bytes 786440 | tf_op jit(solution)/shard_map/ppermute | solution.py:147
  52.2 0.7 copy-start
  53.0 43.6 %copy-start.6 = (bf16[64,2048]{1,0:T(8,128)(2,1)}, bf16[64,2048]{1,0:T(8,128)(2,1)S(1)}, u32[]{:S(2)}) copy-start(bf16[64,2048]{1,0:T(8,128)(2,1)S(1)} %collective-permute-done.6.refs_2_) | copy-start | bytes 786436
  53.0 35.1 %collective-permute-start.8 = (bf16[64,2048]{1,0:T(8,128)(2,1)S(1)}, bf16[64,2048]{1,0:T(8,128)(2,1)}, u32[]{:S(2)}, u32[]{:S(2)}) collective-permute-start(bf16[64,2048]{1,0:T(8,128)(2,1)S(1)} %collective-permute-done.6.refs_2_), channel_id=1, source_target_pairs={{0,32},{1,225},{32,64},{33,1},{64,96},{65,33},{96,128},{97,65},{12... | collective-permute-start | bytes 786440 | tf_op jit(solution)/shard_map/ppermute | solution.py:147
  56.6 39.9 %copy-start.8 = (bf16[64,2048]{1,0:T(8,128)(2,1)}, bf16[64,2048]{1,0:T(8,128)(2,1)S(1)}, u32[]{:S(2)}) copy-start(bf16[64,2048]{1,0:T(8,128)(2,1)S(1)} %collective-permute-done.7.refs_3_) | copy-start | bytes 786436
  56.6 36.3 %collective-permute-start.9 = (bf16[64,2048]{1,0:T(8,128)(2,1)S(1)}, bf16[64,2048]{1,0:T(8,128)(2,1)}, u32[]{:S(2)}, u32[]{:S(2)}) collective-permute-start(bf16[64,2048]{1,0:T(8,128)(2,1)S(1)} %collective-permute-done.7.refs_3_), channel_id=1, source_target_pairs={{0,32},{1,225},{32,64},{33,1},{64,96},{65,33},{96,128},{97,65},{12... | collective-permute-start | bytes 786440 | tf_op jit(solution)/shard_map/ppermute | solution.py:147
  59.6 9.3 %collective-permute-start.2 = (bf16[104,256]{1,0:T(8,128)(2,1)}, bf16[104,256]{1,0:T(8,128)(2,1)S(1)}, u32[]{:S(2)}, u32[]{:S(2)}) collective-permute-start(bf16[104,256]{1,0:T(8,128)(2,1)} %bitcast.24), channel_id=1, source_target_pairs={{0,768},{256,0},{512,256},{768,512},{1,769},{257,1},{513,257},{769... | collective-permute-start | bytes 159752 | tf_op jit(solution)/shard_map/ppermute | solution.py:167
  62.4 34.1 %collective-permute-start.4 = (bf16[104,2048]{1,0:T(8,128)(2,1)}, bf16[104,2048]{1,0:T(8,128)(2,1)S(1)}, u32[]{:S(2)}, u32[]{:S(2)}) collective-permute-start(bf16[104,2048]{1,0:T(8,128)(2,1)} %mine.1), channel_id=1, source_target_pairs={{0,1},{1,0},{2,3},{3,2},{4,5},{5,4},{6,7},{7,6},{8,9},{9,8},{10,11... | collective-permute-start | bytes 1277960 | tf_op jit(solution)/shard_map/ppermute | solution.py:170
  66.0 7.7 %collective-permute-start.1 = (bf16[104,256]{1,0:T(8,128)(2,1)}, bf16[104,256]{1,0:T(8,128)(2,1)S(1)}, u32[]{:S(2)}, u32[]{:S(2)}) collective-permute-start(bf16[104,256]{1,0:T(8,128)(2,1)} %bitcast.25), channel_id=1, source_target_pairs={{0,512},{256,768},{512,0},{768,256},{1,513},{257,769},{513,1},{769... | collective-permute-start | bytes 159752 | tf_op jit(solution)/shard_map/ppermute | solution.py:167
  68.9 11.2 %collective-permute-start = (bf16[104,256]{1,0:T(8,128)(2,1)}, bf16[104,256]{1,0:T(8,128)(2,1)S(1)}, u32[]{:S(2)}, u32[]{:S(2)}) collective-permute-start(bf16[104,256]{1,0:T(8,128)(2,1)} %bitcast.26), channel_id=1, source_target_pairs={{0,256},{256,512},{512,768},{768,0},{1,257},{257,513},{513,769},{7... | collective-permute-start | bytes 159752 | tf_op jit(solution)/shard_map/ppermute | solution.py:167
  73.6 10.2 %collective-permute-start.5 = (bf16[16,2048]{1,0:T(8,128)(2,1)S(1)}, bf16[16,2048]{1,0:T(8,128)(2,1)S(1)}, u32[]{:S(2)}, u32[]{:S(2)}) collective-permute-start(bf16[16,2048]{1,0:T(8,128)(2,1)S(1)} %bitcast.20), channel_id=1, source_target_pairs={{0,128},{32,160},{64,192},{96,224},{128,0},{160,32},{192,64},{224,... | collective-permute-start | bytes 196616 | tf_op jit(solution)/shard_map/ppermute | solution.py:160
  80.9 15.6 %collective-permute-start.3 = (bf16[4,104,256]{2,1,0:T(8,128)(2,1)S(1)}, bf16[4,104,256]{2,1,0:T(8,128)(2,1)S(1)}, u32[]{:S(2)}, u32[]{:S(2)}) collective-permute-start(bf16[4,104,256]{2,1,0:T(8,128)(2,1)S(1)} %pad_maximum_fusion.held), channel_id=1, source_target_pairs={{0,1},{1,0},{2,3},{3,2},{4,5},{5,4},{6,7},{7,6},{8,9},{9,8},{10,11... | collective-permute-start | bytes 638984 | tf_op jit(solution)/shard_map/ppermute | solution.py:169
  84.6 14.1 %all-to-all-start.2 = ((bf16[4,16,2048]{2,1,0:T(8,128)(2,1)}), bf16[4,16,2048]{2,1,0:T(8,128)(2,1)S(1)}, u32[]{:S(2)}, u32[]{:S(2)}) async-start(bf16[4,16,2048]{2,1,0:T(8,128)(2,1)} %broadcast_in_dim.24), calls=%async_computation.2 | async-start | bytes 524288 | tf_op jit(solution)/shard_map/all_to_all | solution.py:162
  88.0 18.9 %collective-permute-start.10 = (bf16[64,2048]{1,0:T(8,128)(2,1)}, bf16[64,2048]{1,0:T(8,128)(2,1)}, u32[]{:S(2)}, u32[]{:S(2)}) collective-permute-start(bf16[64,2048]{1,0:T(8,128)(2,1)} %collective-permute-done.8.refs_2_), channel_id=1, source_target_pairs={{0,32},{1,225},{32,64},{33,1},{64,96},{65,33},{96,128},{97,65},{12... | collective-permute-start | bytes 786440 | tf_op jit(solution)/shard_map/ppermute | solution.py:147
  92.9 14.1 %collective-permute-start.11 = (bf16[64,2048]{1,0:T(8,128)(2,1)}, bf16[64,2048]{1,0:T(8,128)(2,1)}, u32[]{:S(2)}, u32[]{:S(2)}) collective-permute-start(bf16[64,2048]{1,0:T(8,128)(2,1)} %collective-permute-done.9.refs_3_), channel_id=1, source_target_pairs={{0,32},{1,225},{32,64},{33,1},{64,96},{65,33},{96,128},{97,65},{12... | collective-permute-start | bytes 786440 | tf_op jit(solution)/shard_map/ppermute | solution.py:147
  98.0 0.6 copy-start.10
  98.7 0.7 copy-start.2
  99.4 0.9 copy-start.1
  100.4 0.9 copy-start.3
  101.3 0.9 copy-start.7
  102.3 0.9 copy-start.9
  108.6 0.7 copy-start.4
  109.3 12.5 %all-to-all-start.3 = ((bf16[8,104,128]{2,1,0:T(8,128)(2,1)}), bf16[8,104,128]{2,1,0:T(8,128)(2,1)S(1)}, u32[]{:S(2)}, u32[]{:S(2)}) async-start(bf16[8,104,128]{2,1,0:T(8,128)(2,1)} %copy-done.4), calls=%async_computation.3 | async-start | bytes 425984 | tf_op jit(solution)/shard_map/all_to_all | solution.py:200
  114.9 6.8 %copy-start.11 = (bf16[256,256]{1,0:T(8,128)(2,1)S(1)}, bf16[256,256]{1,0:T(8,128)(2,1)}, u32[]{:S(2)}) copy-start(bf16[256,256]{1,0:T(8,128)(2,1)} %copy-done.10) | copy-start | bytes 393220
  116.4 3.7 %collective-permute-start.12 = (bf16[104,2048]{1,0:T(8,128)(2,1)S(1)}, bf16[104,2048]{1,0:T(8,128)(2,1)S(1)}, u32[]{:S(2)}, u32[]{:S(2)}) collective-permute-start(bf16[104,2048]{1,0:T(8,128)(2,1)S(1)} %get-tuple-element.21), channel_id=1, source_target_pairs={{0,1},{1,0},{2,3},{3,2},{4,5},{5,4},{6,7},{7,6},{8,9},{9,8},{10,11... | collective-permute-start | bytes 1277960 | tf_op jit(solution)/shard_map/ppermute | solution.py:205

commit v3 on v2

--- a/solution.py
+++ b/solution.py
@@ -32,7 +32,7 @@
     return lax.dot_general(a, b, (((ca,), (cb,)), ((), ())), preferred_element_type=F32)
 
 
-def call(body, outs, *args, flops=0, aliases=None):
+def call(body, outs, *args, flops=0):
     outs = [jax.ShapeDtypeStruct(s, d) for s, d in outs]
     moved = sum(a.size * a.dtype.itemsize for a in args) + sum(o.size * o.dtype.itemsize for o in outs)
     specs = [SMEM if a.dtype == jnp.int32 else VMEM for a in args]
@@ -41,7 +41,6 @@
         out_shape=outs,
         in_specs=specs,
         out_specs=[VMEM] * len(outs),
-        input_output_aliases=aliases or {},
         cost_estimate=pl.CostEstimate(flops=flops, bytes_accessed=moved, transcendentals=0),
         compiler_params=pltpu.CompilerParams(vmem_limit_bytes=12 * 2**20),
     )(*args)
@@ -86,23 +85,17 @@
     weight[pl.ds(pad + ff, pad - ff)] = blank
 
 
-def early_body(first, units, weight, grouped, *refs):
-    grad, parts = refs[-2:]
-    before, chunks = (refs[:2], refs[2:-2]) if first > 0 else (None, refs[:-2])
-    n = len(chunks) * ROWS
-    start = first * ROWS
+def early_body(units, weight, grouped, *refs):
+    chunks, (grad, parts) = refs[:EARLY], refs[EARLY:]
+    n = EARLY * ROWS
     width = weight.shape[1]
     inner = jnp.concatenate([c[...] for c in chunks], axis=0)
     ig = dot(weight[...], inner, 1, 1).astype(BF16)
-    moved = dot(ig, grouped[pl.ds(start, n)], 1, 0)
-    if before:
-        moved = moved + before[1][...].astype(F32)
-    parts[...] = moved.astype(BF16)
-    left = units[:, start:start + n]
+    parts[...] = dot(ig, grouped[pl.ds(0, n)], 1, 0).astype(BF16)
+    left = units[:, :n]
     for j in range(0, width, 512):
         cols = jnp.concatenate([c[:, j:j + 512] for c in chunks], axis=0)
-        total = dot(left, cols, 1, 0)
-        grad[:, j:j + 512] = before[0][:, j:j + 512] + total if before else total
+        grad[:, j:j + 512] = dot(left, cols, 1, 0)
 
 
 def parts_body(ff, pad, at, weight, grouped, early, *refs):
@@ -154,6 +147,7 @@
 
     row = jnp.broadcast_to(out_grad.reshape(DP, 1, 2, width // 2), (DP, ZH, 2, width // 2))
     row = row.reshape(DP * ZH, 2, width // 2)
+    row, at = lax.optimization_barrier((row, at))
     mine = lax.all_to_all(row, ("dp", "zh"), 0, 0, tiled=True).reshape(DP * ZH, width)
     spread = jnp.broadcast_to(mine[None], (X, DP * ZH, width))
     u0 = lax.all_to_all(spread, "x", 0, 0, tiled=True).reshape(ROWS, width)
@@ -187,11 +181,7 @@
     flops = 4 * pad * width * ROWS * CORE
     shapes = [((2 * pad, width), F32), ((2 * pad, CHUNKS * ROWS), BF16)]
     grad, parts = call(
-        functools.partial(early_body, 0), shapes, units, weight, grouped, u0, u4, u1, v1, flops=4 * flops
-    )
-    grad, parts = call(
-        functools.partial(early_body, 4), shapes, units, weight, grouped, grad, parts, u2, v2,
-        flops=2 * flops, aliases={3: 0, 4: 1},
+        early_body, shapes, units, weight, grouped, u0, u4, u1, v1, u2, v2, flops=EARLY * flops
     )
     (parts,) = call(
         functools.partial(parts_body, ff, pad), [((DP * CORE, ff, HALF), BF16)],

time: 124 us -> 126 us (1.016)
  local copies, waits for them, and re-layouts: 7.38 us -> 8.97 us
    unnamed x25 -> x31, local copies, waits for them, and re-layouts: 6.56 us -> 8.18 us
    pallas_call x7 -> x6, Pallas kernels: 9.9 us -> 8.77 us  [call(): pl.pallas_call(body, out_shape=outs, in_specs=specs, out_specs=[VMEM] * l...]
  transfers between devices with their start and end apart: 15 -> 15, of which waited for: 4 -> 4; matrix products, arithmetic and copies ran while one was open for 1% -> 1% of each run, Pallas kernels for 6% -> 5%
where the time goes in v3:
time: 126 us; the launch traced here: 124 us
  starting transfers between devices  57.2 us (45%)
  blocking collectives  40.2 us (32%)
  local copies, waits for them, and re-layouts  8.97 us (7%)
  Pallas kernels  8.77 us (7%)
  waiting for transfers between devices  5.82 us (5%)
  other arithmetic  1.82 us (1%)
    all_to_all x1, blocking collectives, step(): lax.all_to_all(row, ('dp', 'zh'), 0, 0, tiled=True).reshape(DP * ZH, width)  30.9 us
    ppermute x6, starting transfers between devices, ring(): return lax.ppermute(value, ('y', 'core'), ring_pairs(cross))  25 us
    all_to_all x1, blocking collectives, step(): u0 = lax.all_to_all(spread, 'x', 0, 0, tiled=True).reshape(ROWS, width)  9.34 us
    pallas_call x6, Pallas kernels, call(): pl.pallas_call(body, out_shape=outs, in_specs=specs, out_specs=[VMEM] * l...  8.77 us
    ppermute x3, starting transfers between devices, step(): lax.ppermute(here, 'dp', [(g, (g + k) % DP) for g in range(DP)])  8.18 us
    unnamed x31, local copies, waits for them, and re-layouts  8.18 us
    ppermute x1, starting transfers between devices, step(): away = lax.ppermute(mine, 'y', [(y, (y + Y // 2) % Y) for y in range(Y)])  6.43 us
    all_to_all x1, starting transfers between devices, step(): back = lax.all_to_all(parts, ('dp', 'core'), 0, 0, tiled=True)  5.66 us
  transfers between devices with their start and end apart: 15, of which 4 were waited for; matrix products, arithmetic and copies ran while one was open for 1% of the time, Pallas kernels for 5%

profile of v3, /device:TPU:1, one launch (start us, length us, event | category | flops | bytes accessed | tf_op | source)
XLA Modules:
  0.0 123.7 jit_solution(9411559751912212923)
XLA Ops:
  0.6 0.0 copy-start.6
  0.6 0.9 reduce
  1.6 0.1 pad_add_fusion.at
  1.7 30.9 %all_to_all.20 = bf16[16,2,1024]{2,1,0:T(2,128)(2,1)S(1)} all-to-all(bf16[16,2,1024]{2,1,0:T(2,128)(2,1)S(1)} %bitcast.21), channel_id=1, replica_groups=mesh['dp'=4,'y'=8,'x'=4,'zh'=4,'core'=2] {'dp','zh'}, dimensions={0} | all-to-all | bytes 131072 | tf_op jit(solution)/shard_map/all_to_all | solution.py:151
  32.6 9.3 %all_to_all.21 = bf16[4,16,2048]{2,1,0:T(8,128)(2,1)S(1)} all-to-all(bf16[4,16,2048]{2,1,0:T(8,128)(2,1)S(1)} %broadcast_in_dim.23), channel_id=1, replica_groups=mesh['dp'=4,'y'=8,'x'=4,'zh'=4,'core'=2] {'x'}, dimensions={0} | all-to-all | bytes 524288 | tf_op jit(solution)/shard_map/all_to_all | solution.py:153
  41.9 5.1 %collective-permute-start.6 = (bf16[64,2048]{1,0:T(8,128)(2,1)S(1)}, bf16[64,2048]{1,0:T(8,128)(2,1)S(1)}, u32[]{:S(2)}, u32[]{:S(2)}) collective-permute-start(bf16[64,2048]{1,0:T(8,128)(2,1)S(1)} %bitcast.15), channel_id=1, source_target_pairs={{0,32},{1,225},{32,64},{33,1},{64,96},{65,33},{96,128},{97,65},{12... | collective-permute-start | bytes 786440 | tf_op jit(solution)/shard_map/ppermute | solution.py:140
  47.0 5.3 %collective-permute-start.7 = (bf16[64,2048]{1,0:T(8,128)(2,1)S(1)}, bf16[64,2048]{1,0:T(8,128)(2,1)S(1)}, u32[]{:S(2)}, u32[]{:S(2)}) collective-permute-start(bf16[64,2048]{1,0:T(8,128)(2,1)S(1)} %bitcast.16), channel_id=1, source_target_pairs={{1,32},{0,225},{33,64},{32,1},{65,96},{64,33},{97,128},{96,65},{12... | collective-permute-start | bytes 786440 | tf_op jit(solution)/shard_map/ppermute | solution.py:140
  52.3 0.0 collective-permute-done.6.refs_2_
  52.4 3.3 %collective-permute-start.8 = (bf16[64,2048]{1,0:T(8,128)(2,1)S(1)}, bf16[64,2048]{1,0:T(8,128)(2,1)}, u32[]{:S(2)}, u32[]{:S(2)}) collective-permute-start(bf16[64,2048]{1,0:T(8,128)(2,1)S(1)} %collective-permute-done.6.refs_2_), channel_id=1, source_target_pairs={{0,32},{1,225},{32,64},{33,1},{64,96},{65,33},{96,128},{97,65},{12... | collective-permute-start | bytes 786440 | tf_op jit(solution)/shard_map/ppermute | solution.py:140
  55.6 1.0 collective-permute-done.7.refs_3_
  56.7 3.0 %collective-permute-start.9 = (bf16[64,2048]{1,0:T(8,128)(2,1)S(1)}, bf16[64,2048]{1,0:T(8,128)(2,1)}, u32[]{:S(2)}, u32[]{:S(2)}) collective-permute-start(bf16[64,2048]{1,0:T(8,128)(2,1)S(1)} %collective-permute-done.7.refs_3_), channel_id=1, source_target_pairs={{0,32},{1,225},{32,64},{33,1},{64,96},{65,33},{96,128},{97,65},{12... | collective-permute-start | bytes 786440 | tf_op jit(solution)/shard_map/ppermute | solution.py:140
  59.7 2.8 %collective-permute-start.2 = (bf16[104,256]{1,0:T(8,128)(2,1)}, bf16[104,256]{1,0:T(8,128)(2,1)S(1)}, u32[]{:S(2)}, u32[]{:S(2)}) collective-permute-start(bf16[104,256]{1,0:T(8,128)(2,1)} %bitcast.24), channel_id=1, source_target_pairs={{0,768},{256,0},{512,256},{768,512},{1,769},{257,1},{513,257},{769... | collective-permute-start | bytes 159752 | tf_op jit(solution)/shard_map/ppermute | solution.py:161
  62.5 3.5 %collective-permute-start.4 = (bf16[104,2048]{1,0:T(8,128)(2,1)}, bf16[104,2048]{1,0:T(8,128)(2,1)S(1)}, u32[]{:S(2)}, u32[]{:S(2)}) collective-permute-start(bf16[104,2048]{1,0:T(8,128)(2,1)} %mine.1), channel_id=1, source_target_pairs={{0,1},{1,0},{2,3},{3,2},{4,5},{5,4},{6,7},{7,6},{8,9},{9,8},{10,11... | collective-permute-start | bytes 1277960 | tf_op jit(solution)/shard_map/ppermute | solution.py:164
  66.1 2.9 %collective-permute-start.1 = (bf16[104,256]{1,0:T(8,128)(2,1)}, bf16[104,256]{1,0:T(8,128)(2,1)S(1)}, u32[]{:S(2)}, u32[]{:S(2)}) collective-permute-start(bf16[104,256]{1,0:T(8,128)(2,1)} %bitcast.25), channel_id=1, source_target_pairs={{0,512},{256,768},{512,0},{768,256},{1,513},{257,769},{513,1},{769... | collective-permute-start | bytes 159752 | tf_op jit(solution)/shard_map/ppermute | solution.py:161
  68.9 0.0 collective-permute-done.2
  69.0 2.5 %collective-permute-start = (bf16[104,256]{1,0:T(8,128)(2,1)}, bf16[104,256]{1,0:T(8,128)(2,1)S(1)}, u32[]{:S(2)}, u32[]{:S(2)}) collective-permute-start(bf16[104,256]{1,0:T(8,128)(2,1)} %bitcast.26), channel_id=1, source_target_pairs={{0,256},{256,512},{512,768},{768,0},{1,257},{257,513},{513,769},{7... | collective-permute-start | bytes 159752 | tf_op jit(solution)/shard_map/ppermute | solution.py:161
  71.4 2.3 %collective-permute-done.1 = bf16[104,256]{1,0:T(8,128)(2,1)S(1)} collective-permute-done((bf16[104,256]{1,0:T(8,128)(2,1)}, bf16[104,256]{1,0:T(8,128)(2,1)S(1)}, u32[]{:S(2)}, u32[]{:S(2)}) %collective-permute-start.1) | collective-permute-done | bytes 53280 | tf_op jit(solution)/shard_map/ppermute | solution.py:161
  73.7 6.4 %collective-permute-start.5 = (bf16[16,2048]{1,0:T(8,128)(2,1)S(1)}, bf16[16,2048]{1,0:T(8,128)(2,1)S(1)}, u32[]{:S(2)}, u32[]{:S(2)}) collective-permute-start(bf16[16,2048]{1,0:T(8,128)(2,1)S(1)} %bitcast.20), channel_id=1, source_target_pairs={{0,128},{32,160},{64,192},{96,224},{128,0},{160,32},{192,64},{224,... | collective-permute-start | bytes 196616 | tf_op jit(solution)/shard_map/ppermute | solution.py:154
  80.1 0.0 collective-permute-done
  80.2 0.8 pad_maximum_fusion.held
  81.0 2.9 %collective-permute-start.3 = (bf16[4,104,256]{2,1,0:T(8,128)(2,1)S(1)}, bf16[4,104,256]{2,1,0:T(8,128)(2,1)S(1)}, u32[]{:S(2)}, u32[]{:S(2)}) collective-permute-start(bf16[4,104,256]{2,1,0:T(8,128)(2,1)S(1)} %pad_maximum_fusion.held), channel_id=1, source_target_pairs={{0,1},{1,0},{2,3},{3,2},{4,5},{5,4},{6,7},{7,6},{8,9},{9,8},{10,11... | collective-permute-start | bytes 638984 | tf_op jit(solution)/shard_map/ppermute | solution.py:163
  83.9 0.0 collective-permute-done.5
  83.9 0.7 broadcast_in_dim.24
  84.7 3.4 %all-to-all-start.2 = ((bf16[4,16,2048]{2,1,0:T(8,128)(2,1)}), bf16[4,16,2048]{2,1,0:T(8,128)(2,1)S(1)}, u32[]{:S(2)}, u32[]{:S(2)}) async-start(bf16[4,16,2048]{2,1,0:T(8,128)(2,1)} %broadcast_in_dim.24), calls=%async_computation.2 | async-start | bytes 524288 | tf_op jit(solution)/shard_map/all_to_all | solution.py:156
  88.1 4.8 %collective-permute-start.10 = (bf16[64,2048]{1,0:T(8,128)(2,1)}, bf16[64,2048]{1,0:T(8,128)(2,1)}, u32[]{:S(2)}, u32[]{:S(2)}) collective-permute-start(bf16[64,2048]{1,0:T(8,128)(2,1)} %collective-permute-done.8.refs_4_), channel_id=1, source_target_pairs={{0,32},{1,225},{32,64},{33,1},{64,96},{65,33},{96,128},{97,65},{12... | collective-permute-start | bytes 786440 | tf_op jit(solution)/shard_map/ppermute | solution.py:140
  92.9 3.6 %collective-permute-start.11 = (bf16[64,2048]{1,0:T(8,128)(2,1)}, bf16[64,2048]{1,0:T(8,128)(2,1)}, u32[]{:S(2)}, u32[]{:S(2)}) collective-permute-start(bf16[64,2048]{1,0:T(8,128)(2,1)} %collective-permute-done.9.refs_5_), channel_id=1, source_target_pairs={{0,32},{1,225},{32,64},{33,1},{64,96},{65,33},{96,128},{97,65},{12... | collective-permute-start | bytes 786440 | tf_op jit(solution)/shard_map/ppermute | solution.py:140
  96.5 0.0 collective-permute-done.3.partner
  96.5 0.7 copy-done.11
  97.2 0.0 collective-permute-done.4.other
  97.2 0.9 copy-done.12
  98.2 1.5 %shard_map.50 = (bf16[224,512]{1,0:T(8,128)(2,1)S(1)}, bf16[224,2048]{1,0:T(8,128)(2,1)S(1)}, bf16[512,512]{1,0:T(8,128)(2,1)S(1)}, bf16[256,256]{1,0:T(8,128)(2,1)S(1)}) custom-call(s32[3]{0:T(128)S(1)} %pad_add_fusion.at, bf16[4,104,256]{2,1,0:T(8,128)(2,1)S(1)} %pad_maximum_fusion.held, bf16[4,104,256]{2,1,0:T(8,128)(2,1)S(1)} %copy-done.12, ...), custom_call_target="tpu_custom_call" | custom-call | bytes 3080204 | tf_op jit(solution)/shard_map/pallas_call | solution.py:39
  99.7 0.7 copy-done.2
  100.4 0.6 copy-done.13
  101.0 0.7 copy-done
  101.7 0.9 copy-done.1
  102.7 0.9 copy-done.3
  103.6 0.9 copy-done.8
  104.6 0.9 copy-done.10
  105.5 2.5 %shard_map.51 = (f32[224,2048]{1,0:T(8,128)S(1)}, bf16[224,512]{1,0:T(8,128)(2,1)S(1)}) custom-call(bf16[224,512]{1,0:T(8,128)(2,1)S(1)} %copy-done.3, bf16[224,2048]{1,0:T(8,128)(2,1)S(1)} %get-tuple-element.14.weight, bf16[512,512]{1,0:T(8,128)(2,1)S(1)} %get-tuple-element.15.grouped, bf16[64,2048]{1,0:T(8,128)(2,1)S(1)} %bitcast.17, ...), custom_call_target="tpu_custom_call" | custom-call | flops 704643072 | bytes 5308416 | tf_op jit(solution)/shard_map/pallas_call | solution.py:39
  108.0 1.7 %shard_map.52 = bf16[8,104,128]{2,1,0:T(8,128)(2,1)S(1)} custom-call(s32[3]{0:T(128)S(1)} %pad_add_fusion.at, bf16[224,2048]{1,0:T(8,128)(2,1)S(1)} %get-tuple-element.14.weight, bf16[512,512]{1,0:T(8,128)(2,1)S(1)} %get-tuple-element.15.grouped, bf16[224,512]{1,0:T(8,128)(2,1)S(1)} %get-tuple-element.18.early, ...), custom_call_target="tpu_custom_call" | custom-call | flops 234881024 | bytes 2408460 | tf_op jit(solution)/shard_map/pallas_call | solution.py:39
  109.8 0.7 copy-done.5
  110.5 5.7 %all-to-all-start.3 = ((bf16[8,104,128]{2,1,0:T(8,128)(2,1)}), bf16[8,104,128]{2,1,0:T(8,128)(2,1)S(1)}, u32[]{:S(2)}, u32[]{:S(2)}) async-start(bf16[8,104,128]{2,1,0:T(8,128)(2,1)} %copy-done.5), calls=%async_computation.3 | async-start | bytes 425984 | tf_op jit(solution)/shard_map/all_to_all | solution.py:190
  116.1 1.4 %shard_map.54 = (f32[104,2048]{1,0:T(8,128)S(1)}, bf16[104,2048]{1,0:T(8,128)(2,1)S(1)}) custom-call(bf16[224,512]{1,0:T(8,128)(2,1)S(1)} %copy-done.4, f32[224,2048]{1,0:T(8,128)S(1)} %get-tuple-element.19.grad, bf16[64,2048]{1,0:T(8,128)(2,1)} %collective-permute-done.10.refs_0_, bf16[64,2048]{1,0:T(8,128)(2,1)} %collective-permute-done.11.refs_1_), custom_call_target="tpu_custom_call" | custom-call | flops 234881024 | bytes 3866624 | tf_op jit(solution)/shard_map/pallas_call | solution.py:39
  117.6 2.0 %collective-permute-start.12 = (bf16[104,2048]{1,0:T(8,128)(2,1)S(1)}, bf16[104,2048]{1,0:T(8,128)(2,1)S(1)}, u32[]{:S(2)}, u32[]{:S(2)}) collective-permute-start(bf16[104,2048]{1,0:T(8,128)(2,1)S(1)} %get-tuple-element.21), channel_id=1, source_target_pairs={{0,1},{1,0},{2,3},{3,2},{4,5},{5,4},{6,7},{7,6},{8,9},{9,8},{10,11... | collective-permute-start | bytes 1277960 | tf_op jit(solution)/shard_map/ppermute | solution.py:195
  119.6 1.6 %collective-permute-done.12.taken = bf16[104,2048]{1,0:T(8,128)(2,1)S(1)} collective-permute-done((bf16[104,2048]{1,0:T(8,128)(2,1)S(1)}, bf16[104,2048]{1,0:T(8,128)(2,1)S(1)}, u32[]{:S(2)}, u32[]{:S(2)}) %collective-permute-start.12) | collective-permute-done | bytes 426016 | tf_op jit(solution)/shard_map/ppermute | solution.py:195
  121.2 0.8 shard_map.55
  122.1 0.8 all-to-all-done.3.back
  122.9 0.8 shard_map.53
  (28 shorter events, 0.1 us)
Async XLA Ops:
  0.6 96.6 %copy-start.6 = (bf16[104,2048]{1,0:T(8,128)(2,1)S(1)}, bf16[104,2048]{1,0:T(8,128)(2,1)}, u32[]{:S(2)}) copy-start(bf16[104,2048]{1,0:T(8,128)(2,1)} %mine.1) | copy-start | bytes 1277956
  41.9 10.4 %collective-permute-start.6 = (bf16[64,2048]{1,0:T(8,128)(2,1)S(1)}, bf16[64,2048]{1,0:T(8,128)(2,1)S(1)}, u32[]{:S(2)}, u32[]{:S(2)}) collective-permute-start(bf16[64,2048]{1,0:T(8,128)(2,1)S(1)} %bitcast.15), channel_id=1, source_target_pairs={{0,32},{1,225},{32,64},{33,1},{64,96},{65,33},{96,128},{97,65},{12... | collective-permute-start | bytes 786440 | tf_op jit(solution)/shard_map/ppermute | solution.py:140
  47.0 9.6 %collective-permute-start.7 = (bf16[64,2048]{1,0:T(8,128)(2,1)S(1)}, bf16[64,2048]{1,0:T(8,128)(2,1)S(1)}, u32[]{:S(2)}, u32[]{:S(2)}) collective-permute-start(bf16[64,2048]{1,0:T(8,128)(2,1)S(1)} %bitcast.16), channel_id=1, source_target_pairs={{1,32},{0,225},{33,64},{32,1},{65,96},{64,33},{97,128},{96,65},{12... | collective-permute-start | bytes 786440 | tf_op jit(solution)/shard_map/ppermute | solution.py:140
  52.3 49.4 %copy-start.7 = (bf16[64,2048]{1,0:T(8,128)(2,1)}, bf16[64,2048]{1,0:T(8,128)(2,1)S(1)}, u32[]{:S(2)}) copy-start(bf16[64,2048]{1,0:T(8,128)(2,1)S(1)} %collective-permute-done.6.refs_2_) | copy-start | bytes 786436
  52.4 35.7 %collective-permute-start.8 = (bf16[64,2048]{1,0:T(8,128)(2,1)S(1)}, bf16[64,2048]{1,0:T(8,128)(2,1)}, u32[]{:S(2)}, u32[]{:S(2)}) collective-permute-start(bf16[64,2048]{1,0:T(8,128)(2,1)S(1)} %collective-permute-done.6.refs_2_), channel_id=1, source_target_pairs={{0,32},{1,225},{32,64},{33,1},{64,96},{65,33},{96,128},{97,65},{12... | collective-permute-start | bytes 786440 | tf_op jit(solution)/shard_map/ppermute | solution.py:140
  56.7 39.8 %copy-start.9 = (bf16[64,2048]{1,0:T(8,128)(2,1)}, bf16[64,2048]{1,0:T(8,128)(2,1)S(1)}, u32[]{:S(2)}) copy-start(bf16[64,2048]{1,0:T(8,128)(2,1)S(1)} %collective-permute-done.7.refs_3_) | copy-start | bytes 786436
  56.7 36.2 %collective-permute-start.9 = (bf16[64,2048]{1,0:T(8,128)(2,1)S(1)}, bf16[64,2048]{1,0:T(8,128)(2,1)}, u32[]{:S(2)}, u32[]{:S(2)}) collective-permute-start(bf16[64,2048]{1,0:T(8,128)(2,1)S(1)} %collective-permute-done.7.refs_3_), channel_id=1, source_target_pairs={{0,32},{1,225},{32,64},{33,1},{64,96},{65,33},{96,128},{97,65},{12... | collective-permute-start | bytes 786440 | tf_op jit(solution)/shard_map/ppermute | solution.py:140
  59.7 9.3 %collective-permute-start.2 = (bf16[104,256]{1,0:T(8,128)(2,1)}, bf16[104,256]{1,0:T(8,128)(2,1)S(1)}, u32[]{:S(2)}, u32[]{:S(2)}) collective-permute-start(bf16[104,256]{1,0:T(8,128)(2,1)} %bitcast.24), channel_id=1, source_target_pairs={{0,768},{256,0},{512,256},{768,512},{1,769},{257,1},{513,257},{769... | collective-permute-start | bytes 159752 | tf_op jit(solution)/shard_map/ppermute | solution.py:161
  62.5 34.7 %collective-permute-start.4 = (bf16[104,2048]{1,0:T(8,128)(2,1)}, bf16[104,2048]{1,0:T(8,128)(2,1)S(1)}, u32[]{:S(2)}, u32[]{:S(2)}) collective-permute-start(bf16[104,2048]{1,0:T(8,128)(2,1)} %mine.1), channel_id=1, source_target_pairs={{0,1},{1,0},{2,3},{3,2},{4,5},{5,4},{6,7},{7,6},{8,9},{9,8},{10,11... | collective-permute-start | bytes 1277960 | tf_op jit(solution)/shard_map/ppermute | solution.py:164
  66.1 7.7 %collective-permute-start.1 = (bf16[104,256]{1,0:T(8,128)(2,1)}, bf16[104,256]{1,0:T(8,128)(2,1)S(1)}, u32[]{:S(2)}, u32[]{:S(2)}) collective-permute-start(bf16[104,256]{1,0:T(8,128)(2,1)} %bitcast.25), channel_id=1, source_target_pairs={{0,512},{256,768},{512,0},{768,256},{1,513},{257,769},{513,1},{769... | collective-permute-start | bytes 159752 | tf_op jit(solution)/shard_map/ppermute | solution.py:161
  69.0 11.2 %collective-permute-start = (bf16[104,256]{1,0:T(8,128)(2,1)}, bf16[104,256]{1,0:T(8,128)(2,1)S(1)}, u32[]{:S(2)}, u32[]{:S(2)}) collective-permute-start(bf16[104,256]{1,0:T(8,128)(2,1)} %bitcast.26), channel_id=1, source_target_pairs={{0,256},{256,512},{512,768},{768,0},{1,257},{257,513},{513,769},{7... | collective-permute-start | bytes 159752 | tf_op jit(solution)/shard_map/ppermute | solution.py:161
  73.7 10.2 %collective-permute-start.5 = (bf16[16,2048]{1,0:T(8,128)(2,1)S(1)}, bf16[16,2048]{1,0:T(8,128)(2,1)S(1)}, u32[]{:S(2)}, u32[]{:S(2)}) collective-permute-start(bf16[16,2048]{1,0:T(8,128)(2,1)S(1)} %bitcast.20), channel_id=1, source_target_pairs={{0,128},{32,160},{64,192},{96,224},{128,0},{160,32},{192,64},{224,... | collective-permute-start | bytes 196616 | tf_op jit(solution)/shard_map/ppermute | solution.py:154
  81.0 15.5 %collective-permute-start.3 = (bf16[4,104,256]{2,1,0:T(8,128)(2,1)S(1)}, bf16[4,104,256]{2,1,0:T(8,128)(2,1)S(1)}, u32[]{:S(2)}, u32[]{:S(2)}) collective-permute-start(bf16[4,104,256]{2,1,0:T(8,128)(2,1)S(1)} %pad_maximum_fusion.held), channel_id=1, source_target_pairs={{0,1},{1,0},{2,3},{3,2},{4,5},{5,4},{6,7},{7,6},{8,9},{9,8},{10,11... | collective-permute-start | bytes 638984 | tf_op jit(solution)/shard_map/ppermute | solution.py:163
  84.7 16.4 %all-to-all-start.2 = ((bf16[4,16,2048]{2,1,0:T(8,128)(2,1)}), bf16[4,16,2048]{2,1,0:T(8,128)(2,1)S(1)}, u32[]{:S(2)}, u32[]{:S(2)}) async-start(bf16[4,16,2048]{2,1,0:T(8,128)(2,1)} %broadcast_in_dim.24), calls=%async_computation.2 | async-start | bytes 524288 | tf_op jit(solution)/shard_map/all_to_all | solution.py:156
  88.1 19.9 %collective-permute-start.10 = (bf16[64,2048]{1,0:T(8,128)(2,1)}, bf16[64,2048]{1,0:T(8,128)(2,1)}, u32[]{:S(2)}, u32[]{:S(2)}) collective-permute-start(bf16[64,2048]{1,0:T(8,128)(2,1)} %collective-permute-done.8.refs_4_), channel_id=1, source_target_pairs={{0,32},{1,225},{32,64},{33,1},{64,96},{65,33},{96,128},{97,65},{12... | collective-permute-start | bytes 786440 | tf_op jit(solution)/shard_map/ppermute | solution.py:140
  92.9 15.1 %collective-permute-start.11 = (bf16[64,2048]{1,0:T(8,128)(2,1)}, bf16[64,2048]{1,0:T(8,128)(2,1)}, u32[]{:S(2)}, u32[]{:S(2)}) collective-permute-start(bf16[64,2048]{1,0:T(8,128)(2,1)} %collective-permute-done.9.refs_5_), channel_id=1, source_target_pairs={{0,32},{1,225},{32,64},{33,1},{64,96},{65,33},{96,128},{97,65},{12... | collective-permute-start | bytes 786440 | tf_op jit(solution)/shard_map/ppermute | solution.py:140
  96.5 0.7 copy-start.11
  97.2 0.9 copy-start.12
  99.7 0.7 copy-start.2
  100.4 0.6 copy-start.13
  101.0 0.7 copy-start
  101.7 1.0 copy-start.1
  102.7 0.9 copy-start.3
  103.6 0.9 copy-start.8
  104.6 0.9 copy-start.10
  108.0 8.1 %copy-start.4 = (bf16[224,512]{1,0:T(8,128)(2,1)S(1)}, bf16[224,512]{1,0:T(8,128)(2,1)}, u32[]{:S(2)}) copy-start(bf16[224,512]{1,0:T(8,128)(2,1)} %copy-done.2) | copy-start | bytes 688132
  109.8 0.7 copy-start.5
  110.5 12.5 %all-to-all-start.3 = ((bf16[8,104,128]{2,1,0:T(8,128)(2,1)}), bf16[8,104,128]{2,1,0:T(8,128)(2,1)S(1)}, u32[]{:S(2)}, u32[]{:S(2)}) async-start(bf16[8,104,128]{2,1,0:T(8,128)(2,1)} %copy-done.5), calls=%async_computation.3 | async-start | bytes 425984 | tf_op jit(solution)/shard_map/all_to_all | solution.py:190
  116.1 6.8 %copy-start.14 = (bf16[256,256]{1,0:T(8,128)(2,1)S(1)}, bf16[256,256]{1,0:T(8,128)(2,1)}, u32[]{:S(2)}) copy-start(bf16[256,256]{1,0:T(8,128)(2,1)} %copy-done.13) | copy-start | bytes 393220
  117.6 3.7 %collective-permute-start.12 = (bf16[104,2048]{1,0:T(8,128)(2,1)S(1)}, bf16[104,2048]{1,0:T(8,128)(2,1)S(1)}, u32[]{:S(2)}, u32[]{:S(2)}) collective-permute-start(bf16[104,2048]{1,0:T(8,128)(2,1)S(1)} %get-tuple-element.21), channel_id=1, source_target_pairs={{0,1},{1,0},{2,3},{3,2},{4,5},{5,4},{6,7},{7,6},{8,9},{9,8},{10,11... | collective-permute-start | bytes 1277960 | tf_op jit(solution)/shard_map/ppermute | solution.py:195

commit v4 on v3

--- a/solution.py
+++ b/solution.py
@@ -58,31 +58,26 @@
     return lax.broadcasted_iota(jnp.int32, shape, dim)
 
 
-def units_body(ff, pad, at, held, partner, mine, other, units, weight, grouped, hot_last):
+def units_body(ff, pad, at, held, partner, units, weight, grouped, hot_last):
     me, y, g = at[0], at[1], at[2]
     total = CHUNKS * ROWS
+    width = weight.shape[1]
     a = iota((total, total), 0)
     place = ((a >> 2) & 3) * HALF + (a >> 6) * 16 + ((a >> 4) & 3) * 4 + (a & 3)
     grouped[...] = (place == iota((total, total), 1)).astype(BF16)
+    hot_last[...] = (token_at(iota((TOK, TOK), 0), y) == iota((TOK, TOK), 1)).astype(BF16)
     p = iota((1, total), 1)
-    slot = me * HALF + (p >> 6) * 16 + ((p >> 4) & 3) * 4 + (p & 3)
-    group = (p >> 2) & 3
-    token = token_at(slot, y)
-    hot_last[...] = (token_at(iota((TOK, TOK), 0), y) == iota((TOK, TOK), 1)).astype(BF16)
+    token = token_at(me * HALF + (p >> 6) * 16 + ((p >> 4) & 3) * 4 + (p & 3), y)
+    wanted = ((g - ((p >> 2) & 3)) & 3) * TOK + token
+    hot = (iota((DP * TOK, total), 0) == wanted).astype(BF16)
     gap = jnp.zeros((pad - ff, total), F32)
-    for j in range(CORE):
-        moved = None
-        for k in range(DP):
-            wanted = jnp.where(group == ((g - k) & 3), token, -1)
-            hot = (iota((TOK, total), 0) == wanted).astype(BF16)
-            term = dot((held, partner)[j][k], hot, 1, 0)
-            moved = term if moved is None else moved + term
+    blank = jnp.zeros((pad - ff, width), BF16)
+    for j, source in enumerate((held, partner)):
+        moved = dot(source[:, width:], hot, 1, 0)
         units[pl.ds(j * pad, pad)] = jnp.concatenate([moved, gap], axis=0).astype(BF16)
-    blank = jnp.zeros((pad - ff, mine.shape[1]), BF16)
-    weight[pl.ds(0, ff)] = mine[...]
-    weight[pl.ds(ff, pad - ff)] = blank
-    weight[pl.ds(pad, ff)] = other[...]
-    weight[pl.ds(pad + ff, pad - ff)] = blank
+        row = pl.multiple_of((me ^ j) * pad, 16)
+        weight[pl.ds(row, ff)] = source[:, :width]
+        weight[pl.ds(row + ff, pad - ff)] = blank
 
 
 def early_body(units, weight, grouped, *refs):
@@ -98,16 +93,15 @@
         grad[:, j:j + 512] = dot(left, cols, 1, 0)
 
 
-def parts_body(ff, pad, at, weight, grouped, early, *refs):
+def parts_body(ff, pad, weight, grouped, early, *refs):
     chunks, (out,) = refs[:-1], refs[-1:]
-    me = at[0]
     n = EARLY * ROWS
     inner = jnp.concatenate([c[...] for c in chunks], axis=0)
     ig = dot(weight[...], inner, 1, 1).astype(BF16)
     parts = (dot(ig, grouped[pl.ds(n, CHUNKS * ROWS - n)], 1, 0) + early[...].astype(F32)).astype(BF16)
     for g in range(DP):
         for j in range(CORE):
-            out[g * CORE + (me ^ j)] = parts[j * pad:j * pad + ff, g * HALF:(g + 1) * HALF]
+            out[g * CORE + j] = parts[j * pad:j * pad + ff, g * HALF:(g + 1) * HALF]
 
 
 def late_body(ff, pad, units, grad, *refs):
@@ -159,16 +153,15 @@
     there = []
     for k in range(1, DP):
         there.append(lax.ppermute(here, "dp", [(g, (g + k) % DP) for g in range(DP)]))
-    held = jnp.stack([here] + there)
+    held = jnp.concatenate([down_weight, here] + there, axis=1)
     partner = lax.ppermute(held, "core", SWAP)
-    other = lax.ppermute(down_weight, "core", SWAP)
     units, weight, grouped, hot = call(
         functools.partial(units_body, ff, pad),
         [
             ((2 * pad, CHUNKS * ROWS), BF16), ((2 * pad, width), BF16),
             ((CHUNKS * ROWS, CHUNKS * ROWS), BF16), ((TOK, TOK), BF16),
         ],
-        at, held, partner, down_weight, other,
+        at, held, partner,
     )
 
     u1 = ring(u0)
@@ -185,7 +178,7 @@
     )
     (parts,) = call(
         functools.partial(parts_body, ff, pad), [((DP * CORE, ff, HALF), BF16)],
-        at, weight, grouped, parts, u3, v3, flops=2 * flops,
+        weight, grouped, parts, u3, v3, flops=2 * flops,
     )
     back = lax.all_to_all(parts, ("dp", "core"), 0, 0, tiled=True)
     keep, give = call(

time: 126 us -> 124 us (0.984)
  blocking collectives: 40.2 us -> 0 us
  starting transfers between devices: 57.2 us -> 79.5 us
  waiting for transfers between devices: 5.82 us -> 19.8 us
  local copies, waits for them, and re-layouts: 8.97 us -> 12.4 us
    all_to_all x2 -> x0, blocking collectives: 40.2 us -> none  [the longest x1 30.9 us: step(): lax.all_to_all(row, ('dp', 'zh'), 0, 0, tiled=True).reshape(DP * ZH, width)]
    all_to_all x0 -> x2, starting transfers between devices: none -> 20.8 us  [the longest x1 16.8 us: step(): lax.all_to_all(row, ('dp', 'zh'), 0, 0, tiled=True).reshape(DP * ZH, width)]
    all_to_all x0 -> x2, waiting for transfers between devices: none -> 15.3 us  [the longest x1 9.81 us: step(): lax.all_to_all(row, ('dp', 'zh'), 0, 0, tiled=True).reshape(DP * ZH, width)]
    ppermute x3, starting transfers between devices: 8.18 us -> 12.8 us  [step(): lax.ppermute(here, 'dp', [(g, (g + k) % DP) for g in range(DP)])]
    ppermute x1 -> x0, starting transfers between devices: 3.54 us -> none  [step(): other = lax.ppermute(down_weight, 'core', SWAP)]
    all_to_all x1, starting transfers between devices: 5.66 us -> 8.57 us  [step(): back = lax.all_to_all(parts, ('dp', 'core'), 0, 0, tiled=True)]
    ppermute x1, waiting for transfers between devices: 0.01 us -> 2.79 us  [step(): away = lax.ppermute(mine, 'y', [(y, (y + Y // 2) % Y) for y in range(Y)])]
    ppermute x3, waiting for transfers between devices: 2.3 us -> 0.01 us  [step(): lax.ppermute(here, 'dp', [(g, (g + k) % DP) for g in range(DP)])]
  transfers between devices with their start and end apart: 15 -> 16, of which waited for: 4 -> 4; matrix products, arithmetic and copies ran while one was open for 1% -> 4% of each run, Pallas kernels for 5% -> 5%
where the time goes in v4:
time: 124 us; the launch traced here: 122 us
  starting transfers between devices  79.5 us (64%)
  waiting for transfers between devices  19.8 us (16%)
  local copies, waits for them, and re-layouts  12.4 us (10%)
  Pallas kernels  8.52 us (7%)
    ppermute x6, starting transfers between devices, ring(): return lax.ppermute(value, ('y', 'core'), ring_pairs(cross))  23.1 us
    all_to_all x1, starting transfers between devices, step(): lax.all_to_all(row, ('dp', 'zh'), 0, 0, tiled=True).reshape(DP * ZH, width)  16.8 us
    ppermute x3, starting transfers between devices, step(): lax.ppermute(here, 'dp', [(g, (g + k) % DP) for g in range(DP)])  12.8 us
    unnamed x33, local copies, waits for them, and re-layouts  10.3 us
    all_to_all x1, waiting for transfers between devices, step(): lax.all_to_all(row, ('dp', 'zh'), 0, 0, tiled=True).reshape(DP * ZH, width)  9.81 us
    all_to_all x1, starting transfers between devices, step(): back = lax.all_to_all(parts, ('dp', 'core'), 0, 0, tiled=True)  8.57 us
    pallas_call x6, Pallas kernels, call(): pl.pallas_call(body, out_shape=outs, in_specs=specs, out_specs=[VMEM] * l...  8.52 us
    ppermute x1, starting transfers between devices, step(): away = lax.ppermute(mine, 'y', [(y, (y + Y // 2) % Y) for y in range(Y)])  6.83 us
  transfers between devices with their start and end apart: 16, of which 4 were waited for; matrix products, arithmetic and copies ran while one was open for 4% of the time, Pallas kernels for 5%

profile of v4, /device:TPU:1, one launch (start us, length us, event | category | flops | bytes accessed | tf_op | source)
XLA Modules:
  0.0 122.0 jit_solution(14143451894706676141)
XLA Ops:
  0.6 4.8 %collective-permute-start = (bf16[104,256]{1,0:T(8,128)(2,1)}, bf16[104,256]{1,0:T(8,128)(2,1)S(1)}, u32[]{:S(2)}, u32[]{:S(2)}) collective-permute-start(bf16[104,256]{1,0:T(8,128)(2,1)} %bitcast.19), channel_id=1, source_target_pairs={{0,256},{256,512},{512,768},{768,0},{1,257},{257,513},{513,769},{7... | collective-permute-start | bytes 159752 | tf_op jit(solution)/shard_map/ppermute | solution.py:155
  5.5 5.8 %collective-permute-start.1 = (bf16[104,256]{1,0:T(8,128)(2,1)}, bf16[104,256]{1,0:T(8,128)(2,1)S(1)}, u32[]{:S(2)}, u32[]{:S(2)}) collective-permute-start(bf16[104,256]{1,0:T(8,128)(2,1)} %bitcast.20), channel_id=1, source_target_pairs={{0,512},{256,768},{512,0},{768,256},{1,513},{257,769},{513,1},{769... | collective-permute-start | bytes 159752 | tf_op jit(solution)/shard_map/ppermute | solution.py:155
  11.3 2.2 %collective-permute-start.2 = (bf16[104,256]{1,0:T(8,128)(2,1)}, bf16[104,256]{1,0:T(8,128)(2,1)S(1)}, u32[]{:S(2)}, u32[]{:S(2)}) collective-permute-start(bf16[104,256]{1,0:T(8,128)(2,1)} %bitcast.21), channel_id=1, source_target_pairs={{0,768},{256,0},{512,256},{768,512},{1,769},{257,1},{513,257},{769... | collective-permute-start | bytes 159752 | tf_op jit(solution)/shard_map/ppermute | solution.py:155
  13.5 0.8 reduce
  14.3 0.1 pad_add_fusion.at
  14.4 0.7 broadcast_in_dim.21
  15.1 16.8 %all-to-all-start = ((bf16[16,2,1024]{2,1,0:T(2,128)(2,1)}), bf16[16,2,1024]{2,1,0:T(2,128)(2,1)S(1)}, u32[]{:S(2)}, u32[]{:S(2)}) async-start(bf16[16,2,1024]{2,1,0:T(2,128)(2,1)} %bitcast), calls=%async_computation | async-start | bytes 131072 | tf_op jit(solution)/shard_map/all_to_all | solution.py:145
  31.9 1.0 constant_dynamic-update-slice_fusion.4
  32.9 0.8 constant_dynamic-update-slice_fusion.3
  33.7 9.8 %all-to-all-done = bf16[16,2,1024]{2,1,0:T(2,128)(2,1)S(1)} async-done(((bf16[16,2,1024]{2,1,0:T(2,128)(2,1)}), bf16[16,2,1024]{2,1,0:T(2,128)(2,1)S(1)}, u32[]{:S(2)}, u32[]{:S(2)}) %all-to-all-start) | async-done | bytes 65568 | tf_op jit(solution)/shard_map/all_to_all | solution.py:145
  43.5 0.7 broadcast_in_dim.23
  44.3 4.0 %all-to-all-start.1 = ((bf16[4,16,2048]{2,1,0:T(8,128)(2,1)}), bf16[4,16,2048]{2,1,0:T(8,128)(2,1)S(1)}, u32[]{:S(2)}, u32[]{:S(2)}) async-start(bf16[4,16,2048]{2,1,0:T(8,128)(2,1)} %broadcast_in_dim.23), calls=%async_computation.1 | async-start | bytes 524288 | tf_op jit(solution)/shard_map/all_to_all | solution.py:147
  48.3 0.0 collective-permute-done.1
  48.3 5.5 %all-to-all-done.1 = bf16[4,16,2048]{2,1,0:T(8,128)(2,1)S(1)} async-done(((bf16[4,16,2048]{2,1,0:T(8,128)(2,1)}), bf16[4,16,2048]{2,1,0:T(8,128)(2,1)S(1)}, u32[]{:S(2)}, u32[]{:S(2)}) %all-to-all-start.1) | async-done | bytes 262176 | tf_op jit(solution)/shard_map/all_to_all | solution.py:147
  53.8 5.1 %collective-permute-start.5 = (bf16[64,2048]{1,0:T(8,128)(2,1)S(1)}, bf16[64,2048]{1,0:T(8,128)(2,1)S(1)}, u32[]{:S(2)}, u32[]{:S(2)}) collective-permute-start(bf16[64,2048]{1,0:T(8,128)(2,1)S(1)} %bitcast.11), channel_id=1, source_target_pairs={{0,32},{1,225},{32,64},{33,1},{64,96},{65,33},{96,128},{97,65},{12... | collective-permute-start | bytes 786440 | tf_op jit(solution)/shard_map/ppermute | solution.py:134
  58.9 6.0 %collective-permute-start.6 = (bf16[64,2048]{1,0:T(8,128)(2,1)S(1)}, bf16[64,2048]{1,0:T(8,128)(2,1)S(1)}, u32[]{:S(2)}, u32[]{:S(2)}) collective-permute-start(bf16[64,2048]{1,0:T(8,128)(2,1)S(1)} %bitcast.12), channel_id=1, source_target_pairs={{1,32},{0,225},{33,64},{32,1},{65,96},{64,33},{97,128},{96,65},{12... | collective-permute-start | bytes 786440 | tf_op jit(solution)/shard_map/ppermute | solution.py:134
  65.0 1.9 %collective-permute-start.3 = (bf16[104,3072]{1,0:T(8,128)(2,1)S(1)}, bf16[104,3072]{1,0:T(8,128)(2,1)S(1)}, u32[]{:S(2)}, u32[]{:S(2)}) collective-permute-start(bf16[104,3072]{1,0:T(8,128)(2,1)S(1)} %constant_dynamic-update-slice_fusion.held), channel_id=1, source_target_pairs={{0,1},{1,0},{2,3},{3,2},{4,5},{5,4},{6,7},{7,6},{8,9},{9,8},{10,11... | collective-permute-start | bytes 1916936 | tf_op jit(solution)/shard_map/ppermute | solution.py:157
  66.9 3.3 %collective-permute-start.7 = (bf16[64,2048]{1,0:T(8,128)(2,1)S(1)}, bf16[64,2048]{1,0:T(8,128)(2,1)}, u32[]{:S(2)}, u32[]{:S(2)}) collective-permute-start(bf16[64,2048]{1,0:T(8,128)(2,1)S(1)} %collective-permute-done.5.refs_2_), channel_id=1, source_target_pairs={{0,32},{1,225},{32,64},{33,1},{64,96},{65,33},{96,128},{97,65},{12... | collective-permute-start | bytes 786440 | tf_op jit(solution)/shard_map/ppermute | solution.py:134
  70.2 0.0 collective-permute-done.6.refs_3_
  70.2 2.7 %collective-permute-start.8 = (bf16[64,2048]{1,0:T(8,128)(2,1)S(1)}, bf16[64,2048]{1,0:T(8,128)(2,1)}, u32[]{:S(2)}, u32[]{:S(2)}) collective-permute-start(bf16[64,2048]{1,0:T(8,128)(2,1)S(1)} %collective-permute-done.6.refs_3_), channel_id=1, source_target_pairs={{0,32},{1,225},{32,64},{33,1},{64,96},{65,33},{96,128},{97,65},{12... | collective-permute-start | bytes 786440 | tf_op jit(solution)/shard_map/ppermute | solution.py:134
  73.0 6.8 %collective-permute-start.4 = (bf16[16,2048]{1,0:T(8,128)(2,1)S(1)}, bf16[16,2048]{1,0:T(8,128)(2,1)S(1)}, u32[]{:S(2)}, u32[]{:S(2)}) collective-permute-start(bf16[16,2048]{1,0:T(8,128)(2,1)S(1)} %bitcast.16), channel_id=1, source_target_pairs={{0,128},{32,160},{64,192},{96,224},{128,0},{160,32},{192,64},{224,... | collective-permute-start | bytes 196616 | tf_op jit(solution)/shard_map/ppermute | solution.py:148
  79.8 2.8 %collective-permute-done.4 = bf16[16,2048]{1,0:T(8,128)(2,1)S(1)} collective-permute-done((bf16[16,2048]{1,0:T(8,128)(2,1)S(1)}, bf16[16,2048]{1,0:T(8,128)(2,1)S(1)}, u32[]{:S(2)}, u32[]{:S(2)}) %collective-permute-start.4) | collective-permute-done | bytes 65568 | tf_op jit(solution)/shard_map/ppermute | solution.py:148
  82.6 0.7 broadcast_in_dim.24
  83.3 3.4 %all-to-all-start.2 = ((bf16[4,16,2048]{2,1,0:T(8,128)(2,1)}), bf16[4,16,2048]{2,1,0:T(8,128)(2,1)S(1)}, u32[]{:S(2)}, u32[]{:S(2)}) async-start(bf16[4,16,2048]{2,1,0:T(8,128)(2,1)} %broadcast_in_dim.24), calls=%async_computation.2 | async-start | bytes 524288 | tf_op jit(solution)/shard_map/all_to_all | solution.py:150
  86.7 2.6 %collective-permute-start.9 = (bf16[64,2048]{1,0:T(8,128)(2,1)}, bf16[64,2048]{1,0:T(8,128)(2,1)S(1)}, u32[]{:S(2)}, u32[]{:S(2)}) collective-permute-start(bf16[64,2048]{1,0:T(8,128)(2,1)} %collective-permute-done.7.refs_4_), channel_id=1, source_target_pairs={{0,32},{1,225},{32,64},{33,1},{64,96},{65,33},{96,128},{97,65},{12... | collective-permute-start | bytes 786440 | tf_op jit(solution)/shard_map/ppermute | solution.py:134
  89.3 0.0 collective-permute-done.8.refs_5_
  89.3 3.5 %collective-permute-start.10 = (bf16[64,2048]{1,0:T(8,128)(2,1)}, bf16[64,2048]{1,0:T(8,128)(2,1)}, u32[]{:S(2)}, u32[]{:S(2)}) collective-permute-start(bf16[64,2048]{1,0:T(8,128)(2,1)} %collective-permute-done.8.refs_5_), channel_id=1, source_target_pairs={{0,32},{1,225},{32,64},{33,1},{64,96},{65,33},{96,128},{97,65},{12... | collective-permute-start | bytes 786440 | tf_op jit(solution)/shard_map/ppermute | solution.py:134
  92.8 1.5 %shard_map.50 = (bf16[224,512]{1,0:T(8,128)(2,1)S(1)}, bf16[224,2048]{1,0:T(8,128)(2,1)S(1)}, bf16[512,512]{1,0:T(8,128)(2,1)S(1)}, bf16[256,256]{1,0:T(8,128)(2,1)S(1)}) custom-call(s32[3]{0:T(128)S(1)} %pad_add_fusion.at, bf16[104,3072]{1,0:T(8,128)(2,1)S(1)} %constant_dynamic-update-slice_fusion.held, bf16[104,3072]{1,0:T(8,128)(2,1)S(1)} %collective-permute-done.3.partner), custom_call_target="tpu_custom_call" | custom-call | bytes 3080204 | tf_op jit(solution)/shard_map/pallas_call | solution.py:39
  94.3 0.7 copy-done.4
  95.0 0.6 copy-done.12
  95.7 0.7 copy-done.2
  96.4 0.9 copy-done.1
  97.3 0.9 copy-done.3
  98.3 0.9 copy-done.5
  99.2 0.9 copy-done.9
  100.1 0.9 copy-done.11
  101.1 2.5 %shard_map.51 = (f32[224,2048]{1,0:T(8,128)S(1)}, bf16[224,512]{1,0:T(8,128)(2,1)S(1)}) custom-call(bf16[224,512]{1,0:T(8,128)(2,1)S(1)} %copy-done.5, bf16[224,2048]{1,0:T(8,128)(2,1)S(1)} %get-tuple-element.14.weight, bf16[512,512]{1,0:T(8,128)(2,1)S(1)} %get-tuple-element.15.grouped, bf16[64,2048]{1,0:T(8,128)(2,1)S(1)} %bitcast.13, ...), custom_call_target="tpu_custom_call" | custom-call | flops 704643072 | bytes 5308416 | tf_op jit(solution)/shard_map/pallas_call | solution.py:39
  103.6 0.0 collective-permute-done.9.refs_0_
  103.6 1.6 %shard_map.52 = bf16[8,104,128]{2,1,0:T(8,128)(2,1)S(1)} custom-call(bf16[224,2048]{1,0:T(8,128)(2,1)S(1)} %get-tuple-element.14.weight, bf16[512,512]{1,0:T(8,128)(2,1)S(1)} %get-tuple-element.15.grouped, bf16[224,512]{1,0:T(8,128)(2,1)S(1)} %get-tuple-element.18.early, bf16[64,2048]{1,0:T(8,128)(2,1)S(1)} %collective-permute-done.9.refs_0_, ...), custom_call_target="tpu_custom_call" | custom-call | flops 234881024 | bytes 2408448 | tf_op jit(solution)/shard_map/pallas_call | solution.py:39
  105.2 0.7 copy-done.7
  105.9 8.6 %all-to-all-start.3 = ((bf16[8,104,128]{2,1,0:T(8,128)(2,1)}), bf16[8,104,128]{2,1,0:T(8,128)(2,1)S(1)}, u32[]{:S(2)}, u32[]{:S(2)}) async-start(bf16[8,104,128]{2,1,0:T(8,128)(2,1)} %copy-done.7), calls=%async_computation.3 | async-start | bytes 425984 | tf_op jit(solution)/shard_map/all_to_all | solution.py:183
  114.4 0.9 copy-done.6
  115.4 1.4 %shard_map.54 = (f32[104,2048]{1,0:T(8,128)S(1)}, bf16[104,2048]{1,0:T(8,128)(2,1)S(1)}) custom-call(bf16[224,512]{1,0:T(8,128)(2,1)S(1)} %copy-done.6, f32[224,2048]{1,0:T(8,128)S(1)} %get-tuple-element.19.grad, bf16[64,2048]{1,0:T(8,128)(2,1)S(1)} %collective-permute-done.9.refs_0_, bf16[64,2048]{1,0:T(8,128)(2,1)} %collective-permute-done.10.refs_1_), custom_call_target="tpu_custom_call" | custom-call | flops 234881024 | bytes 3866624 | tf_op jit(solution)/shard_map/pallas_call | solution.py:39
  116.8 2.0 %collective-permute-start.11 = (bf16[104,2048]{1,0:T(8,128)(2,1)S(1)}, bf16[104,2048]{1,0:T(8,128)(2,1)S(1)}, u32[]{:S(2)}, u32[]{:S(2)}) collective-permute-start(bf16[104,2048]{1,0:T(8,128)(2,1)S(1)} %get-tuple-element.21), channel_id=1, source_target_pairs={{0,1},{1,0},{2,3},{3,2},{4,5},{5,4},{6,7},{7,6},{8,9},{9,8},{10,11... | collective-permute-start | bytes 1277960 | tf_op jit(solution)/shard_map/ppermute | solution.py:188
  118.8 1.6 %collective-permute-done.11.taken = bf16[104,2048]{1,0:T(8,128)(2,1)S(1)} collective-permute-done((bf16[104,2048]{1,0:T(8,128)(2,1)S(1)}, bf16[104,2048]{1,0:T(8,128)(2,1)S(1)}, u32[]{:S(2)}, u32[]{:S(2)}) %collective-permute-start.11) | collective-permute-done | bytes 426016 | tf_op jit(solution)/shard_map/ppermute | solution.py:188
  120.4 0.8 shard_map.55
  121.2 0.0 all-to-all-done.3.back
  121.2 0.8 shard_map.53
  (30 shorter events, 0.1 us)
Async XLA Ops:
  0.6 47.6 %collective-permute-start = (bf16[104,256]{1,0:T(8,128)(2,1)}, bf16[104,256]{1,0:T(8,128)(2,1)S(1)}, u32[]{:S(2)}, u32[]{:S(2)}) collective-permute-start(bf16[104,256]{1,0:T(8,128)(2,1)} %bitcast.19), channel_id=1, source_target_pairs={{0,256},{256,512},{512,768},{768,0},{1,257},{257,513},{513,769},{7... | collective-permute-start | bytes 159752 | tf_op jit(solution)/shard_map/ppermute | solution.py:155
  5.5 42.8 %collective-permute-start.1 = (bf16[104,256]{1,0:T(8,128)(2,1)}, bf16[104,256]{1,0:T(8,128)(2,1)S(1)}, u32[]{:S(2)}, u32[]{:S(2)}) collective-permute-start(bf16[104,256]{1,0:T(8,128)(2,1)} %bitcast.20), channel_id=1, source_target_pairs={{0,512},{256,768},{512,0},{768,256},{1,513},{257,769},{513,1},{769... | collective-permute-start | bytes 159752 | tf_op jit(solution)/shard_map/ppermute | solution.py:155
  11.3 53.7 %collective-permute-start.2 = (bf16[104,256]{1,0:T(8,128)(2,1)}, bf16[104,256]{1,0:T(8,128)(2,1)S(1)}, u32[]{:S(2)}, u32[]{:S(2)}) collective-permute-start(bf16[104,256]{1,0:T(8,128)(2,1)} %bitcast.21), channel_id=1, source_target_pairs={{0,768},{256,0},{512,256},{768,512},{1,769},{257,1},{513,257},{769... | collective-permute-start | bytes 159752 | tf_op jit(solution)/shard_map/ppermute | solution.py:155
  15.1 28.4 %all-to-all-start = ((bf16[16,2,1024]{2,1,0:T(2,128)(2,1)}), bf16[16,2,1024]{2,1,0:T(2,128)(2,1)S(1)}, u32[]{:S(2)}, u32[]{:S(2)}) async-start(bf16[16,2,1024]{2,1,0:T(2,128)(2,1)} %bitcast), calls=%async_computation | async-start | bytes 131072 | tf_op jit(solution)/shard_map/all_to_all | solution.py:145
  44.3 9.5 %all-to-all-start.1 = ((bf16[4,16,2048]{2,1,0:T(8,128)(2,1)}), bf16[4,16,2048]{2,1,0:T(8,128)(2,1)S(1)}, u32[]{:S(2)}, u32[]{:S(2)}) async-start(bf16[4,16,2048]{2,1,0:T(8,128)(2,1)} %broadcast_in_dim.23), calls=%async_computation.1 | async-start | bytes 524288 | tf_op jit(solution)/shard_map/all_to_all | solution.py:147
  53.8 39.0 %copy-start = (bf16[4,16,2048]{2,1,0:T(8,128)(2,1)}, bf16[4,16,2048]{2,1,0:T(8,128)(2,1)S(1)}, u32[]{:S(2)}) copy-start(bf16[4,16,2048]{2,1,0:T(8,128)(2,1)S(1)} %all-to-all-done.1) | copy-start | bytes 786436
  53.8 13.1 %collective-permute-start.5 = (bf16[64,2048]{1,0:T(8,128)(2,1)S(1)}, bf16[64,2048]{1,0:T(8,128)(2,1)S(1)}, u32[]{:S(2)}, u32[]{:S(2)}) collective-permute-start(bf16[64,2048]{1,0:T(8,128)(2,1)S(1)} %bitcast.11), channel_id=1, source_target_pairs={{0,32},{1,225},{32,64},{33,1},{64,96},{65,33},{96,128},{97,65},{12... | collective-permute-start | bytes 786440 | tf_op jit(solution)/shard_map/ppermute | solution.py:134
  58.9 11.3 %collective-permute-start.6 = (bf16[64,2048]{1,0:T(8,128)(2,1)S(1)}, bf16[64,2048]{1,0:T(8,128)(2,1)S(1)}, u32[]{:S(2)}, u32[]{:S(2)}) collective-permute-start(bf16[64,2048]{1,0:T(8,128)(2,1)S(1)} %bitcast.12), channel_id=1, source_target_pairs={{1,32},{0,225},{33,64},{32,1},{65,96},{64,33},{97,128},{96,65},{12... | collective-permute-start | bytes 786440 | tf_op jit(solution)/shard_map/ppermute | solution.py:134
  65.0 27.8 %collective-permute-start.3 = (bf16[104,3072]{1,0:T(8,128)(2,1)S(1)}, bf16[104,3072]{1,0:T(8,128)(2,1)S(1)}, u32[]{:S(2)}, u32[]{:S(2)}) collective-permute-start(bf16[104,3072]{1,0:T(8,128)(2,1)S(1)} %constant_dynamic-update-slice_fusion.held), channel_id=1, source_target_pairs={{0,1},{1,0},{2,3},{3,2},{4,5},{5,4},{6,7},{7,6},{8,9},{9,8},{10,11... | collective-permute-start | bytes 1916936 | tf_op jit(solution)/shard_map/ppermute | solution.py:157
  66.9 25.9 %copy-start.8 = (bf16[64,2048]{1,0:T(8,128)(2,1)}, bf16[64,2048]{1,0:T(8,128)(2,1)S(1)}, u32[]{:S(2)}) copy-start(bf16[64,2048]{1,0:T(8,128)(2,1)S(1)} %collective-permute-done.5.refs_2_) | copy-start | bytes 786436
  66.9 19.8 %collective-permute-start.7 = (bf16[64,2048]{1,0:T(8,128)(2,1)S(1)}, bf16[64,2048]{1,0:T(8,128)(2,1)}, u32[]{:S(2)}, u32[]{:S(2)}) collective-permute-start(bf16[64,2048]{1,0:T(8,128)(2,1)S(1)} %collective-permute-done.5.refs_2_), channel_id=1, source_target_pairs={{0,32},{1,225},{32,64},{33,1},{64,96},{65,33},{96,128},{97,65},{12... | collective-permute-start | bytes 786440 | tf_op jit(solution)/shard_map/ppermute | solution.py:134
  70.2 26.1 %copy-start.10 = (bf16[64,2048]{1,0:T(8,128)(2,1)}, bf16[64,2048]{1,0:T(8,128)(2,1)S(1)}, u32[]{:S(2)}) copy-start(bf16[64,2048]{1,0:T(8,128)(2,1)S(1)} %collective-permute-done.6.refs_3_) | copy-start | bytes 786436
  70.2 19.0 %collective-permute-start.8 = (bf16[64,2048]{1,0:T(8,128)(2,1)S(1)}, bf16[64,2048]{1,0:T(8,128)(2,1)}, u32[]{:S(2)}, u32[]{:S(2)}) collective-permute-start(bf16[64,2048]{1,0:T(8,128)(2,1)S(1)} %collective-permute-done.6.refs_3_), channel_id=1, source_target_pairs={{0,32},{1,225},{32,64},{33,1},{64,96},{65,33},{96,128},{97,65},{12... | collective-permute-start | bytes 786440 | tf_op jit(solution)/shard_map/ppermute | solution.py:134
  73.0 9.6 %collective-permute-start.4 = (bf16[16,2048]{1,0:T(8,128)(2,1)S(1)}, bf16[16,2048]{1,0:T(8,128)(2,1)S(1)}, u32[]{:S(2)}, u32[]{:S(2)}) collective-permute-start(bf16[16,2048]{1,0:T(8,128)(2,1)S(1)} %bitcast.16), channel_id=1, source_target_pairs={{0,128},{32,160},{64,192},{96,224},{128,0},{160,32},{192,64},{224,... | collective-permute-start | bytes 196616 | tf_op jit(solution)/shard_map/ppermute | solution.py:148
  83.3 12.4 %all-to-all-start.2 = ((bf16[4,16,2048]{2,1,0:T(8,128)(2,1)}), bf16[4,16,2048]{2,1,0:T(8,128)(2,1)S(1)}, u32[]{:S(2)}, u32[]{:S(2)}) async-start(bf16[4,16,2048]{2,1,0:T(8,128)(2,1)} %broadcast_in_dim.24), calls=%async_computation.2 | async-start | bytes 524288 | tf_op jit(solution)/shard_map/all_to_all | solution.py:150
  86.7 16.9 %collective-permute-start.9 = (bf16[64,2048]{1,0:T(8,128)(2,1)}, bf16[64,2048]{1,0:T(8,128)(2,1)S(1)}, u32[]{:S(2)}, u32[]{:S(2)}) collective-permute-start(bf16[64,2048]{1,0:T(8,128)(2,1)} %collective-permute-done.7.refs_4_), channel_id=1, source_target_pairs={{0,32},{1,225},{32,64},{33,1},{64,96},{65,33},{96,128},{97,65},{12... | collective-permute-start | bytes 786440 | tf_op jit(solution)/shard_map/ppermute | solution.py:134
  89.3 14.3 %collective-permute-start.10 = (bf16[64,2048]{1,0:T(8,128)(2,1)}, bf16[64,2048]{1,0:T(8,128)(2,1)}, u32[]{:S(2)}, u32[]{:S(2)}) collective-permute-start(bf16[64,2048]{1,0:T(8,128)(2,1)} %collective-permute-done.8.refs_5_), channel_id=1, source_target_pairs={{0,32},{1,225},{32,64},{33,1},{64,96},{65,33},{96,128},{97,65},{12... | collective-permute-start | bytes 786440 | tf_op jit(solution)/shard_map/ppermute | solution.py:134
  94.3 0.7 copy-start.4
  95.0 0.7 copy-start.12
  95.7 0.7 copy-start.2
  96.4 1.0 copy-start.1
  97.3 0.9 copy-start.3
  98.3 0.9 copy-start.5
  99.2 0.9 copy-start.9
  100.1 0.9 copy-start.11
  105.2 0.7 copy-start.7
  105.9 15.4 %all-to-all-start.3 = ((bf16[8,104,128]{2,1,0:T(8,128)(2,1)}), bf16[8,104,128]{2,1,0:T(8,128)(2,1)S(1)}, u32[]{:S(2)}, u32[]{:S(2)}) async-start(bf16[8,104,128]{2,1,0:T(8,128)(2,1)} %copy-done.7), calls=%async_computation.3 | async-start | bytes 425984 | tf_op jit(solution)/shard_map/all_to_all | solution.py:183
  114.4 0.9 copy-start.6
  115.4 5.9 %copy-start.13 = (bf16[256,256]{1,0:T(8,128)(2,1)S(1)}, bf16[256,256]{1,0:T(8,128)(2,1)}, u32[]{:S(2)}) copy-start(bf16[256,256]{1,0:T(8,128)(2,1)} %copy-done.12) | copy-start | bytes 393220
  116.8 3.7 %collective-permute-start.11 = (bf16[104,2048]{1,0:T(8,128)(2,1)S(1)}, bf16[104,2048]{1,0:T(8,128)(2,1)S(1)}, u32[]{:S(2)}, u32[]{:S(2)}) collective-permute-start(bf16[104,2048]{1,0:T(8,128)(2,1)S(1)} %get-tuple-element.21), channel_id=1, source_target_pairs={{0,1},{1,0},{2,3},{3,2},{4,5},{5,4},{6,7},{7,6},{8,9},{9,8},{10,11... | collective-permute-start | bytes 1277960 | tf_op jit(solution)/shard_map/ppermute | solution.py:188

commit v5 on v4

--- a/solution.py
+++ b/solution.py
@@ -80,17 +80,11 @@
         weight[pl.ds(row + ff, pad - ff)] = blank
 
 
-def early_body(units, weight, grouped, *refs):
-    chunks, (grad, parts) = refs[:EARLY], refs[EARLY:]
-    n = EARLY * ROWS
-    width = weight.shape[1]
+def early_body(weight, grouped, *refs):
+    chunks, (parts,) = refs[:-1], refs[-1:]
     inner = jnp.concatenate([c[...] for c in chunks], axis=0)
     ig = dot(weight[...], inner, 1, 1).astype(BF16)
-    parts[...] = dot(ig, grouped[pl.ds(0, n)], 1, 0).astype(BF16)
-    left = units[:, :n]
-    for j in range(0, width, 512):
-        cols = jnp.concatenate([c[:, j:j + 512] for c in chunks], axis=0)
-        grad[:, j:j + 512] = dot(left, cols, 1, 0)
+    parts[...] = dot(ig, grouped[pl.ds(0, EARLY * ROWS)], 1, 0).astype(BF16)
 
 
 def parts_body(ff, pad, weight, grouped, early, *refs):
@@ -104,14 +98,12 @@
             out[g * CORE + j] = parts[j * pad:j * pad + ff, g * HALF:(g + 1) * HALF]
 
 
-def late_body(ff, pad, units, grad, *refs):
+def grad_body(ff, pad, units, *refs):
     chunks, (keep, give) = refs[:-2], refs[-2:]
-    n = EARLY * ROWS
-    width = grad.shape[1]
-    left = units[:, n:]
-    for k in range(0, width, 512):
+    left = units[...]
+    for k in range(0, give.shape[1], 512):
         cols = jnp.concatenate([c[:, k:k + 512] for c in chunks], axis=0)
-        total = grad[:, k:k + 512] + dot(left, cols, 1, 0)
+        total = dot(left, cols, 1, 0)
         keep[:, k:k + 512] = total[:ff]
         give[:, k:k + 512] = total[pad:pad + ff].astype(BF16)
 
@@ -153,7 +145,8 @@
     there = []
     for k in range(1, DP):
         there.append(lax.ppermute(here, "dp", [(g, (g + k) % DP) for g in range(DP)]))
-    held = jnp.concatenate([down_weight, here] + there, axis=1)
+    *pieces, _ = lax.optimization_barrier((down_weight, here, *there, u0))
+    held = jnp.concatenate(pieces, axis=1)
     partner = lax.ppermute(held, "core", SWAP)
     units, weight, grouped, hot = call(
         functools.partial(units_body, ff, pad),
@@ -171,10 +164,9 @@
     u3 = ring(u2)
     v3 = ring(v2)
 
-    flops = 4 * pad * width * ROWS * CORE
-    shapes = [((2 * pad, width), F32), ((2 * pad, CHUNKS * ROWS), BF16)]
-    grad, parts = call(
-        early_body, shapes, units, weight, grouped, u0, u4, u1, v1, u2, v2, flops=EARLY * flops
+    flops = 2 * pad * width * ROWS * CORE
+    (parts,) = call(
+        early_body, [((2 * pad, CHUNKS * ROWS), BF16)], weight, grouped, u0, u4, u1, v1, u2, v2, flops=EARLY * flops
     )
     (parts,) = call(
         functools.partial(parts_body, ff, pad), [((DP * CORE, ff, HALF), BF16)],
@@ -182,8 +174,8 @@
     )
     back = lax.all_to_all(parts, ("dp", "core"), 0, 0, tiled=True)
     keep, give = call(
-        functools.partial(late_body, ff, pad), [((ff, width), F32), ((ff, width), BF16)],
-        units, grad, u3, v3, flops=2 * flops,
+        functools.partial(grad_body, ff, pad), [((ff, width), F32), ((ff, width), BF16)],
+        units, u0, u4, u1, v1, u2, v2, u3, v3, flops=CHUNKS * flops,
     )
     taken = lax.ppermute(give, "core", SWAP)
     (weight_grad,) = call(add_body, [((ff, width), BF16)], keep, taken)

time: 124 us -> 108 us (0.87)
  the two profiles are of different devices: /device:TPU:1 before, /device:TPU:16 now
where the time goes in v5:
time: 108 us; the launch traced here: 107 us
  starting transfers between devices  52.1 us (48%)
  blocking collectives  31.8 us (29%)
  Pallas kernels  9.1 us (8%)
  waiting for transfers between devices  7.69 us (7%)
  local copies, waits for them, and re-layouts  4.2 us (4%)
    all_to_all x1, blocking collectives, step(): lax.all_to_all(row, ('dp', 'zh'), 0, 0, tiled=True).reshape(DP * ZH, width)  31.8 us
    ppermute x6, starting transfers between devices, ring(): return lax.ppermute(value, ('y', 'core'), ring_pairs(cross))  20.4 us
    ppermute x3, starting transfers between devices, step(): lax.ppermute(here, 'dp', [(g, (g + k) % DP) for g in range(DP)])  9.9 us
    pallas_call x6, Pallas kernels, call(): pl.pallas_call(body, out_shape=outs, in_specs=specs, out_specs=[VMEM] * l...  9.1 us
    ppermute x1, starting transfers between devices, step(): partner = lax.ppermute(held, 'core', SWAP)  4.8 us
    all_to_all x1, starting transfers between devices, step(): u4 = lax.all_to_all(away, 'x', 0, 0, tiled=True).reshape(ROWS, width)  4.8 us
    all_to_all x1, starting transfers between devices, step(): u0 = lax.all_to_all(spread, 'x', 0, 0, tiled=True).reshape(ROWS, width)  4.42 us
    all_to_all x1, starting transfers between devices, step(): back = lax.all_to_all(parts, ('dp', 'core'), 0, 0, tiled=True)  3.53 us
  transfers between devices with their start and end apart: 15, of which 4 were waited for; matrix products, arithmetic and copies ran while one was open for 1% of the time, Pallas kernels for 6%

profile of v5, /device:TPU:16, one launch (start us, length us, event | category | flops | bytes accessed | tf_op | source)
XLA Modules:
  0.0 106.7 jit_solution(6933005111592873459)
XLA Ops:
  0.6 0.8 reduce
  1.5 0.1 pad_add_fusion.at
  1.6 31.8 %all_to_all.20 = bf16[16,2,1024]{2,1,0:T(2,128)(2,1)S(1)} all-to-all(bf16[16,2,1024]{2,1,0:T(2,128)(2,1)S(1)} %bitcast.18), channel_id=1, replica_groups=mesh['dp'=4,'y'=8,'x'=4,'zh'=4,'core'=2] {'dp','zh'}, dimensions={0} | all-to-all | bytes 131072 | tf_op jit(solution)/shard_map/all_to_all | solution.py:137
  33.4 0.0 copy-start.4
  33.4 0.7 broadcast_in_dim.23
  34.1 4.4 %all-to-all-start.1 = ((bf16[4,16,2048]{2,1,0:T(8,128)(2,1)}), bf16[4,16,2048]{2,1,0:T(8,128)(2,1)S(1)}, u32[]{:S(2)}, u32[]{:S(2)}) async-start(bf16[4,16,2048]{2,1,0:T(8,128)(2,1)} %broadcast_in_dim.23), calls=%async_computation.1 | async-start | bytes 524288 | tf_op jit(solution)/shard_map/all_to_all | solution.py:139
  38.6 0.0 copy-done.5
  38.6 2.9 %collective-permute-start = (bf16[104,256]{1,0:T(8,128)(2,1)S(1)}, bf16[104,256]{1,0:T(8,128)(2,1)S(1)}, u32[]{:S(2)}, u32[]{:S(2)}) collective-permute-start(bf16[104,256]{1,0:T(8,128)(2,1)S(1)} %bitcast.21), channel_id=1, source_target_pairs={{0,256},{256,512},{512,768},{768,0},{1,257},{257,513},{513,769},{7... | collective-permute-start | bytes 159752 | tf_op jit(solution)/shard_map/ppermute | solution.py:147
  41.5 2.7 %collective-permute-start.1 = (bf16[104,256]{1,0:T(8,128)(2,1)S(1)}, bf16[104,256]{1,0:T(8,128)(2,1)S(1)}, u32[]{:S(2)}, u32[]{:S(2)}) collective-permute-start(bf16[104,256]{1,0:T(8,128)(2,1)S(1)} %bitcast.22), channel_id=1, source_target_pairs={{0,512},{256,768},{512,0},{768,256},{1,513},{257,769},{513,1},{769... | collective-permute-start | bytes 159752 | tf_op jit(solution)/shard_map/ppermute | solution.py:147
  44.2 4.3 %collective-permute-start.2 = (bf16[104,256]{1,0:T(8,128)(2,1)S(1)}, bf16[104,256]{1,0:T(8,128)(2,1)S(1)}, u32[]{:S(2)}, u32[]{:S(2)}) collective-permute-start(bf16[104,256]{1,0:T(8,128)(2,1)S(1)} %bitcast.23), channel_id=1, source_target_pairs={{0,768},{256,0},{512,256},{768,512},{1,769},{257,1},{513,257},{769... | collective-permute-start | bytes 159752 | tf_op jit(solution)/shard_map/ppermute | solution.py:147
  48.5 0.0 all-to-all-done.1
  48.5 3.5 %collective-permute-start.5 = (bf16[64,2048]{1,0:T(8,128)(2,1)S(1)}, bf16[64,2048]{1,0:T(8,128)(2,1)S(1)}, u32[]{:S(2)}, u32[]{:S(2)}) collective-permute-start(bf16[64,2048]{1,0:T(8,128)(2,1)S(1)} %bitcast.10), channel_id=1, source_target_pairs={{0,32},{1,225},{32,64},{33,1},{64,96},{65,33},{96,128},{97,65},{12... | collective-permute-start | bytes 786440 | tf_op jit(solution)/shard_map/ppermute | solution.py:126
  52.0 1.9 %collective-permute-start.6 = (bf16[64,2048]{1,0:T(8,128)(2,1)S(1)}, bf16[64,2048]{1,0:T(8,128)(2,1)S(1)}, u32[]{:S(2)}, u32[]{:S(2)}) collective-permute-start(bf16[64,2048]{1,0:T(8,128)(2,1)S(1)} %bitcast.11), channel_id=1, source_target_pairs={{1,32},{0,225},{33,64},{32,1},{65,96},{64,33},{97,128},{96,65},{12... | collective-permute-start | bytes 786440 | tf_op jit(solution)/shard_map/ppermute | solution.py:126
  53.9 0.0 collective-permute-done
  53.9 0.0 collective-permute-done.1
  53.9 0.0 collective-permute-done.2
  53.9 0.0 copy-done.4
  54.0 4.8 %collective-permute-start.3 = (bf16[104,3072]{1,0:T(8,128)(2,1)S(1)}, bf16[104,3072]{1,0:T(8,128)(2,1)S(1)}, u32[]{:S(2)}, u32[]{:S(2)}) collective-permute-start(bf16[104,3072]{1,0:T(8,128)(2,1)S(1)} %constant_dynamic-update-slice_fusion.held), channel_id=1, source_target_pairs={{0,1},{1,0},{2,3},{3,2},{4,5},{5,4},{6,7},{7,6},{8,9},{9,8},{10,11... | collective-permute-start | bytes 1916936 | tf_op jit(solution)/shard_map/ppermute | solution.py:150
  58.9 0.0 collective-permute-done.5.refs_2_
  58.9 2.6 %collective-permute-start.7 = (bf16[64,2048]{1,0:T(8,128)(2,1)S(1)}, bf16[64,2048]{1,0:T(8,128)(2,1)S(1)}, u32[]{:S(2)}, u32[]{:S(2)}) collective-permute-start(bf16[64,2048]{1,0:T(8,128)(2,1)S(1)} %collective-permute-done.5.refs_2_), channel_id=1, source_target_pairs={{0,32},{1,225},{32,64},{33,1},{64,96},{65,33},{96,128},{97,65},{12... | collective-permute-start | bytes 786440 | tf_op jit(solution)/shard_map/ppermute | solution.py:126
  61.5 0.0 collective-permute-done.6.refs_3_
  61.5 5.5 %collective-permute-start.8 = (bf16[64,2048]{1,0:T(8,128)(2,1)S(1)}, bf16[64,2048]{1,0:T(8,128)(2,1)}, u32[]{:S(2)}, u32[]{:S(2)}) collective-permute-start(bf16[64,2048]{1,0:T(8,128)(2,1)S(1)} %collective-permute-done.6.refs_3_), channel_id=1, source_target_pairs={{0,32},{1,225},{32,64},{33,1},{64,96},{65,33},{96,128},{97,65},{12... | collective-permute-start | bytes 786440 | tf_op jit(solution)/shard_map/ppermute | solution.py:126
  67.0 1.9 %collective-permute-start.4 = (bf16[16,2048]{1,0:T(8,128)(2,1)S(1)}, bf16[16,2048]{1,0:T(8,128)(2,1)S(1)}, u32[]{:S(2)}, u32[]{:S(2)}) collective-permute-start(bf16[16,2048]{1,0:T(8,128)(2,1)S(1)} %bitcast.17), channel_id=1, source_target_pairs={{0,128},{32,160},{64,192},{96,224},{128,0},{160,32},{192,64},{224,... | collective-permute-start | bytes 196616 | tf_op jit(solution)/shard_map/ppermute | solution.py:140
  68.9 0.0 collective-permute-done.7.refs_4_
  68.9 2.5 %collective-permute-start.9 = (bf16[64,2048]{1,0:T(8,128)(2,1)S(1)}, bf16[64,2048]{1,0:T(8,128)(2,1)}, u32[]{:S(2)}, u32[]{:S(2)}) collective-permute-start(bf16[64,2048]{1,0:T(8,128)(2,1)S(1)} %collective-permute-done.7.refs_4_), channel_id=1, source_target_pairs={{0,32},{1,225},{32,64},{33,1},{64,96},{65,33},{96,128},{97,65},{12... | collective-permute-start | bytes 786440 | tf_op jit(solution)/shard_map/ppermute | solution.py:126
  71.4 1.4 %collective-permute-done.8.refs_5_ = bf16[64,2048]{1,0:T(8,128)(2,1)} collective-permute-done((bf16[64,2048]{1,0:T(8,128)(2,1)S(1)}, bf16[64,2048]{1,0:T(8,128)(2,1)}, u32[]{:S(2)}, u32[]{:S(2)}) %collective-permute-start.8) | collective-permute-done | bytes 262176 | tf_op jit(solution)/shard_map/ppermute | solution.py:126
  72.8 4.5 %collective-permute-start.10 = (bf16[64,2048]{1,0:T(8,128)(2,1)}, bf16[64,2048]{1,0:T(8,128)(2,1)}, u32[]{:S(2)}, u32[]{:S(2)}) collective-permute-start(bf16[64,2048]{1,0:T(8,128)(2,1)} %collective-permute-done.8.refs_5_), channel_id=1, source_target_pairs={{0,32},{1,225},{32,64},{33,1},{64,96},{65,33},{96,128},{97,65},{12... | collective-permute-start | bytes 786440 | tf_op jit(solution)/shard_map/ppermute | solution.py:126
  77.3 0.0 collective-permute-done.4
  77.3 0.7 broadcast_in_dim.24
  78.0 4.8 %all-to-all-start.2 = ((bf16[4,16,2048]{2,1,0:T(8,128)(2,1)}), bf16[4,16,2048]{2,1,0:T(8,128)(2,1)S(1)}, u32[]{:S(2)}, u32[]{:S(2)}) async-start(bf16[4,16,2048]{2,1,0:T(8,128)(2,1)} %broadcast_in_dim.24), calls=%async_computation.2 | async-start | bytes 524288 | tf_op jit(solution)/shard_map/all_to_all | solution.py:142
  82.8 0.0 collective-permute-done.3.partner
  82.8 0.9 copy-done
  83.7 1.1 %copy-done.1 = bf16[104,3072]{1,0:T(8,128)(2,1)S(1)} copy-done((bf16[104,3072]{1,0:T(8,128)(2,1)S(1)}, bf16[104,3072]{1,0:T(8,128)(2,1)}, u32[]{:S(2)}) %copy-start.1) | copy-done | bytes 639000
  84.8 1.5 %shard_map.50 = (bf16[224,512]{1,0:T(8,128)(2,1)S(1)}, bf16[224,2048]{1,0:T(8,128)(2,1)S(1)}, bf16[512,512]{1,0:T(8,128)(2,1)S(1)}, bf16[256,256]{1,0:T(8,128)(2,1)S(1)}) custom-call(s32[3]{0:T(128)S(1)} %pad_add_fusion.at, bf16[104,3072]{1,0:T(8,128)(2,1)S(1)} %constant_dynamic-update-slice_fusion.held, bf16[104,3072]{1,0:T(8,128)(2,1)S(1)} %copy-done.1), custom_call_target="tpu_custom_call" | custom-call | bytes 3080204 | tf_op jit(solution)/shard_map/pallas_call | solution.py:39
  86.3 0.7 copy-done.2
  87.0 2.5 %all-to-all-done.2 = bf16[4,16,2048]{2,1,0:T(8,128)(2,1)S(1)} async-done(((bf16[4,16,2048]{2,1,0:T(8,128)(2,1)}), bf16[4,16,2048]{2,1,0:T(8,128)(2,1)S(1)}, u32[]{:S(2)}, u32[]{:S(2)}) %all-to-all-start.2) | async-done | bytes 262176 | tf_op jit(solution)/shard_map/all_to_all | solution.py:142
  89.5 1.9 %shard_map.51.early = bf16[224,512]{1,0:T(8,128)(2,1)S(1)} custom-call(bf16[224,2048]{1,0:T(8,128)(2,1)S(1)} %get-tuple-element.23.weight, bf16[512,512]{1,0:T(8,128)(2,1)S(1)} %get-tuple-element.24.grouped, bf16[64,2048]{1,0:T(8,128)(2,1)S(1)} %bitcast.12, bf16[64,2048]{1,0:T(8,128)(2,1)S(1)} %bitcast.14, ...), custom_call_target="tpu_custom_call" | custom-call | flops 352321536 | bytes 3244032 | tf_op jit(solution)/shard_map/pallas_call | solution.py:39
  91.4 0.0 collective-permute-done.9.refs_0_.refs_6_
  91.4 0.0 collective-permute-done.10.refs_1_.refs_7_
  91.4 2.3 %shard_map.52 = bf16[8,104,128]{2,1,0:T(8,128)(2,1)} custom-call(bf16[224,2048]{1,0:T(8,128)(2,1)S(1)} %get-tuple-element.23.weight, bf16[512,512]{1,0:T(8,128)(2,1)S(1)} %get-tuple-element.24.grouped, bf16[224,512]{1,0:T(8,128)(2,1)S(1)} %shard_map.51.early, bf16[64,2048]{1,0:T(8,128)(2,1)} %collective-permute-done.9.refs_0_.refs_6_, ...), custom_call_target="tpu_custom_call" | custom-call | flops 117440512 | bytes 2408448 | tf_op jit(solution)/shard_map/pallas_call | solution.py:39
  93.8 3.5 %all-to-all-start.3 = ((bf16[8,104,128]{2,1,0:T(8,128)(2,1)}), bf16[8,104,128]{2,1,0:T(8,128)(2,1)S(1)}, u32[]{:S(2)}, u32[]{:S(2)}) async-start(bf16[8,104,128]{2,1,0:T(8,128)(2,1)} %shard_map.52), calls=%async_computation.3 | async-start | bytes 425984 | tf_op jit(solution)/shard_map/all_to_all | solution.py:175
  97.3 0.0 copy-done.3
  97.3 1.8 %shard_map.54 = (f32[104,2048]{1,0:T(8,128)S(1)}, bf16[104,2048]{1,0:T(8,128)(2,1)S(1)}) custom-call(bf16[224,512]{1,0:T(8,128)(2,1)S(1)} %copy-done.3, bf16[64,2048]{1,0:T(8,128)(2,1)S(1)} %bitcast.13, bf16[64,2048]{1,0:T(8,128)(2,1)S(1)} %bitcast.15, bf16[64,2048]{1,0:T(8,128)(2,1)S(1)} %collective-permute-done.5.refs_2_, ...), custom_call_target="tpu_custom_call" | custom-call | flops 469762048 | bytes 3604480 | tf_op jit(solution)/shard_map/pallas_call | solution.py:39
  99.1 2.3 %collective-permute-start.11 = (bf16[104,2048]{1,0:T(8,128)(2,1)S(1)}, bf16[104,2048]{1,0:T(8,128)(2,1)S(1)}, u32[]{:S(2)}, u32[]{:S(2)}) collective-permute-start(bf16[104,2048]{1,0:T(8,128)(2,1)S(1)} %get-tuple-element.27), channel_id=1, source_target_pairs={{0,1},{1,0},{2,3},{3,2},{4,5},{5,4},{6,7},{7,6},{8,9},{9,8},{10,11... | collective-permute-start | bytes 1277960 | tf_op jit(solution)/shard_map/ppermute | solution.py:180
  101.4 1.4 %collective-permute-done.11.taken = bf16[104,2048]{1,0:T(8,128)(2,1)S(1)} collective-permute-done((bf16[104,2048]{1,0:T(8,128)(2,1)S(1)}, bf16[104,2048]{1,0:T(8,128)(2,1)S(1)}, u32[]{:S(2)}, u32[]{:S(2)}) %collective-permute-start.11) | collective-permute-done | bytes 426016 | tf_op jit(solution)/shard_map/ppermute | solution.py:180
  102.8 0.8 shard_map.55
  103.6 2.3 %all-to-all-done.3.back = bf16[8,104,128]{2,1,0:T(8,128)(2,1)S(1)} async-done(((bf16[8,104,128]{2,1,0:T(8,128)(2,1)}), bf16[8,104,128]{2,1,0:T(8,128)(2,1)S(1)}, u32[]{:S(2)}, u32[]{:S(2)}) %all-to-all-start.3) | async-done | bytes 213024 | tf_op jit(solution)/shard_map/all_to_all | solution.py:175
  105.9 0.8 shard_map.53
  (13 shorter events, 0.1 us)
Async XLA Ops:
  33.4 20.6 %copy-start.4 = (bf16[104,2048]{1,0:T(8,128)(2,1)S(1)}, bf16[104,2048]{1,0:T(8,128)(2,1)}, u32[]{:S(2)}) copy-start(bf16[104,2048]{1,0:T(8,128)(2,1)} %param.5) | copy-start | bytes 1277956
  34.1 4.4 %copy-start.5 = (bf16[256,104]{0,1:T(8,128)(2,1)S(1)}, bf16[256,104]{0,1:T(8,128)(2,1)}, u32[]{:S(2)}) copy-start(bf16[256,104]{0,1:T(8,128)(2,1)} %param.3) | copy-start | bytes 159748
  34.1 14.4 %all-to-all-start.1 = ((bf16[4,16,2048]{2,1,0:T(8,128)(2,1)}), bf16[4,16,2048]{2,1,0:T(8,128)(2,1)S(1)}, u32[]{:S(2)}, u32[]{:S(2)}) async-start(bf16[4,16,2048]{2,1,0:T(8,128)(2,1)} %broadcast_in_dim.23), calls=%async_computation.1 | async-start | bytes 524288 | tf_op jit(solution)/shard_map/all_to_all | solution.py:139
  38.6 15.4 %collective-permute-start = (bf16[104,256]{1,0:T(8,128)(2,1)S(1)}, bf16[104,256]{1,0:T(8,128)(2,1)S(1)}, u32[]{:S(2)}, u32[]{:S(2)}) collective-permute-start(bf16[104,256]{1,0:T(8,128)(2,1)S(1)} %bitcast.21), channel_id=1, source_target_pairs={{0,256},{256,512},{512,768},{768,0},{1,257},{257,513},{513,769},{7... | collective-permute-start | bytes 159752 | tf_op jit(solution)/shard_map/ppermute | solution.py:147
  41.5 12.5 %collective-permute-start.1 = (bf16[104,256]{1,0:T(8,128)(2,1)S(1)}, bf16[104,256]{1,0:T(8,128)(2,1)S(1)}, u32[]{:S(2)}, u32[]{:S(2)}) collective-permute-start(bf16[104,256]{1,0:T(8,128)(2,1)S(1)} %bitcast.22), channel_id=1, source_target_pairs={{0,512},{256,768},{512,0},{768,256},{1,513},{257,769},{513,1},{769... | collective-permute-start | bytes 159752 | tf_op jit(solution)/shard_map/ppermute | solution.py:147
  44.2 9.8 %collective-permute-start.2 = (bf16[104,256]{1,0:T(8,128)(2,1)S(1)}, bf16[104,256]{1,0:T(8,128)(2,1)S(1)}, u32[]{:S(2)}, u32[]{:S(2)}) collective-permute-start(bf16[104,256]{1,0:T(8,128)(2,1)S(1)} %bitcast.23), channel_id=1, source_target_pairs={{0,768},{256,0},{512,256},{768,512},{1,769},{257,1},{513,257},{769... | collective-permute-start | bytes 159752 | tf_op jit(solution)/shard_map/ppermute | solution.py:147
  48.5 10.4 %collective-permute-start.5 = (bf16[64,2048]{1,0:T(8,128)(2,1)S(1)}, bf16[64,2048]{1,0:T(8,128)(2,1)S(1)}, u32[]{:S(2)}, u32[]{:S(2)}) collective-permute-start(bf16[64,2048]{1,0:T(8,128)(2,1)S(1)} %bitcast.10), channel_id=1, source_target_pairs={{0,32},{1,225},{32,64},{33,1},{64,96},{65,33},{96,128},{97,65},{12... | collective-permute-start | bytes 786440 | tf_op jit(solution)/shard_map/ppermute | solution.py:126
  52.0 9.5 %collective-permute-start.6 = (bf16[64,2048]{1,0:T(8,128)(2,1)S(1)}, bf16[64,2048]{1,0:T(8,128)(2,1)S(1)}, u32[]{:S(2)}, u32[]{:S(2)}) collective-permute-start(bf16[64,2048]{1,0:T(8,128)(2,1)S(1)} %bitcast.11), channel_id=1, source_target_pairs={{1,32},{0,225},{33,64},{32,1},{65,96},{64,33},{97,128},{96,65},{12... | collective-permute-start | bytes 786440 | tf_op jit(solution)/shard_map/ppermute | solution.py:126
  54.0 28.8 %collective-permute-start.3 = (bf16[104,3072]{1,0:T(8,128)(2,1)S(1)}, bf16[104,3072]{1,0:T(8,128)(2,1)S(1)}, u32[]{:S(2)}, u32[]{:S(2)}) collective-permute-start(bf16[104,3072]{1,0:T(8,128)(2,1)S(1)} %constant_dynamic-update-slice_fusion.held), channel_id=1, source_target_pairs={{0,1},{1,0},{2,3},{3,2},{4,5},{5,4},{6,7},{7,6},{8,9},{9,8},{10,11... | collective-permute-start | bytes 1916936 | tf_op jit(solution)/shard_map/ppermute | solution.py:150
  58.9 10.0 %collective-permute-start.7 = (bf16[64,2048]{1,0:T(8,128)(2,1)S(1)}, bf16[64,2048]{1,0:T(8,128)(2,1)S(1)}, u32[]{:S(2)}, u32[]{:S(2)}) collective-permute-start(bf16[64,2048]{1,0:T(8,128)(2,1)S(1)} %collective-permute-done.5.refs_2_), channel_id=1, source_target_pairs={{0,32},{1,225},{32,64},{33,1},{64,96},{65,33},{96,128},{97,65},{12... | collective-permute-start | bytes 786440 | tf_op jit(solution)/shard_map/ppermute | solution.py:126
  61.5 11.4 %collective-permute-start.8 = (bf16[64,2048]{1,0:T(8,128)(2,1)S(1)}, bf16[64,2048]{1,0:T(8,128)(2,1)}, u32[]{:S(2)}, u32[]{:S(2)}) collective-permute-start(bf16[64,2048]{1,0:T(8,128)(2,1)S(1)} %collective-permute-done.6.refs_3_), channel_id=1, source_target_pairs={{0,32},{1,225},{32,64},{33,1},{64,96},{65,33},{96,128},{97,65},{12... | collective-permute-start | bytes 786440 | tf_op jit(solution)/shard_map/ppermute | solution.py:126
  67.0 10.3 %collective-permute-start.4 = (bf16[16,2048]{1,0:T(8,128)(2,1)S(1)}, bf16[16,2048]{1,0:T(8,128)(2,1)S(1)}, u32[]{:S(2)}, u32[]{:S(2)}) collective-permute-start(bf16[16,2048]{1,0:T(8,128)(2,1)S(1)} %bitcast.17), channel_id=1, source_target_pairs={{0,128},{32,160},{64,192},{96,224},{128,0},{160,32},{192,64},{224,... | collective-permute-start | bytes 196616 | tf_op jit(solution)/shard_map/ppermute | solution.py:140
  68.9 22.5 %collective-permute-start.9 = (bf16[64,2048]{1,0:T(8,128)(2,1)S(1)}, bf16[64,2048]{1,0:T(8,128)(2,1)}, u32[]{:S(2)}, u32[]{:S(2)}) collective-permute-start(bf16[64,2048]{1,0:T(8,128)(2,1)S(1)} %collective-permute-done.7.refs_4_), channel_id=1, source_target_pairs={{0,32},{1,225},{32,64},{33,1},{64,96},{65,33},{96,128},{97,65},{12... | collective-permute-start | bytes 786440 | tf_op jit(solution)/shard_map/ppermute | solution.py:126
  72.8 18.6 %collective-permute-start.10 = (bf16[64,2048]{1,0:T(8,128)(2,1)}, bf16[64,2048]{1,0:T(8,128)(2,1)}, u32[]{:S(2)}, u32[]{:S(2)}) collective-permute-start(bf16[64,2048]{1,0:T(8,128)(2,1)} %collective-permute-done.8.refs_5_), channel_id=1, source_target_pairs={{0,32},{1,225},{32,64},{33,1},{64,96},{65,33},{96,128},{97,65},{12... | collective-permute-start | bytes 786440 | tf_op jit(solution)/shard_map/ppermute | solution.py:126
  78.0 11.5 %all-to-all-start.2 = ((bf16[4,16,2048]{2,1,0:T(8,128)(2,1)}), bf16[4,16,2048]{2,1,0:T(8,128)(2,1)S(1)}, u32[]{:S(2)}, u32[]{:S(2)}) async-start(bf16[4,16,2048]{2,1,0:T(8,128)(2,1)} %broadcast_in_dim.24), calls=%async_computation.2 | async-start | bytes 524288 | tf_op jit(solution)/shard_map/all_to_all | solution.py:142
  82.8 0.9 copy-start
  83.7 1.1 %copy-start.1 = (bf16[104,3072]{1,0:T(8,128)(2,1)S(1)}, bf16[104,3072]{1,0:T(8,128)(2,1)}, u32[]{:S(2)}) copy-start(bf16[104,3072]{1,0:T(8,128)(2,1)} %copy-done) | copy-start | bytes 1916932
  86.3 0.7 copy-start.2
  93.8 3.5 %copy-start.3 = (bf16[224,512]{1,0:T(8,128)(2,1)S(1)}, bf16[224,512]{1,0:T(8,128)(2,1)}, u32[]{:S(2)}) copy-start(bf16[224,512]{1,0:T(8,128)(2,1)} %copy-done.2) | copy-start | bytes 688132
  93.8 12.1 %all-to-all-start.3 = ((bf16[8,104,128]{2,1,0:T(8,128)(2,1)}), bf16[8,104,128]{2,1,0:T(8,128)(2,1)S(1)}, u32[]{:S(2)}, u32[]{:S(2)}) async-start(bf16[8,104,128]{2,1,0:T(8,128)(2,1)} %shard_map.52), calls=%async_computation.3 | async-start | bytes 425984 | tf_op jit(solution)/shard_map/all_to_all | solution.py:175
  99.1 3.7 %collective-permute-start.11 = (bf16[104,2048]{1,0:T(8,128)(2,1)S(1)}, bf16[104,2048]{1,0:T(8,128)(2,1)S(1)}, u32[]{:S(2)}, u32[]{:S(2)}) collective-permute-start(bf16[104,2048]{1,0:T(8,128)(2,1)S(1)} %get-tuple-element.27), channel_id=1, source_target_pairs={{0,1},{1,0},{2,3},{3,2},{4,5},{5,4},{6,7},{7,6},{8,9},{9,8},{10,11... | collective-permute-start | bytes 1277960 | tf_op jit(solution)/shard_map/ppermute | solution.py:180

commit v6 on v5

--- a/solution.py
+++ b/solution.py
@@ -68,7 +68,7 @@
     hot_last[...] = (token_at(iota((TOK, TOK), 0), y) == iota((TOK, TOK), 1)).astype(BF16)
     p = iota((1, total), 1)
     token = token_at(me * HALF + (p >> 6) * 16 + ((p >> 4) & 3) * 4 + (p & 3), y)
-    wanted = ((g - ((p >> 2) & 3)) & 3) * TOK + token
+    wanted = (g ^ ((p >> 2) & 3)) * TOK + token
     hot = (iota((DP * TOK, total), 0) == wanted).astype(BF16)
     gap = jnp.zeros((pad - ff, total), F32)
     blank = jnp.zeros((pad - ff, width), BF16)
@@ -142,10 +142,9 @@
     u4 = lax.all_to_all(away, "x", 0, 0, tiled=True).reshape(ROWS, width)
 
     here = hidden.T
-    there = []
-    for k in range(1, DP):
-        there.append(lax.ppermute(here, "dp", [(g, (g + k) % DP) for g in range(DP)]))
-    *pieces, _ = lax.optimization_barrier((down_weight, here, *there, u0))
+    one = lax.ppermute(here, "dp", [(g, g ^ 1) for g in range(DP)])
+    two = lax.ppermute(jnp.concatenate([here, one], axis=1), "dp", [(g, g ^ 2) for g in range(DP)])
+    *pieces, _ = lax.optimization_barrier((down_weight, here, one, two, u0))
     held = jnp.concatenate(pieces, axis=1)
     partner = lax.ppermute(held, "core", SWAP)
     units, weight, grouped, hot = call(

time: 108 us -> 104 us (0.963)
  blocking collectives: 31.8 us -> 0 us
  starting transfers between devices: 52.1 us -> 66.5 us
  waiting for transfers between devices: 7.69 us -> 20.9 us
    all_to_all x1 -> x0, blocking collectives: 31.8 us -> none  [step(): lax.all_to_all(row, ('dp', 'zh'), 0, 0, tiled=True).reshape(DP * ZH, width)]
    all_to_all x0 -> x1, starting transfers between devices: none -> 19 us  [step(): lax.all_to_all(row, ('dp', 'zh'), 0, 0, tiled=True).reshape(DP * ZH, width)]
    all_to_all x0 -> x1, waiting for transfers between devices: none -> 9.49 us  [step(): lax.all_to_all(row, ('dp', 'zh'), 0, 0, tiled=True).reshape(DP * ZH, width)]
    all_to_all x1, waiting for transfers between devices: 0.01 us -> 3.73 us  [step(): u0 = lax.all_to_all(spread, 'x', 0, 0, tiled=True).reshape(ROWS, width)]
    ppermute x3 -> x2, starting transfers between devices: 9.9 us -> 6.76 us  [the longest x1 3.83 us: step(): one = lax.ppermute(here, 'dp', [(g, g ^ 1) for g in range(DP)])]
    all_to_all x1, starting transfers between devices: 4.8 us -> 3.41 us  [step(): u4 = lax.all_to_all(away, 'x', 0, 0, tiled=True).reshape(ROWS, width)]
    unnamed x17 -> x16, local copies, waits for them, and re-layouts: 2.7 us -> 2.68 us
  transfers between devices with their start and end apart: 15 -> 15, of which waited for: 4 -> 6; matrix products, arithmetic and copies ran while one was open for 1% -> 1% of each run, Pallas kernels for 6% -> 6%
where the time goes in v6:
time: 104 us; the launch traced here: 103 us
  starting transfers between devices  66.5 us (64%)
  waiting for transfers between devices  20.9 us (20%)
  Pallas kernels  9.11 us (9%)
  local copies, waits for them, and re-layouts  4.82 us (5%)
    ppermute x6, starting transfers between devices, ring(): return lax.ppermute(value, ('y', 'core'), ring_pairs(cross))  20.4 us
    all_to_all x1, starting transfers between devices, step(): lax.all_to_all(row, ('dp', 'zh'), 0, 0, tiled=True).reshape(DP * ZH, width)  19 us
    all_to_all x1, waiting for transfers between devices, step(): lax.all_to_all(row, ('dp', 'zh'), 0, 0, tiled=True).reshape(DP * ZH, width)  9.49 us
    pallas_call x6, Pallas kernels, call(): pl.pallas_call(body, out_shape=outs, in_specs=specs, out_specs=[VMEM] * l...  9.11 us
    ppermute x1, starting transfers between devices, step(): partner = lax.ppermute(held, 'core', SWAP)  4.8 us
    all_to_all x1, starting transfers between devices, step(): u0 = lax.all_to_all(spread, 'x', 0, 0, tiled=True).reshape(ROWS, width)  4.42 us
    ppermute x1, starting transfers between devices, step(): one = lax.ppermute(here, 'dp', [(g, g ^ 1) for g in range(DP)])  3.83 us
    all_to_all x1, waiting for transfers between devices, step(): u0 = lax.all_to_all(spread, 'x', 0, 0, tiled=True).reshape(ROWS, width)  3.73 us
  transfers between devices with their start and end apart: 15, of which 6 were waited for; matrix products, arithmetic and copies ran while one was open for 1% of the time, Pallas kernels for 6%

profile of v6, /device:TPU:16, one launch (start us, length us, event | category | flops | bytes accessed | tf_op | source)
XLA Modules:
  0.0 103.2 jit_solution(13760796741562971667)
XLA Ops:
  0.6 0.8 reduce
  1.5 0.1 pad_add_fusion.at
  1.6 0.7 broadcast_in_dim.21
  2.3 19.0 %all-to-all-start = ((bf16[16,2,1024]{2,1,0:T(2,128)(2,1)}), bf16[16,2,1024]{2,1,0:T(2,128)(2,1)S(1)}, u32[]{:S(2)}, u32[]{:S(2)}) async-start(bf16[16,2,1024]{2,1,0:T(2,128)(2,1)} %bitcast), calls=%async_computation | async-start | bytes 131072 | tf_op jit(solution)/shard_map/all_to_all | solution.py:137
  21.3 0.0 copy-done.5
  21.3 3.8 %collective-permute-start = (bf16[104,256]{1,0:T(8,128)(2,1)S(1)}, bf16[104,256]{1,0:T(8,128)(2,1)S(1)}, u32[]{:S(2)}, u32[]{:S(2)}) collective-permute-start(bf16[104,256]{1,0:T(8,128)(2,1)S(1)} %bitcast.19), channel_id=1, source_target_pairs={{0,256},{256,0},{512,768},{768,512},{1,257},{257,1},{513,769},{769... | collective-permute-start | bytes 159752 | tf_op jit(solution)/shard_map/ppermute | solution.py:145
  25.1 9.5 %all-to-all-done = bf16[16,2,1024]{2,1,0:T(2,128)(2,1)S(1)} async-done(((bf16[16,2,1024]{2,1,0:T(2,128)(2,1)}), bf16[16,2,1024]{2,1,0:T(2,128)(2,1)S(1)}, u32[]{:S(2)}, u32[]{:S(2)}) %all-to-all-start) | async-done | bytes 65568 | tf_op jit(solution)/shard_map/all_to_all | solution.py:137
  34.6 0.7 broadcast_in_dim.23
  35.3 4.4 %all-to-all-start.1 = ((bf16[4,16,2048]{2,1,0:T(8,128)(2,1)}), bf16[4,16,2048]{2,1,0:T(8,128)(2,1)S(1)}, u32[]{:S(2)}, u32[]{:S(2)}) async-start(bf16[4,16,2048]{2,1,0:T(8,128)(2,1)} %broadcast_in_dim.23), calls=%async_computation.1 | async-start | bytes 524288 | tf_op jit(solution)/shard_map/all_to_all | solution.py:139
  39.8 0.0 collective-permute-done
  39.8 2.9 %collective-permute-start.1 = (bf16[104,512]{1,0:T(8,128)(2,1)S(1)}, bf16[104,512]{1,0:T(8,128)(2,1)S(1)}, u32[]{:S(2)}, u32[]{:S(2)}) collective-permute-start(bf16[104,512]{1,0:T(8,128)(2,1)S(1)} %pad_maximum_fusion), channel_id=1, source_target_pairs={{0,512},{256,768},{512,0},{768,256},{1,513},{257,769},{513,1},{769... | collective-permute-start | bytes 319496 | tf_op jit(solution)/shard_map/ppermute | solution.py:146
  42.7 3.7 %all-to-all-done.1 = bf16[4,16,2048]{2,1,0:T(8,128)(2,1)S(1)} async-done(((bf16[4,16,2048]{2,1,0:T(8,128)(2,1)}), bf16[4,16,2048]{2,1,0:T(8,128)(2,1)S(1)}, u32[]{:S(2)}, u32[]{:S(2)}) %all-to-all-start.1) | async-done | bytes 262176 | tf_op jit(solution)/shard_map/all_to_all | solution.py:139
  46.4 3.5 %collective-permute-start.4 = (bf16[64,2048]{1,0:T(8,128)(2,1)S(1)}, bf16[64,2048]{1,0:T(8,128)(2,1)S(1)}, u32[]{:S(2)}, u32[]{:S(2)}) collective-permute-start(bf16[64,2048]{1,0:T(8,128)(2,1)S(1)} %bitcast.10), channel_id=1, source_target_pairs={{0,32},{1,225},{32,64},{33,1},{64,96},{65,33},{96,128},{97,65},{12... | collective-permute-start | bytes 786440 | tf_op jit(solution)/shard_map/ppermute | solution.py:126
  49.9 1.9 %collective-permute-start.5 = (bf16[64,2048]{1,0:T(8,128)(2,1)S(1)}, bf16[64,2048]{1,0:T(8,128)(2,1)S(1)}, u32[]{:S(2)}, u32[]{:S(2)}) collective-permute-start(bf16[64,2048]{1,0:T(8,128)(2,1)S(1)} %bitcast.11), channel_id=1, source_target_pairs={{1,32},{0,225},{33,64},{32,1},{65,96},{64,33},{97,128},{96,65},{12... | collective-permute-start | bytes 786440 | tf_op jit(solution)/shard_map/ppermute | solution.py:126
  51.8 0.0 collective-permute-done.1
  51.9 0.0 copy-done.4
  51.9 4.8 %collective-permute-start.2 = (bf16[104,3072]{1,0:T(8,128)(2,1)S(1)}, bf16[104,3072]{1,0:T(8,128)(2,1)S(1)}, u32[]{:S(2)}, u32[]{:S(2)}) collective-permute-start(bf16[104,3072]{1,0:T(8,128)(2,1)S(1)} %constant_dynamic-update-slice_fusion.held), channel_id=1, source_target_pairs={{0,1},{1,0},{2,3},{3,2},{4,5},{5,4},{6,7},{7,6},{8,9},{9,8},{10,11... | collective-permute-start | bytes 1916936 | tf_op jit(solution)/shard_map/ppermute | solution.py:149
  56.8 0.0 collective-permute-done.4.refs_2_
  56.8 2.6 %collective-permute-start.6 = (bf16[64,2048]{1,0:T(8,128)(2,1)S(1)}, bf16[64,2048]{1,0:T(8,128)(2,1)S(1)}, u32[]{:S(2)}, u32[]{:S(2)}) collective-permute-start(bf16[64,2048]{1,0:T(8,128)(2,1)S(1)} %collective-permute-done.4.refs_2_), channel_id=1, source_target_pairs={{0,32},{1,225},{32,64},{33,1},{64,96},{65,33},{96,128},{97,65},{12... | collective-permute-start | bytes 786440 | tf_op jit(solution)/shard_map/ppermute | solution.py:126
  59.4 0.0 collective-permute-done.5.refs_3_
  59.4 5.5 %collective-permute-start.7 = (bf16[64,2048]{1,0:T(8,128)(2,1)S(1)}, bf16[64,2048]{1,0:T(8,128)(2,1)}, u32[]{:S(2)}, u32[]{:S(2)}) collective-permute-start(bf16[64,2048]{1,0:T(8,128)(2,1)S(1)} %collective-permute-done.5.refs_3_), channel_id=1, source_target_pairs={{0,32},{1,225},{32,64},{33,1},{64,96},{65,33},{96,128},{97,65},{12... | collective-permute-start | bytes 786440 | tf_op jit(solution)/shard_map/ppermute | solution.py:126
  64.9 1.9 %collective-permute-start.3 = (bf16[16,2048]{1,0:T(8,128)(2,1)S(1)}, bf16[16,2048]{1,0:T(8,128)(2,1)S(1)}, u32[]{:S(2)}, u32[]{:S(2)}) collective-permute-start(bf16[16,2048]{1,0:T(8,128)(2,1)S(1)} %bitcast.17), channel_id=1, source_target_pairs={{0,128},{32,160},{64,192},{96,224},{128,0},{160,32},{192,64},{224,... | collective-permute-start | bytes 196616 | tf_op jit(solution)/shard_map/ppermute | solution.py:140
  66.8 0.0 collective-permute-done.6.refs_4_
  66.8 2.5 %collective-permute-start.8 = (bf16[64,2048]{1,0:T(8,128)(2,1)S(1)}, bf16[64,2048]{1,0:T(8,128)(2,1)}, u32[]{:S(2)}, u32[]{:S(2)}) collective-permute-start(bf16[64,2048]{1,0:T(8,128)(2,1)S(1)} %collective-permute-done.6.refs_4_), channel_id=1, source_target_pairs={{0,32},{1,225},{32,64},{33,1},{64,96},{65,33},{96,128},{97,65},{12... | collective-permute-start | bytes 786440 | tf_op jit(solution)/shard_map/ppermute | solution.py:126
  69.3 1.4 %collective-permute-done.7.refs_5_ = bf16[64,2048]{1,0:T(8,128)(2,1)} collective-permute-done((bf16[64,2048]{1,0:T(8,128)(2,1)S(1)}, bf16[64,2048]{1,0:T(8,128)(2,1)}, u32[]{:S(2)}, u32[]{:S(2)}) %collective-permute-start.7) | collective-permute-done | bytes 262176 | tf_op jit(solution)/shard_map/ppermute | solution.py:126
  70.7 4.5 %collective-permute-start.9 = (bf16[64,2048]{1,0:T(8,128)(2,1)}, bf16[64,2048]{1,0:T(8,128)(2,1)}, u32[]{:S(2)}, u32[]{:S(2)}) collective-permute-start(bf16[64,2048]{1,0:T(8,128)(2,1)} %collective-permute-done.7.refs_5_), channel_id=1, source_target_pairs={{0,32},{1,225},{32,64},{33,1},{64,96},{65,33},{96,128},{97,65},{12... | collective-permute-start | bytes 786440 | tf_op jit(solution)/shard_map/ppermute | solution.py:126
  75.2 0.0 collective-permute-done.3
  75.2 0.7 broadcast_in_dim.24
  75.9 3.4 %all-to-all-start.2 = ((bf16[4,16,2048]{2,1,0:T(8,128)(2,1)}), bf16[4,16,2048]{2,1,0:T(8,128)(2,1)S(1)}, u32[]{:S(2)}, u32[]{:S(2)}) async-start(bf16[4,16,2048]{2,1,0:T(8,128)(2,1)} %broadcast_in_dim.24), calls=%async_computation.2 | async-start | bytes 524288 | tf_op jit(solution)/shard_map/all_to_all | solution.py:142
  79.3 0.0 collective-permute-done.2.partner
  79.3 0.0 copy-start
  79.4 0.9 copy-done
  80.2 1.1 %copy-done.1 = bf16[104,3072]{1,0:T(8,128)(2,1)S(1)} copy-done((bf16[104,3072]{1,0:T(8,128)(2,1)S(1)}, bf16[104,3072]{1,0:T(8,128)(2,1)}, u32[]{:S(2)}) %copy-start.1) | copy-done | bytes 639000
  81.3 1.5 %shard_map.50 = (bf16[224,512]{1,0:T(8,128)(2,1)S(1)}, bf16[224,2048]{1,0:T(8,128)(2,1)S(1)}, bf16[512,512]{1,0:T(8,128)(2,1)S(1)}, bf16[256,256]{1,0:T(8,128)(2,1)S(1)}) custom-call(s32[3]{0:T(128)S(1)} %pad_add_fusion.at, bf16[104,3072]{1,0:T(8,128)(2,1)S(1)} %constant_dynamic-update-slice_fusion.held, bf16[104,3072]{1,0:T(8,128)(2,1)S(1)} %copy-done.1), custom_call_target="tpu_custom_call" | custom-call | bytes 3080204 | tf_op jit(solution)/shard_map/pallas_call | solution.py:39
  82.8 0.7 copy-done.2
  83.5 2.5 %all-to-all-done.2 = bf16[4,16,2048]{2,1,0:T(8,128)(2,1)S(1)} async-done(((bf16[4,16,2048]{2,1,0:T(8,128)(2,1)}), bf16[4,16,2048]{2,1,0:T(8,128)(2,1)S(1)}, u32[]{:S(2)}, u32[]{:S(2)}) %all-to-all-start.2) | async-done | bytes 262176 | tf_op jit(solution)/shard_map/all_to_all | solution.py:142
  86.0 1.9 %shard_map.51.early = bf16[224,512]{1,0:T(8,128)(2,1)S(1)} custom-call(bf16[224,2048]{1,0:T(8,128)(2,1)S(1)} %get-tuple-element.21.weight, bf16[512,512]{1,0:T(8,128)(2,1)S(1)} %get-tuple-element.22.grouped, bf16[64,2048]{1,0:T(8,128)(2,1)S(1)} %bitcast.12, bf16[64,2048]{1,0:T(8,128)(2,1)S(1)} %bitcast.14, ...), custom_call_target="tpu_custom_call" | custom-call | flops 352321536 | bytes 3244032 | tf_op jit(solution)/shard_map/pallas_call | solution.py:39
  87.9 0.0 collective-permute-done.8.refs_0_.refs_6_
  87.9 0.0 collective-permute-done.9.refs_1_.refs_7_
  87.9 2.3 %shard_map.52 = bf16[8,104,128]{2,1,0:T(8,128)(2,1)} custom-call(bf16[224,2048]{1,0:T(8,128)(2,1)S(1)} %get-tuple-element.21.weight, bf16[512,512]{1,0:T(8,128)(2,1)S(1)} %get-tuple-element.22.grouped, bf16[224,512]{1,0:T(8,128)(2,1)S(1)} %shard_map.51.early, bf16[64,2048]{1,0:T(8,128)(2,1)} %collective-permute-done.8.refs_0_.refs_6_, ...), custom_call_target="tpu_custom_call" | custom-call | flops 117440512 | bytes 2408448 | tf_op jit(solution)/shard_map/pallas_call | solution.py:39
  90.3 3.5 %all-to-all-start.3 = ((bf16[8,104,128]{2,1,0:T(8,128)(2,1)}), bf16[8,104,128]{2,1,0:T(8,128)(2,1)S(1)}, u32[]{:S(2)}, u32[]{:S(2)}) async-start(bf16[8,104,128]{2,1,0:T(8,128)(2,1)} %shard_map.52), calls=%async_computation.3 | async-start | bytes 425984 | tf_op jit(solution)/shard_map/all_to_all | solution.py:174
  93.8 0.0 copy-done.3
  93.8 1.8 %shard_map.54 = (f32[104,2048]{1,0:T(8,128)S(1)}, bf16[104,2048]{1,0:T(8,128)(2,1)S(1)}) custom-call(bf16[224,512]{1,0:T(8,128)(2,1)S(1)} %copy-done.3, bf16[64,2048]{1,0:T(8,128)(2,1)S(1)} %bitcast.13, bf16[64,2048]{1,0:T(8,128)(2,1)S(1)} %bitcast.15, bf16[64,2048]{1,0:T(8,128)(2,1)S(1)} %collective-permute-done.4.refs_2_, ...), custom_call_target="tpu_custom_call" | custom-call | flops 469762048 | bytes 3604480 | tf_op jit(solution)/shard_map/pallas_call | solution.py:39
  95.6 2.3 %collective-permute-start.10 = (bf16[104,2048]{1,0:T(8,128)(2,1)S(1)}, bf16[104,2048]{1,0:T(8,128)(2,1)S(1)}, u32[]{:S(2)}, u32[]{:S(2)}) collective-permute-start(bf16[104,2048]{1,0:T(8,128)(2,1)S(1)} %get-tuple-element.25), channel_id=1, source_target_pairs={{0,1},{1,0},{2,3},{3,2},{4,5},{5,4},{6,7},{7,6},{8,9},{9,8},{10,11... | collective-permute-start | bytes 1277960 | tf_op jit(solution)/shard_map/ppermute | solution.py:179
  97.9 1.4 %collective-permute-done.10.taken = bf16[104,2048]{1,0:T(8,128)(2,1)S(1)} collective-permute-done((bf16[104,2048]{1,0:T(8,128)(2,1)S(1)}, bf16[104,2048]{1,0:T(8,128)(2,1)S(1)}, u32[]{:S(2)}, u32[]{:S(2)}) %collective-permute-start.10) | collective-permute-done | bytes 426016 | tf_op jit(solution)/shard_map/ppermute | solution.py:179
  99.3 0.8 shard_map.55
  100.1 2.3 %all-to-all-done.3.back = bf16[8,104,128]{2,1,0:T(8,128)(2,1)S(1)} async-done(((bf16[8,104,128]{2,1,0:T(8,128)(2,1)}), bf16[8,104,128]{2,1,0:T(8,128)(2,1)S(1)}, u32[]{:S(2)}, u32[]{:S(2)}) %all-to-all-start.3) | async-done | bytes 213024 | tf_op jit(solution)/shard_map/all_to_all | solution.py:174
  102.4 0.8 shard_map.53
  (12 shorter events, 0.1 us)
Async XLA Ops:
  2.2 19.0 %copy-start.5 = (bf16[256,104]{0,1:T(8,128)(2,1)S(1)}, bf16[256,104]{0,1:T(8,128)(2,1)}, u32[]{:S(2)}) copy-start(bf16[256,104]{0,1:T(8,128)(2,1)} %param.3) | copy-start | bytes 159748
  2.3 32.3 %all-to-all-start = ((bf16[16,2,1024]{2,1,0:T(2,128)(2,1)}), bf16[16,2,1024]{2,1,0:T(2,128)(2,1)S(1)}, u32[]{:S(2)}, u32[]{:S(2)}) async-start(bf16[16,2,1024]{2,1,0:T(2,128)(2,1)} %bitcast), calls=%async_computation | async-start | bytes 131072 | tf_op jit(solution)/shard_map/all_to_all | solution.py:137
  21.3 18.5 %collective-permute-start = (bf16[104,256]{1,0:T(8,128)(2,1)S(1)}, bf16[104,256]{1,0:T(8,128)(2,1)S(1)}, u32[]{:S(2)}, u32[]{:S(2)}) collective-permute-start(bf16[104,256]{1,0:T(8,128)(2,1)S(1)} %bitcast.19), channel_id=1, source_target_pairs={{0,256},{256,0},{512,768},{768,512},{1,257},{257,1},{513,769},{769... | collective-permute-start | bytes 159752 | tf_op jit(solution)/shard_map/ppermute | solution.py:145
  35.3 16.5 %copy-start.4 = (bf16[104,2048]{1,0:T(8,128)(2,1)S(1)}, bf16[104,2048]{1,0:T(8,128)(2,1)}, u32[]{:S(2)}) copy-start(bf16[104,2048]{1,0:T(8,128)(2,1)} %param.5) | copy-start | bytes 1277956
  35.3 11.1 %all-to-all-start.1 = ((bf16[4,16,2048]{2,1,0:T(8,128)(2,1)}), bf16[4,16,2048]{2,1,0:T(8,128)(2,1)S(1)}, u32[]{:S(2)}, u32[]{:S(2)}) async-start(bf16[4,16,2048]{2,1,0:T(8,128)(2,1)} %broadcast_in_dim.23), calls=%async_computation.1 | async-start | bytes 524288 | tf_op jit(solution)/shard_map/all_to_all | solution.py:139
  39.8 12.1 %collective-permute-start.1 = (bf16[104,512]{1,0:T(8,128)(2,1)S(1)}, bf16[104,512]{1,0:T(8,128)(2,1)S(1)}, u32[]{:S(2)}, u32[]{:S(2)}) collective-permute-start(bf16[104,512]{1,0:T(8,128)(2,1)S(1)} %pad_maximum_fusion), channel_id=1, source_target_pairs={{0,512},{256,768},{512,0},{768,256},{1,513},{257,769},{513,1},{769... | collective-permute-start | bytes 319496 | tf_op jit(solution)/shard_map/ppermute | solution.py:146
  46.4 10.3 %collective-permute-start.4 = (bf16[64,2048]{1,0:T(8,128)(2,1)S(1)}, bf16[64,2048]{1,0:T(8,128)(2,1)S(1)}, u32[]{:S(2)}, u32[]{:S(2)}) collective-permute-start(bf16[64,2048]{1,0:T(8,128)(2,1)S(1)} %bitcast.10), channel_id=1, source_target_pairs={{0,32},{1,225},{32,64},{33,1},{64,96},{65,33},{96,128},{97,65},{12... | collective-permute-start | bytes 786440 | tf_op jit(solution)/shard_map/ppermute | solution.py:126
  49.9 9.4 %collective-permute-start.5 = (bf16[64,2048]{1,0:T(8,128)(2,1)S(1)}, bf16[64,2048]{1,0:T(8,128)(2,1)S(1)}, u32[]{:S(2)}, u32[]{:S(2)}) collective-permute-start(bf16[64,2048]{1,0:T(8,128)(2,1)S(1)} %bitcast.11), channel_id=1, source_target_pairs={{1,32},{0,225},{33,64},{32,1},{65,96},{64,33},{97,128},{96,65},{12... | collective-permute-start | bytes 786440 | tf_op jit(solution)/shard_map/ppermute | solution.py:126
  51.9 27.4 %collective-permute-start.2 = (bf16[104,3072]{1,0:T(8,128)(2,1)S(1)}, bf16[104,3072]{1,0:T(8,128)(2,1)S(1)}, u32[]{:S(2)}, u32[]{:S(2)}) collective-permute-start(bf16[104,3072]{1,0:T(8,128)(2,1)S(1)} %constant_dynamic-update-slice_fusion.held), channel_id=1, source_target_pairs={{0,1},{1,0},{2,3},{3,2},{4,5},{5,4},{6,7},{7,6},{8,9},{9,8},{10,11... | collective-permute-start | bytes 1916936 | tf_op jit(solution)/shard_map/ppermute | solution.py:149
  56.8 10.0 %collective-permute-start.6 = (bf16[64,2048]{1,0:T(8,128)(2,1)S(1)}, bf16[64,2048]{1,0:T(8,128)(2,1)S(1)}, u32[]{:S(2)}, u32[]{:S(2)}) collective-permute-start(bf16[64,2048]{1,0:T(8,128)(2,1)S(1)} %collective-permute-done.4.refs_2_), channel_id=1, source_target_pairs={{0,32},{1,225},{32,64},{33,1},{64,96},{65,33},{96,128},{97,65},{12... | collective-permute-start | bytes 786440 | tf_op jit(solution)/shard_map/ppermute | solution.py:126
  59.4 11.4 %collective-permute-start.7 = (bf16[64,2048]{1,0:T(8,128)(2,1)S(1)}, bf16[64,2048]{1,0:T(8,128)(2,1)}, u32[]{:S(2)}, u32[]{:S(2)}) collective-permute-start(bf16[64,2048]{1,0:T(8,128)(2,1)S(1)} %collective-permute-done.5.refs_3_), channel_id=1, source_target_pairs={{0,32},{1,225},{32,64},{33,1},{64,96},{65,33},{96,128},{97,65},{12... | collective-permute-start | bytes 786440 | tf_op jit(solution)/shard_map/ppermute | solution.py:126
  64.9 10.3 %collective-permute-start.3 = (bf16[16,2048]{1,0:T(8,128)(2,1)S(1)}, bf16[16,2048]{1,0:T(8,128)(2,1)S(1)}, u32[]{:S(2)}, u32[]{:S(2)}) collective-permute-start(bf16[16,2048]{1,0:T(8,128)(2,1)S(1)} %bitcast.17), channel_id=1, source_target_pairs={{0,128},{32,160},{64,192},{96,224},{128,0},{160,32},{192,64},{224,... | collective-permute-start | bytes 196616 | tf_op jit(solution)/shard_map/ppermute | solution.py:140
  66.8 21.1 %collective-permute-start.8 = (bf16[64,2048]{1,0:T(8,128)(2,1)S(1)}, bf16[64,2048]{1,0:T(8,128)(2,1)}, u32[]{:S(2)}, u32[]{:S(2)}) collective-permute-start(bf16[64,2048]{1,0:T(8,128)(2,1)S(1)} %collective-permute-done.6.refs_4_), channel_id=1, source_target_pairs={{0,32},{1,225},{32,64},{33,1},{64,96},{65,33},{96,128},{97,65},{12... | collective-permute-start | bytes 786440 | tf_op jit(solution)/shard_map/ppermute | solution.py:126
  70.7 17.2 %collective-permute-start.9 = (bf16[64,2048]{1,0:T(8,128)(2,1)}, bf16[64,2048]{1,0:T(8,128)(2,1)}, u32[]{:S(2)}, u32[]{:S(2)}) collective-permute-start(bf16[64,2048]{1,0:T(8,128)(2,1)} %collective-permute-done.7.refs_5_), channel_id=1, source_target_pairs={{0,32},{1,225},{32,64},{33,1},{64,96},{65,33},{96,128},{97,65},{12... | collective-permute-start | bytes 786440 | tf_op jit(solution)/shard_map/ppermute | solution.py:126
  75.9 10.1 %all-to-all-start.2 = ((bf16[4,16,2048]{2,1,0:T(8,128)(2,1)}), bf16[4,16,2048]{2,1,0:T(8,128)(2,1)S(1)}, u32[]{:S(2)}, u32[]{:S(2)}) async-start(bf16[4,16,2048]{2,1,0:T(8,128)(2,1)} %broadcast_in_dim.24), calls=%async_computation.2 | async-start | bytes 524288 | tf_op jit(solution)/shard_map/all_to_all | solution.py:142
  79.3 0.9 copy-start
  80.2 1.1 %copy-start.1 = (bf16[104,3072]{1,0:T(8,128)(2,1)S(1)}, bf16[104,3072]{1,0:T(8,128)(2,1)}, u32[]{:S(2)}) copy-start(bf16[104,3072]{1,0:T(8,128)(2,1)} %copy-done) | copy-start | bytes 1916932
  82.8 0.7 copy-start.2
  90.3 3.5 %copy-start.3 = (bf16[224,512]{1,0:T(8,128)(2,1)S(1)}, bf16[224,512]{1,0:T(8,128)(2,1)}, u32[]{:S(2)}) copy-start(bf16[224,512]{1,0:T(8,128)(2,1)} %copy-done.2) | copy-start | bytes 688132
  90.3 12.1 %all-to-all-start.3 = ((bf16[8,104,128]{2,1,0:T(8,128)(2,1)}), bf16[8,104,128]{2,1,0:T(8,128)(2,1)S(1)}, u32[]{:S(2)}, u32[]{:S(2)}) async-start(bf16[8,104,128]{2,1,0:T(8,128)(2,1)} %shard_map.52), calls=%async_computation.3 | async-start | bytes 425984 | tf_op jit(solution)/shard_map/all_to_all | solution.py:174
  95.6 3.7 %collective-permute-start.10 = (bf16[104,2048]{1,0:T(8,128)(2,1)S(1)}, bf16[104,2048]{1,0:T(8,128)(2,1)S(1)}, u32[]{:S(2)}, u32[]{:S(2)}) collective-permute-start(bf16[104,2048]{1,0:T(8,128)(2,1)S(1)} %get-tuple-element.25), channel_id=1, source_target_pairs={{0,1},{1,0},{2,3},{3,2},{4,5},{5,4},{6,7},{7,6},{8,9},{9,8},{10,11... | collective-permute-start | bytes 1277960 | tf_op jit(solution)/shard_map/ppermute | solution.py:179
